TPU v7x, 32 devices: a whole 2x2x4 slice. The times are simulated.
32 devices in a mesh: group: 2 (over x), section: 4 (over y, core), dp: 4 (over z).
Axes of the slice: x: 2, y: 2, z: 4, core: 2. Of those that a mesh axis runs over, the one named last changes fastest.
Arguments:
- inputs: bfloat16 [4, 256, 1024], P(None, ('group', 'dp')), parts along dimension 1, may hold values from -6 to 6
- cotangent: bfloat16 [4, 256, 1024], P(None, ('group', 'dp')), parts along dimension 1, may hold values from -0.1796875 to 0.1796875
- enc_weights: bfloat16 [4, 1024, 1024], P('section'), may hold values from -0.1875 to 0.1875
- dec_weights: bfloat16 [4, 2048, 1024], P('section'), may hold values from -0.125 to 0.125
Outputs:
- enc_grads: float32 [8, 1024, 1024], P(('group', 'section'), 'dp'), parts along dimension 0
- dec_grads: float32 [8, 2048, 1024], P(('group', 'section'), 'dp'), parts along dimension 0
There are 2 independent parts, one for each index of `group`. A program takes and returns all parts, laid end to end along the dimension named above; an argument that names none is the same for every part. Nothing has to cross between parts.
All inputs are finite; a program needn't handle non-finite values.
Results may differ from a plain program's by a relative error of at most 0.014.
Values may be sent and summed in bfloat16 or wider, within the bound.
No kernel may reach another device: no remote copies, remote signals or barrier semaphores. Data moves between devices by JAX's collectives and lax.ppermute only.
A program may use at most 64 MiB of HBM per device.

v0:
```python
import jax
import jax.numpy as jnp
from jax import lax
from jax.sharding import PartitionSpec as P

EPS = 1e-06


def from_behind(value, axis, by):
    length = lax.axis_size(axis)
    pairs = [(i, i + by) for i in range(length) if 0 <= i + by < length]
    return lax.ppermute(value, axis, pairs)


def normalize(values):
    return values * lax.rsqrt(jnp.mean(values * values, axis=-1, keepdims=True) + EPS)


def norm_back(values, grad):
    inv_rms = lax.rsqrt(jnp.mean(values * values, axis=-1, keepdims=True) + EPS)
    normed = values * inv_rms
    return inv_rms * (grad - normed * jnp.mean(grad * normed, axis=-1, keepdims=True))


def silu_grad(pre_act):
    sigma = jax.nn.sigmoid(pre_act)
    return sigma * (1.0 + pre_act * (1.0 - sigma))


def transpose_dot(left, right):
    return lax.dot_general(
        left, right, (((1,), (1,)), ((), ())), preferred_element_type=jnp.float32
    )


def row_sum_dot(left, right):
    return lax.dot_general(
        left, right, (((0,), (0,)), ((), ())), preferred_element_type=jnp.float32
    )


def encode(hidden, weight):
    values = hidden.astype(jnp.float32)
    normed = normalize(values).astype(jnp.bfloat16)
    pre_act = jnp.dot(normed, weight, preferred_element_type=jnp.float32)
    return (values + jax.nn.silu(pre_act)).astype(jnp.bfloat16)


def decode_mix(state, skip_in):
    both = jnp.concatenate(
        [normalize(state.astype(jnp.float32)), normalize(skip_in.astype(jnp.float32))], axis=-1
    )
    return both.astype(jnp.bfloat16)


def decode(state, skip_in, weight):
    mixed = decode_mix(state, skip_in)
    pre_act = jnp.dot(mixed, weight, preferred_element_type=jnp.float32)
    return (state.astype(jnp.float32) + jax.nn.silu(pre_act)).astype(jnp.bfloat16)


def encode_back(hidden, weight, grads):
    values = hidden.astype(jnp.float32)
    normed = normalize(values).astype(jnp.bfloat16)
    pre_act = jnp.dot(normed, weight, preferred_element_type=jnp.float32)
    act_grad = (grads.astype(jnp.float32) * silu_grad(pre_act)).astype(jnp.bfloat16)
    norm_grad = transpose_dot(act_grad, weight)
    return grads.astype(jnp.float32) + norm_back(values, norm_grad)


def decode_back(state, skip_in, weight, grads):
    mixed = decode_mix(state, skip_in)
    pre_act = jnp.dot(mixed, weight, preferred_element_type=jnp.float32)
    act_grad = (grads.astype(jnp.float32) * silu_grad(pre_act)).astype(jnp.bfloat16)
    mix_grad = transpose_dot(act_grad, weight)
    channels = state.shape[-1]
    state_grad = grads.astype(jnp.float32) + norm_back(
        state.astype(jnp.float32), mix_grad[:, :channels]
    )
    skip_grad = norm_back(skip_in.astype(jnp.float32), mix_grad[:, channels:])
    return (state_grad.astype(jnp.bfloat16), skip_grad.astype(jnp.bfloat16))


def encode_wgrad(hidden, weight, grads):
    normed = normalize(hidden.astype(jnp.float32)).astype(jnp.bfloat16)
    pre_act = jnp.dot(normed, weight, preferred_element_type=jnp.float32)
    act_grad = (grads.astype(jnp.float32) * silu_grad(pre_act)).astype(jnp.bfloat16)
    return row_sum_dot(normed, act_grad)


def decode_wgrad(state, skip_in, weight, grads):
    mixed = decode_mix(state, skip_in)
    pre_act = jnp.dot(mixed, weight, preferred_element_type=jnp.float32)
    act_grad = (grads.astype(jnp.float32) * silu_grad(pre_act)).astype(jnp.bfloat16)
    return row_sum_dot(mixed, act_grad)


def pick(buffer, position):
    return lax.dynamic_index_in_dim(buffer, position, 0, keepdims=False)


def store(buffer, position, value, is_live):
    previous = pick(buffer, position)
    return lax.dynamic_update_index_in_dim(buffer, jnp.where(is_live, value, previous), position, 0)


def body(inputs, cotangent, enc_weights, dec_weights):
    section_count = lax.axis_size("section")
    section_index = lax.axis_index("section")
    batches, row_count, channels = inputs.shape
    levels = enc_weights.shape[0]
    step_count = section_count + batches - 1
    top_section = section_count - 1
    empty_rows = jnp.zeros((row_count, channels), jnp.bfloat16)
    empty_batches = jnp.zeros((batches, row_count, channels), jnp.bfloat16)
    empty_store = jnp.zeros((batches, levels, row_count, channels), jnp.bfloat16)
    spare_stack = jnp.zeros((levels, row_count, channels), jnp.bfloat16)

    def timing(moment, rising):
        if rising:
            micro_slot = moment - section_index
        else:
            micro_slot = moment - (top_section - section_index)
        is_live = (micro_slot >= 0) & (micro_slot < batches)
        return (jnp.clip(micro_slot, 0, batches - 1), is_live)

    def spare_one(values):
        return (values, spare_stack)

    def spare_two(values):
        return (values, spare_stack, spare_stack)

    def rise_step(moment, state_tuple):
        inbox, skips, bottom = state_tuple
        micro_slot, is_live = timing(moment, True)
        incoming = jnp.where(section_index == 0, pick(inputs, micro_slot), inbox)

        def encode_all(hidden):
            saved_list = [hidden]
            hidden = encode(hidden, enc_weights[0])
            return (hidden, jnp.stack(saved_list))

        outgoing, saved = lax.cond(is_live, encode_all, spare_one, incoming)
        skips = store(skips, micro_slot, saved, is_live)
        bottom = store(bottom, micro_slot, outgoing, is_live & (section_index == top_section))
        inbox = from_behind(outgoing, "section", 1)
        return (inbox, skips, bottom)

    inbox, skips, bottom = lax.fori_loop(
        0, step_count, rise_step, (empty_rows, empty_store, empty_batches)
    )

    def descend_step(moment, state_tuple):
        inbox, dec_inputs = state_tuple
        micro_slot, is_live = timing(moment, False)
        incoming = jnp.where(section_index == top_section, pick(bottom, micro_slot), inbox)
        kept_skips = pick(skips, micro_slot)

        def decode_all(state):
            saved_list = [None] * levels
            for level in reversed(range(levels)):
                saved_list[level] = state
                state = decode(state, kept_skips[level], dec_weights[level])
            return (state, jnp.stack(saved_list))

        outgoing, saved = lax.cond(is_live, decode_all, spare_one, incoming)
        dec_inputs = store(dec_inputs, micro_slot, saved, is_live)
        inbox = from_behind(outgoing, "section", -1)
        return (inbox, dec_inputs)

    inbox, dec_inputs = lax.fori_loop(0, step_count, descend_step, (empty_rows, empty_store))

    def climb_step(moment, state_tuple):
        inbox, dec_seen, skip_grads, top_grads = state_tuple
        micro_slot, is_live = timing(moment, True)
        incoming = jnp.where(section_index == 0, pick(cotangent, micro_slot), inbox)
        kept_skips = pick(skips, micro_slot)
        kept_inputs = pick(dec_inputs, micro_slot)

        def climb_all(grads):
            seen_list = [grads]
            grads, skip_grad = decode_back(kept_inputs[0], kept_skips[0], dec_weights[0], grads)
            skip_list = [skip_grad]
            return (grads, jnp.stack(seen_list), jnp.stack(skip_list))

        outgoing, seen, skip_part = lax.cond(is_live, climb_all, spare_two, incoming)
        dec_seen = store(dec_seen, micro_slot, seen, is_live)
        skip_grads = store(skip_grads, micro_slot, skip_part, is_live)
        top_grads = store(top_grads, micro_slot, outgoing, is_live & (section_index == top_section))
        inbox = from_behind(outgoing, "section", 1)
        return (inbox, dec_seen, skip_grads, top_grads)

    inbox, dec_seen, skip_grads, top_grads = lax.fori_loop(
        0, step_count, climb_step, (empty_rows, empty_store, empty_store, empty_batches)
    )

    def merged(buffer, level):
        return buffer[:, level].reshape(batches * row_count, channels)

    def return_step(moment, state_tuple):
        inbox, enc_seen = state_tuple
        micro_slot, is_live = timing(moment, False)
        incoming = jnp.where(section_index == top_section, pick(top_grads, micro_slot), inbox)
        kept_skips = pick(skips, micro_slot)
        kept_grads = pick(skip_grads, micro_slot)

        def return_all(grads):
            seen_list = [None] * levels
            for level in reversed(range(levels)):
                seen_list[level] = grads
                summed = encode_back(kept_skips[level], enc_weights[level], grads) + kept_grads[
                    level
                ].astype(jnp.float32)
                grads = summed.astype(jnp.bfloat16)
            return (grads, jnp.stack(seen_list))

        outgoing, seen = lax.cond(is_live, return_all, spare_one, incoming)
        enc_seen = store(enc_seen, micro_slot, seen, is_live)
        inbox = from_behind(outgoing, "section", -1)
        return (inbox, enc_seen)

    inbox, enc_seen = lax.fori_loop(0, step_count, return_step, (empty_rows, empty_store))
    encoder_partial = jnp.stack(
        [encode_wgrad(merged(skips, 0), enc_weights[0], merged(enc_seen, 0))]
    )
    enc_grads = lax.psum_scatter(
        encoder_partial.astype(jnp.bfloat16), "dp", scatter_dimension=1, tiled=True
    ).astype(jnp.float32)
    dec_grads = lax.psum_scatter(
        jnp.stack(
            [
                decode_wgrad(
                    merged(dec_inputs, 0), merged(skips, 0), dec_weights[0], merged(dec_seen, 0)
                )
            ]
        ).astype(jnp.bfloat16),
        "dp",
        scatter_dimension=1,
        tiled=True,
    ).astype(jnp.float32)
    return (enc_grads, dec_grads)


def solution(mesh):
    in_specs = (
        P(None, ("group", "dp"), None),
        P(None, ("group", "dp"), None),
        P("section", None, None),
        P("section", None, None),
    )
    out_specs = (P(("group", "section"), "dp", None), P(("group", "section"), "dp", None))
    return jax.shard_map(body, mesh=mesh, in_specs=in_specs, out_specs=out_specs, check_vma=False)
```

profile of v0, /device:TPU:0, one launch (start us, length us, event | category | flops | bytes accessed | tf_op | source)
XLA Modules:
  0.0 385.3 jit_solution(2864087980407264191)
XLA Ops:
  7.3 52.3 %while.72 = (s32[]{:T(128)}, bf16[32,1024]{1,0:T(8,128)(2,1)S(1)}, bf16[4,1,32,1024]{3,2,1,0:T(8,128)(2,1)S(1)}, bf16[4,32,1024]{2,1,0:T(8,128)(2,1)S(1)}, s32[]...) while((s32[]{:T(128)}, bf16[32,1024]{1,0:T(8,128)(2,1)S(1)}, ...), condition=%wide.region_4.5_spmd, body=%wide.region_0.4_spmd.sunk | while | flops 67633192 | bytes 3408669 | solution.py:149
  30.1 4.7 %collective-permute-start = (bf16[32,1024]{1,0:T(8,128)(2,1)S(1)}, bf16[32,1024]{1,0:T(8,128)(2,1)S(1)}, u32[]{:S(2)}, u32[]{:S(2)}) collective-permute-start(bf16[32,1024]{1,0:T(8,128)(2,1)S(1)} %get-tuple-element.1198), channel_id=1, source_target_pairs={{0,4},{4,8},{8,12},{1,5},{5,9},{9,13},{2,6},{6,10},{10,14},{3,7},{... | collective-permute-start | bytes 196616 | tf_op jit(solution)/shard_map/while/body/eval_jaxpr/ppermute | solution.py:12
  36.6 6.9 %collective-permute-start = (bf16[32,1024]{1,0:T(8,128)(2,1)S(1)}, bf16[32,1024]{1,0:T(8,128)(2,1)S(1)}, u32[]{:S(2)}, u32[]{:S(2)}) collective-permute-start(bf16[32,1024]{1,0:T(8,128)(2,1)S(1)} %get-tuple-element.1198), channel_id=1, source_target_pairs={{0,4},{4,8},{8,12},{1,5},{5,9},{9,13},{2,6},{6,10},{10,14},{3,7},{... | collective-permute-start | bytes 196616 | tf_op jit(solution)/shard_map/while/body/eval_jaxpr/ppermute | solution.py:12
  45.3 4.7 %collective-permute-start = (bf16[32,1024]{1,0:T(8,128)(2,1)S(1)}, bf16[32,1024]{1,0:T(8,128)(2,1)S(1)}, u32[]{:S(2)}, u32[]{:S(2)}) collective-permute-start(bf16[32,1024]{1,0:T(8,128)(2,1)S(1)} %get-tuple-element.1198), channel_id=1, source_target_pairs={{0,4},{4,8},{8,12},{1,5},{5,9},{9,13},{2,6},{6,10},{10,14},{3,7},{... | collective-permute-start | bytes 196616 | tf_op jit(solution)/shard_map/while/body/eval_jaxpr/ppermute | solution.py:12
  51.8 6.9 %collective-permute-start = (bf16[32,1024]{1,0:T(8,128)(2,1)S(1)}, bf16[32,1024]{1,0:T(8,128)(2,1)S(1)}, u32[]{:S(2)}, u32[]{:S(2)}) collective-permute-start(bf16[32,1024]{1,0:T(8,128)(2,1)S(1)} %get-tuple-element.1198), channel_id=1, source_target_pairs={{0,4},{4,8},{8,12},{1,5},{5,9},{9,13},{2,6},{6,10},{10,14},{3,7},{... | collective-permute-start | bytes 196616 | tf_op jit(solution)/shard_map/while/body/eval_jaxpr/ppermute | solution.py:12
  60.7 55.9 %while.73 = (s32[]{:T(128)}, bf16[32,1024]{1,0:T(8,128)(2,1)S(1)}, bf16[4,1,32,1024]{3,2,1,0:T(8,128)(2,1)S(1)}, s32[]{:T(128)}, pred[]{:T(512)}, /*index=5*/bf1...) while((s32[]{:T(128)}, bf16[32,1024]{1,0:T(8,128)(2,1)S(1)}, ...), condition=%wide.region_11.12_spmd, body=%wide.region_6.11_spmd.sunk | while | flops 135168064 | bytes 5637409 | solution.py:171
  62.1 4.1 %collective-permute-done.1 = bf16[32,1024]{1,0:T(8,128)(2,1)S(1)} collective-permute-done((bf16[32,1024]{1,0:T(8,128)(2,1)S(1)}, bf16[32,1024]{1,0:T(8,128)(2,1)S(1)}, u32[]{:S(2)}, u32[]{:S(2)}) %collective-permute-start.1) | collective-permute-done | bytes 65568 | tf_op jit(solution)/shard_map/while/body/eval_jaxpr/ppermute | solution.py:12
  67.6 4.9 %collective-permute-done.1 = bf16[32,1024]{1,0:T(8,128)(2,1)S(1)} collective-permute-done((bf16[32,1024]{1,0:T(8,128)(2,1)S(1)}, bf16[32,1024]{1,0:T(8,128)(2,1)S(1)}, u32[]{:S(2)}, u32[]{:S(2)}) %collective-permute-start.1) | collective-permute-done | bytes 65568 | tf_op jit(solution)/shard_map/while/body/eval_jaxpr/ppermute | solution.py:12
  73.9 9.1 %collective-permute-done.1 = bf16[32,1024]{1,0:T(8,128)(2,1)S(1)} collective-permute-done((bf16[32,1024]{1,0:T(8,128)(2,1)S(1)}, bf16[32,1024]{1,0:T(8,128)(2,1)S(1)}, u32[]{:S(2)}, u32[]{:S(2)}) %collective-permute-start.1) | collective-permute-done | bytes 65568 | tf_op jit(solution)/shard_map/while/body/eval_jaxpr/ppermute | solution.py:12
  87.8 4.2 %collective-permute-done.1 = bf16[32,1024]{1,0:T(8,128)(2,1)S(1)} collective-permute-done((bf16[32,1024]{1,0:T(8,128)(2,1)S(1)}, bf16[32,1024]{1,0:T(8,128)(2,1)S(1)}, u32[]{:S(2)}, u32[]{:S(2)}) %collective-permute-start.1) | collective-permute-done | bytes 65568 | tf_op jit(solution)/shard_map/while/body/eval_jaxpr/ppermute | solution.py:12
  96.8 4.2 %collective-permute-done.1 = bf16[32,1024]{1,0:T(8,128)(2,1)S(1)} collective-permute-done((bf16[32,1024]{1,0:T(8,128)(2,1)S(1)}, bf16[32,1024]{1,0:T(8,128)(2,1)S(1)}, u32[]{:S(2)}, u32[]{:S(2)}) %collective-permute-start.1) | collective-permute-done | bytes 65568 | tf_op jit(solution)/shard_map/while/body/eval_jaxpr/ppermute | solution.py:12
  105.8 4.2 %collective-permute-done.1 = bf16[32,1024]{1,0:T(8,128)(2,1)S(1)} collective-permute-done((bf16[32,1024]{1,0:T(8,128)(2,1)S(1)}, bf16[32,1024]{1,0:T(8,128)(2,1)S(1)}, u32[]{:S(2)}, u32[]{:S(2)}) %collective-permute-start.1) | collective-permute-done | bytes 65568 | tf_op jit(solution)/shard_map/while/body/eval_jaxpr/ppermute | solution.py:12
  119.2 77.7 %while.74 = (s32[]{:T(128)}, bf16[32,1024]{1,0:T(8,128)(2,1)S(1)}, bf16[4,1,32,1024]{3,2,1,0:T(8,128)(2,1)}, bf16[4,1,32,1024]{3,2,1,0:T(8,128)(2,1)}, bf16[4,32...) while((s32[]{:T(128)}, bf16[32,1024]{1,0:T(8,128)(2,1)S(1)}, ...), condition=%wide.region_19.20_spmd, body=%wide.region_12.19_spmd.sunk | while | flops 270270528 | bytes 7605609 | solution.py:193
  120.3 6.3 %conditional.10 = (bf16[32,1024]{1,0:T(8,128)(2,1)S(1)}, bf16[1,32,1024]{2,1,0:T(8,128)(2,1)S(1)}, bf16[1,32,1024]{2,1,0:T(8,128)(2,1)S(1)}) conditional(s32[]{:T(128)} %convert_element_type.389, bf16[32,1024]{1,0:T(8,128)(2,1)S(1)} %bitcast_select_fusion.17, (bf16[32,1024]{1,0:T(8,128)(2,1)S(1)}, bf16[4,1,32,1024]{3,2,1,0:T(8,128)(2,1)S(1)}, ...), branch_computations={%region_13.13_spmd, %region_14.18_spmd} | conditional | flops 270139456 | bytes 6162988 | solution.py:186
  120.7 5.5 %fusion.24 = f32[32,2048]{1,0:T(8,128)S(1)} fusion(bf16[1,2048,1024]{2,1,0:T(8,128)(2,1)} %get-tuple-element.844, bf16[32,1024]{1,0:T(8,128)(2,1)S(1)} %get-tuple-element.840, bf16[32,1024]{1,0:T(8,128)(2,1)S(1)} %get-tuple-element.976, bf16[32,1024]{1,0:T(8,128)(2,1)S(1)} %get-tuple-element.977), kind=kOutput, calls=%fused_computation.39 | convolution fusion | flops 269025280 | bytes 4653056 | tf_op jit(solution)/shard_map/while/body/eval_jaxpr/cond/branch_1_fun/dot_general | solution.py:31
  131.2 6.3 %conditional.10 = (bf16[32,1024]{1,0:T(8,128)(2,1)S(1)}, bf16[1,32,1024]{2,1,0:T(8,128)(2,1)S(1)}, bf16[1,32,1024]{2,1,0:T(8,128)(2,1)S(1)}) conditional(s32[]{:T(128)} %convert_element_type.389, bf16[32,1024]{1,0:T(8,128)(2,1)S(1)} %bitcast_select_fusion.17, (bf16[32,1024]{1,0:T(8,128)(2,1)S(1)}, bf16[4,1,32,1024]{3,2,1,0:T(8,128)(2,1)S(1)}, ...), branch_computations={%region_13.13_spmd, %region_14.18_spmd} | conditional | flops 270139456 | bytes 6162988 | solution.py:186
  131.6 5.5 %fusion.24 = f32[32,2048]{1,0:T(8,128)S(1)} fusion(bf16[1,2048,1024]{2,1,0:T(8,128)(2,1)} %get-tuple-element.844, bf16[32,1024]{1,0:T(8,128)(2,1)S(1)} %get-tuple-element.840, bf16[32,1024]{1,0:T(8,128)(2,1)S(1)} %get-tuple-element.976, bf16[32,1024]{1,0:T(8,128)(2,1)S(1)} %get-tuple-element.977), kind=kOutput, calls=%fused_computation.39 | convolution fusion | flops 269025280 | bytes 4653056 | tf_op jit(solution)/shard_map/while/body/eval_jaxpr/cond/branch_1_fun/dot_general | solution.py:31
  142.1 6.3 %conditional.10 = (bf16[32,1024]{1,0:T(8,128)(2,1)S(1)}, bf16[1,32,1024]{2,1,0:T(8,128)(2,1)S(1)}, bf16[1,32,1024]{2,1,0:T(8,128)(2,1)S(1)}) conditional(s32[]{:T(128)} %convert_element_type.389, bf16[32,1024]{1,0:T(8,128)(2,1)S(1)} %bitcast_select_fusion.17, (bf16[32,1024]{1,0:T(8,128)(2,1)S(1)}, bf16[4,1,32,1024]{3,2,1,0:T(8,128)(2,1)S(1)}, ...), branch_computations={%region_13.13_spmd, %region_14.18_spmd} | conditional | flops 270139456 | bytes 6162988 | solution.py:186
  142.5 5.5 %fusion.24 = f32[32,2048]{1,0:T(8,128)S(1)} fusion(bf16[1,2048,1024]{2,1,0:T(8,128)(2,1)} %get-tuple-element.844, bf16[32,1024]{1,0:T(8,128)(2,1)S(1)} %get-tuple-element.840, bf16[32,1024]{1,0:T(8,128)(2,1)S(1)} %get-tuple-element.976, bf16[32,1024]{1,0:T(8,128)(2,1)S(1)} %get-tuple-element.977), kind=kOutput, calls=%fused_computation.39 | convolution fusion | flops 269025280 | bytes 4653056 | tf_op jit(solution)/shard_map/while/body/eval_jaxpr/cond/branch_1_fun/dot_general | solution.py:31
  153.1 6.3 %conditional.10 = (bf16[32,1024]{1,0:T(8,128)(2,1)S(1)}, bf16[1,32,1024]{2,1,0:T(8,128)(2,1)S(1)}, bf16[1,32,1024]{2,1,0:T(8,128)(2,1)S(1)}) conditional(s32[]{:T(128)} %convert_element_type.389, bf16[32,1024]{1,0:T(8,128)(2,1)S(1)} %bitcast_select_fusion.17, (bf16[32,1024]{1,0:T(8,128)(2,1)S(1)}, bf16[4,1,32,1024]{3,2,1,0:T(8,128)(2,1)S(1)}, ...), branch_computations={%region_13.13_spmd, %region_14.18_spmd} | conditional | flops 270139456 | bytes 6162988 | solution.py:186
  153.5 5.5 %fusion.24 = f32[32,2048]{1,0:T(8,128)S(1)} fusion(bf16[1,2048,1024]{2,1,0:T(8,128)(2,1)} %get-tuple-element.844, bf16[32,1024]{1,0:T(8,128)(2,1)S(1)} %get-tuple-element.840, bf16[32,1024]{1,0:T(8,128)(2,1)S(1)} %get-tuple-element.976, bf16[32,1024]{1,0:T(8,128)(2,1)S(1)} %get-tuple-element.977), kind=kOutput, calls=%fused_computation.39 | convolution fusion | flops 269025280 | bytes 4653056 | tf_op jit(solution)/shard_map/while/body/eval_jaxpr/cond/branch_1_fun/dot_general | solution.py:31
  165.9 9.4 %collective-permute-start.2 = (bf16[32,1024]{1,0:T(8,128)(2,1)S(1)}, bf16[32,1024]{1,0:T(8,128)(2,1)S(1)}, u32[]{:S(2)}, u32[]{:S(2)}) collective-permute-start(bf16[32,1024]{1,0:T(8,128)(2,1)S(1)} %get-tuple-element.1222), channel_id=1, source_target_pairs={{0,4},{4,8},{8,12},{1,5},{5,9},{9,13},{2,6},{6,10},{10,14},{3,7},{... | collective-permute-start | bytes 196616 | tf_op jit(solution)/shard_map/while/body/eval_jaxpr/ppermute | solution.py:12
  185.1 9.4 %collective-permute-start.2 = (bf16[32,1024]{1,0:T(8,128)(2,1)S(1)}, bf16[32,1024]{1,0:T(8,128)(2,1)S(1)}, u32[]{:S(2)}, u32[]{:S(2)}) collective-permute-start(bf16[32,1024]{1,0:T(8,128)(2,1)S(1)} %get-tuple-element.1222), channel_id=1, source_target_pairs={{0,4},{4,8},{8,12},{1,5},{5,9},{9,13},{2,6},{6,10},{10,14},{3,7},{... | collective-permute-start | bytes 196616 | tf_op jit(solution)/shard_map/while/body/eval_jaxpr/ppermute | solution.py:12
  197.0 49.8 %while.75 = (s32[]{:T(128)}, bf16[32,1024]{1,0:T(8,128)(2,1)S(1)}, bf16[4,1,32,1024]{3,2,1,0:T(8,128)(2,1)S(1)}, s32[]{:T(128)}, pred[]{:T(512)}, /*index=5*/bf1...) while((s32[]{:T(128)}, bf16[32,1024]{1,0:T(8,128)(2,1)S(1)}, ...), condition=%wide.region_25.26_spmd, body=%wide.region_20.25_spmd.sunk | while | flops 135266336 | bytes 5901617 | solution.py:222
  202.3 6.3 %collective-permute-done.3 = bf16[32,1024]{1,0:T(8,128)(2,1)S(1)} collective-permute-done((bf16[32,1024]{1,0:T(8,128)(2,1)S(1)}, bf16[32,1024]{1,0:T(8,128)(2,1)S(1)}, u32[]{:S(2)}, u32[]{:S(2)}) %collective-permute-start.3) | collective-permute-done | bytes 65568 | tf_op jit(solution)/shard_map/while/body/eval_jaxpr/ppermute | solution.py:12
  210.1 7.2 %collective-permute-done.3 = bf16[32,1024]{1,0:T(8,128)(2,1)S(1)} collective-permute-done((bf16[32,1024]{1,0:T(8,128)(2,1)S(1)}, bf16[32,1024]{1,0:T(8,128)(2,1)S(1)}, u32[]{:S(2)}, u32[]{:S(2)}) %collective-permute-start.3) | collective-permute-done | bytes 65568 | tf_op jit(solution)/shard_map/while/body/eval_jaxpr/ppermute | solution.py:12
  221.0 4.2 %collective-permute-done.3 = bf16[32,1024]{1,0:T(8,128)(2,1)S(1)} collective-permute-done((bf16[32,1024]{1,0:T(8,128)(2,1)S(1)}, bf16[32,1024]{1,0:T(8,128)(2,1)S(1)}, u32[]{:S(2)}, u32[]{:S(2)}) %collective-permute-start.3) | collective-permute-done | bytes 65568 | tf_op jit(solution)/shard_map/while/body/eval_jaxpr/ppermute | solution.py:12
  229.0 4.2 %collective-permute-done.3 = bf16[32,1024]{1,0:T(8,128)(2,1)S(1)} collective-permute-done((bf16[32,1024]{1,0:T(8,128)(2,1)S(1)}, bf16[32,1024]{1,0:T(8,128)(2,1)S(1)}, u32[]{:S(2)}, u32[]{:S(2)}) %collective-permute-start.3) | collective-permute-done | bytes 65568 | tf_op jit(solution)/shard_map/while/body/eval_jaxpr/ppermute | solution.py:12
  237.0 4.2 %collective-permute-done.3 = bf16[32,1024]{1,0:T(8,128)(2,1)S(1)} collective-permute-done((bf16[32,1024]{1,0:T(8,128)(2,1)S(1)}, bf16[32,1024]{1,0:T(8,128)(2,1)S(1)}, u32[]{:S(2)}, u32[]{:S(2)}) %collective-permute-start.3) | collective-permute-done | bytes 65568 | tf_op jit(solution)/shard_map/while/body/eval_jaxpr/ppermute | solution.py:12
  250.3 6.1 %convert_bitcast_fusion.2 = bf16[1,2048,1024]{2,1,0:T(8,128)(2,1)} fusion(bf16[128,1024]{1,0:T(8,128)(2,1)S(1)} %bitcast.218, bf16[1,2048,1024]{2,1,0:T(8,128)(2,1)} %get-tuple-element.1421, bf16[128,1024]{1,0:T(8,128)(2,1)S(1)} %copy-done.3, bf16[128,1024]{1,0:T(8,128)(2,1)S(1)} %copy-done.2), kind=kOutput, calls=%fused_computation.122 | convolution fusion | flops 1079246848 | bytes 9175040 | tf_op jit(solution)/shard_map/dot_general | solution.py:37
  256.5 40.7 %reduce-scatter.3.cloned.1.call-done = bf16[1,256,1024]{2,1,0:T(8,128)(2,1)} async-done(((bf16[1,1024,1024]{2,1,0:T(8,128)(2,1)}), bf16[1,256,1024]{2,1,0:T(8,128)(2,1)}) %reduce-scatter.3.cloned.1.call-update) | async-done | bytes 524304 | tf_op jit(solution)/shard_map/reduce_scatter | solution.py:226
  299.3 76.4 %reduce-scatter.5.cloned.1.call-done = bf16[1,512,1024]{2,1,0:T(8,128)(2,1)} async-done(((bf16[1,2048,1024]{2,1,0:T(8,128)(2,1)}), bf16[1,512,1024]{2,1,0:T(8,128)(2,1)}) %reduce-scatter.5.cloned.1.call-update) | async-done | bytes 1048592 | tf_op jit(solution)/shard_map/reduce_scatter | solution.py:229
  (337 shorter events, 157.2 us)
Async XLA Ops:
  7.2 290.0 %reduce-scatter.3.cloned.1.call-start = ((), (), s32[]{:S(2)}) async-start(), calls=%async_computation.2 | async-start | bytes 2621440 | tf_op jit(solution)/shard_map/reduce_scatter | solution.py:226
  10.5 2.2 collective-permute-start
  15.8 4.7 %collective-permute-start = (bf16[32,1024]{1,0:T(8,128)(2,1)S(1)}, bf16[32,1024]{1,0:T(8,128)(2,1)S(1)}, u32[]{:S(2)}, u32[]{:S(2)}) collective-permute-start(bf16[32,1024]{1,0:T(8,128)(2,1)S(1)} %get-tuple-element.1198), channel_id=1, source_target_pairs={{0,4},{4,8},{8,12},{1,5},{5,9},{9,13},{2,6},{6,10},{10,14},{3,7},{... | collective-permute-start | bytes 196616 | tf_op jit(solution)/shard_map/while/body/eval_jaxpr/ppermute | solution.py:12
  23.6 3.3 collective-permute-start
  30.1 5.6 %collective-permute-start = (bf16[32,1024]{1,0:T(8,128)(2,1)S(1)}, bf16[32,1024]{1,0:T(8,128)(2,1)S(1)}, u32[]{:S(2)}, u32[]{:S(2)}) collective-permute-start(bf16[32,1024]{1,0:T(8,128)(2,1)S(1)} %get-tuple-element.1198), channel_id=1, source_target_pairs={{0,4},{4,8},{8,12},{1,5},{5,9},{9,13},{2,6},{6,10},{10,14},{3,7},{... | collective-permute-start | bytes 196616 | tf_op jit(solution)/shard_map/while/body/eval_jaxpr/ppermute | solution.py:12
  36.6 7.8 %collective-permute-start = (bf16[32,1024]{1,0:T(8,128)(2,1)S(1)}, bf16[32,1024]{1,0:T(8,128)(2,1)S(1)}, u32[]{:S(2)}, u32[]{:S(2)}) collective-permute-start(bf16[32,1024]{1,0:T(8,128)(2,1)S(1)} %get-tuple-element.1198), channel_id=1, source_target_pairs={{0,4},{4,8},{8,12},{1,5},{5,9},{9,13},{2,6},{6,10},{10,14},{3,7},{... | collective-permute-start | bytes 196616 | tf_op jit(solution)/shard_map/while/body/eval_jaxpr/ppermute | solution.py:12
  45.3 5.6 %collective-permute-start = (bf16[32,1024]{1,0:T(8,128)(2,1)S(1)}, bf16[32,1024]{1,0:T(8,128)(2,1)S(1)}, u32[]{:S(2)}, u32[]{:S(2)}) collective-permute-start(bf16[32,1024]{1,0:T(8,128)(2,1)S(1)} %get-tuple-element.1198), channel_id=1, source_target_pairs={{0,4},{4,8},{8,12},{1,5},{5,9},{9,13},{2,6},{6,10},{10,14},{3,7},{... | collective-permute-start | bytes 196616 | tf_op jit(solution)/shard_map/while/body/eval_jaxpr/ppermute | solution.py:12
  51.8 7.8 %collective-permute-start = (bf16[32,1024]{1,0:T(8,128)(2,1)S(1)}, bf16[32,1024]{1,0:T(8,128)(2,1)S(1)}, u32[]{:S(2)}, u32[]{:S(2)}) collective-permute-start(bf16[32,1024]{1,0:T(8,128)(2,1)S(1)} %get-tuple-element.1198), channel_id=1, source_target_pairs={{0,4},{4,8},{8,12},{1,5},{5,9},{9,13},{2,6},{6,10},{10,14},{3,7},{... | collective-permute-start | bytes 196616 | tf_op jit(solution)/shard_map/while/body/eval_jaxpr/ppermute | solution.py:12
  60.8 5.4 %collective-permute-start.1 = (bf16[32,1024]{1,0:T(8,128)(2,1)S(1)}, bf16[32,1024]{1,0:T(8,128)(2,1)S(1)}, u32[]{:S(2)}, u32[]{:S(2)}) collective-permute-start(bf16[32,1024]{1,0:T(8,128)(2,1)S(1)} %get-tuple-element.1208), channel_id=1, source_target_pairs={{4,0},{8,4},{12,8},{5,1},{9,5},{13,9},{6,2},{10,6},{14,10},{7,3},{... | collective-permute-start | bytes 196616 | tf_op jit(solution)/shard_map/while/body/eval_jaxpr/ppermute | solution.py:12
  66.3 6.2 %collective-permute-start.1 = (bf16[32,1024]{1,0:T(8,128)(2,1)S(1)}, bf16[32,1024]{1,0:T(8,128)(2,1)S(1)}, u32[]{:S(2)}, u32[]{:S(2)}) collective-permute-start(bf16[32,1024]{1,0:T(8,128)(2,1)S(1)} %get-tuple-element.1208), channel_id=1, source_target_pairs={{4,0},{8,4},{12,8},{5,1},{9,5},{13,9},{6,2},{10,6},{14,10},{7,3},{... | collective-permute-start | bytes 196616 | tf_op jit(solution)/shard_map/while/body/eval_jaxpr/ppermute | solution.py:12
  72.5 10.5 %collective-permute-start.1 = (bf16[32,1024]{1,0:T(8,128)(2,1)S(1)}, bf16[32,1024]{1,0:T(8,128)(2,1)S(1)}, u32[]{:S(2)}, u32[]{:S(2)}) collective-permute-start(bf16[32,1024]{1,0:T(8,128)(2,1)S(1)} %get-tuple-element.1208), channel_id=1, source_target_pairs={{4,0},{8,4},{12,8},{5,1},{9,5},{13,9},{6,2},{10,6},{14,10},{7,3},{... | collective-permute-start | bytes 196616 | tf_op jit(solution)/shard_map/while/body/eval_jaxpr/ppermute | solution.py:12
  86.4 5.6 %collective-permute-start.1 = (bf16[32,1024]{1,0:T(8,128)(2,1)S(1)}, bf16[32,1024]{1,0:T(8,128)(2,1)S(1)}, u32[]{:S(2)}, u32[]{:S(2)}) collective-permute-start(bf16[32,1024]{1,0:T(8,128)(2,1)S(1)} %get-tuple-element.1208), channel_id=1, source_target_pairs={{4,0},{8,4},{12,8},{5,1},{9,5},{13,9},{6,2},{10,6},{14,10},{7,3},{... | collective-permute-start | bytes 196616 | tf_op jit(solution)/shard_map/while/body/eval_jaxpr/ppermute | solution.py:12
  95.4 5.6 %collective-permute-start.1 = (bf16[32,1024]{1,0:T(8,128)(2,1)S(1)}, bf16[32,1024]{1,0:T(8,128)(2,1)S(1)}, u32[]{:S(2)}, u32[]{:S(2)}) collective-permute-start(bf16[32,1024]{1,0:T(8,128)(2,1)S(1)} %get-tuple-element.1208), channel_id=1, source_target_pairs={{4,0},{8,4},{12,8},{5,1},{9,5},{13,9},{6,2},{10,6},{14,10},{7,3},{... | collective-permute-start | bytes 196616 | tf_op jit(solution)/shard_map/while/body/eval_jaxpr/ppermute | solution.py:12
  104.4 5.6 %collective-permute-start.1 = (bf16[32,1024]{1,0:T(8,128)(2,1)S(1)}, bf16[32,1024]{1,0:T(8,128)(2,1)S(1)}, u32[]{:S(2)}, u32[]{:S(2)}) collective-permute-start(bf16[32,1024]{1,0:T(8,128)(2,1)S(1)} %get-tuple-element.1208), channel_id=1, source_target_pairs={{4,0},{8,4},{12,8},{5,1},{9,5},{13,9},{6,2},{10,6},{14,10},{7,3},{... | collective-permute-start | bytes 196616 | tf_op jit(solution)/shard_map/while/body/eval_jaxpr/ppermute | solution.py:12
  113.4 3.1 collective-permute-start.1
  119.2 77.7 %copy-start = (bf16[1,1024,1024]{2,1,0:T(8,128)(2,1)S(1)}, bf16[1,1024,1024]{2,1,0:T(8,128)(2,1)}, u32[]{:S(2)}) copy-start(bf16[1,1024,1024]{2,1,0:T(8,128)(2,1)} %get-tuple-element.1422) | copy-start | bytes 6291460
  126.6 3.7 collective-permute-start.2
  137.5 3.7 collective-permute-start.2
  148.5 3.7 collective-permute-start.2
  159.4 5.5 %collective-permute-start.2 = (bf16[32,1024]{1,0:T(8,128)(2,1)S(1)}, bf16[32,1024]{1,0:T(8,128)(2,1)S(1)}, u32[]{:S(2)}, u32[]{:S(2)}) collective-permute-start(bf16[32,1024]{1,0:T(8,128)(2,1)S(1)} %get-tuple-element.1222), channel_id=1, source_target_pairs={{0,4},{4,8},{8,12},{1,5},{5,9},{9,13},{2,6},{6,10},{10,14},{3,7},{... | collective-permute-start | bytes 196616 | tf_op jit(solution)/shard_map/while/body/eval_jaxpr/ppermute | solution.py:12
  165.9 11.8 %collective-permute-start.2 = (bf16[32,1024]{1,0:T(8,128)(2,1)S(1)}, bf16[32,1024]{1,0:T(8,128)(2,1)S(1)}, u32[]{:S(2)}, u32[]{:S(2)}) collective-permute-start(bf16[32,1024]{1,0:T(8,128)(2,1)S(1)} %get-tuple-element.1222), channel_id=1, source_target_pairs={{0,4},{4,8},{8,12},{1,5},{5,9},{9,13},{2,6},{6,10},{10,14},{3,7},{... | collective-permute-start | bytes 196616 | tf_op jit(solution)/shard_map/while/body/eval_jaxpr/ppermute | solution.py:12
  178.6 5.5 %collective-permute-start.2 = (bf16[32,1024]{1,0:T(8,128)(2,1)S(1)}, bf16[32,1024]{1,0:T(8,128)(2,1)S(1)}, u32[]{:S(2)}, u32[]{:S(2)}) collective-permute-start(bf16[32,1024]{1,0:T(8,128)(2,1)S(1)} %get-tuple-element.1222), channel_id=1, source_target_pairs={{0,4},{4,8},{8,12},{1,5},{5,9},{9,13},{2,6},{6,10},{10,14},{3,7},{... | collective-permute-start | bytes 196616 | tf_op jit(solution)/shard_map/while/body/eval_jaxpr/ppermute | solution.py:12
  185.1 11.8 %collective-permute-start.2 = (bf16[32,1024]{1,0:T(8,128)(2,1)S(1)}, bf16[32,1024]{1,0:T(8,128)(2,1)S(1)}, u32[]{:S(2)}, u32[]{:S(2)}) collective-permute-start(bf16[32,1024]{1,0:T(8,128)(2,1)S(1)} %get-tuple-element.1222), channel_id=1, source_target_pairs={{0,4},{4,8},{8,12},{1,5},{5,9},{9,13},{2,6},{6,10},{10,14},{3,7},{... | collective-permute-start | bytes 196616 | tf_op jit(solution)/shard_map/while/body/eval_jaxpr/ppermute | solution.py:12
  197.0 49.8 %copy-start.3 = (bf16[128,1024]{1,0:T(8,128)(2,1)S(1)}, bf16[128,1024]{1,0:T(8,128)(2,1)}, u32[]{:S(2)}) copy-start(bf16[128,1024]{1,0:T(8,128)(2,1)} %get-tuple-element.983) | copy-start | bytes 786436
  197.1 3.9 collective-permute-start.3
  201.0 7.7 %collective-permute-start.3 = (bf16[32,1024]{1,0:T(8,128)(2,1)S(1)}, bf16[32,1024]{1,0:T(8,128)(2,1)S(1)}, u32[]{:S(2)}, u32[]{:S(2)}) collective-permute-start(bf16[32,1024]{1,0:T(8,128)(2,1)S(1)} %get-tuple-element.1236), channel_id=1, source_target_pairs={{4,0},{8,4},{12,8},{5,1},{9,5},{13,9},{6,2},{10,6},{14,10},{7,3},{... | collective-permute-start | bytes 196616 | tf_op jit(solution)/shard_map/while/body/eval_jaxpr/ppermute | solution.py:12
  208.7 8.5 %collective-permute-start.3 = (bf16[32,1024]{1,0:T(8,128)(2,1)S(1)}, bf16[32,1024]{1,0:T(8,128)(2,1)S(1)}, u32[]{:S(2)}, u32[]{:S(2)}) collective-permute-start(bf16[32,1024]{1,0:T(8,128)(2,1)S(1)} %get-tuple-element.1236), channel_id=1, source_target_pairs={{4,0},{8,4},{12,8},{5,1},{9,5},{13,9},{6,2},{10,6},{14,10},{7,3},{... | collective-permute-start | bytes 196616 | tf_op jit(solution)/shard_map/while/body/eval_jaxpr/ppermute | solution.py:12
  219.6 5.6 %collective-permute-start.3 = (bf16[32,1024]{1,0:T(8,128)(2,1)S(1)}, bf16[32,1024]{1,0:T(8,128)(2,1)S(1)}, u32[]{:S(2)}, u32[]{:S(2)}) collective-permute-start(bf16[32,1024]{1,0:T(8,128)(2,1)S(1)} %get-tuple-element.1236), channel_id=1, source_target_pairs={{4,0},{8,4},{12,8},{5,1},{9,5},{13,9},{6,2},{10,6},{14,10},{7,3},{... | collective-permute-start | bytes 196616 | tf_op jit(solution)/shard_map/while/body/eval_jaxpr/ppermute | solution.py:12
  227.6 5.6 %collective-permute-start.3 = (bf16[32,1024]{1,0:T(8,128)(2,1)S(1)}, bf16[32,1024]{1,0:T(8,128)(2,1)S(1)}, u32[]{:S(2)}, u32[]{:S(2)}) collective-permute-start(bf16[32,1024]{1,0:T(8,128)(2,1)S(1)} %get-tuple-element.1236), channel_id=1, source_target_pairs={{4,0},{8,4},{12,8},{5,1},{9,5},{13,9},{6,2},{10,6},{14,10},{7,3},{... | collective-permute-start | bytes 196616 | tf_op jit(solution)/shard_map/while/body/eval_jaxpr/ppermute | solution.py:12
  235.6 5.6 %collective-permute-start.3 = (bf16[32,1024]{1,0:T(8,128)(2,1)S(1)}, bf16[32,1024]{1,0:T(8,128)(2,1)S(1)}, u32[]{:S(2)}, u32[]{:S(2)}) collective-permute-start(bf16[32,1024]{1,0:T(8,128)(2,1)S(1)} %get-tuple-element.1236), channel_id=1, source_target_pairs={{4,0},{8,4},{12,8},{5,1},{9,5},{13,9},{6,2},{10,6},{14,10},{7,3},{... | collective-permute-start | bytes 196616 | tf_op jit(solution)/shard_map/while/body/eval_jaxpr/ppermute | solution.py:12
  243.6 3.2 collective-permute-start.3
  250.3 125.4 %reduce-scatter.5.cloned.1.call-start = ((), (), s32[]{:S(2)}) async-start(), calls=%async_computation.3 | async-start | bytes 5242880 | tf_op jit(solution)/shard_map/reduce_scatter | solution.py:229
  (2 other events, 7.0 us)
Sparse Core Ops, SparseCore 0:
  250.4 46.7 reduce-scatter.2
  299.6 76.0 reduce-scatter.4
where the time goes:
time: 388 us; the launch traced here: 385 us
  waiting for transfers between devices  186 us (48%)
  starting transfers between devices  77.8 us (20%)
  matrix products  57.2 us (15%)
  other arithmetic  33.8 us (9%)
  local copies, waits for them, and re-layouts  14.3 us (4%)
  between operations  14.2 us (4%)
    ppermute x28, starting transfers between devices, from_behind(): return lax.ppermute(value, axis, pairs)  77.7 us
    reduce_scatter x1, waiting for transfers between devices, body(): lax.psum_scatter(jnp.stack([decode_wgrad(merged(dec_inputs, 0), merged(sk...  76.4 us
    ppermute x28, waiting for transfers between devices, from_behind(): return lax.ppermute(value, axis, pairs)  68.5 us
    reduce_scatter x1, waiting for transfers between devices, body(): lax.psum_scatter(encoder_partial.astype(jnp.bfloat16), 'dp', scatter_dime...  40.7 us
    dot_general x8, matrix products, transpose_dot(): lax.dot_general(left, right, (((1,), (1,)), ((), ())), preferred_element_...  27.1 us
    dynamic_slice x49, local copies, waits for them, and re-layouts, pick(): return lax.dynamic_index_in_dim(buffer, position, 0, keepdims=False)  12.3 us
    dot_general x4, matrix products, decode(): pre_act = jnp.dot(mixed, weight, preferred_element_type=jnp.float32)  12.2 us
    dot_general x2, matrix products, row_sum_dot(): lax.dot_general(left, right, (((0,), (0,)), ((), ())), preferred_element_...  9.5 us
  transfers between devices with their start and end apart: 30, of which 23 were waited for; matrix products, arithmetic and copies ran while one was open for 7% of the time, Pallas kernels for 0%

commit v1 on v0

v1 whole, which is shorter than its diff:
```python
import functools

import jax
import jax.numpy as jnp
from jax import lax
from jax.experimental import pallas as pl
from jax.experimental.pallas import tpu as pltpu
from jax.sharding import PartitionSpec as P

EPS = 1e-06
TILE = 256
VMEM_LIMIT = 58 * 1024 * 1024


def dot(left, right):
    return lax.dot_general(
        left, right, (((1,), (0,)), ((), ())), preferred_element_type=jnp.float32
    )


def dot_t(left, right):
    return lax.dot_general(
        left, right, (((1,), (1,)), ((), ())), preferred_element_type=jnp.float32
    )


def dot_rows(left, right):
    return lax.dot_general(
        left, right, (((0,), (0,)), ((), ())), preferred_element_type=jnp.float32
    )


NEEDS = {
    "enc": (),
    "dec": ("n",),
    "decb": ("n", "r", "nd", "rd", "gb"),
    "encb": ("n", "r", "ga", "k"),
}
MAKES = {
    "enc": ("n", "r", "ga"),
    "dec": ("nd", "rd", "gb"),
    "decb": ("k",),
    "encb": (),
}
SENDS = {"enc": ("nc",), "dec": ("mc",), "decb": ("u",), "encb": ("e",)}


def stage_kernel(cfg, *refs):
    ops, pair, wide, last, blocks, names = (
        cfg["ops"], cfg["pair"], cfg["wide"], cfg["last"], cfg["blocks"], cfg["names"]
    )
    ref = dict(zip(names, refs))
    sems = ref["sems"]
    section = lax.axis_index("section")
    core = lax.rem(section, 2)
    live = True if pair is None else lax.div(section, 2) == pair
    dp = lax.axis_index("dp")
    dp_count = cfg["dp_count"]
    x, ybuf = ref["v_x"], ref["v_y"]
    rows, channels = x.shape
    block_rows = rows // blocks
    tile_count = channels // TILE

    def for_tiles(step, carry=0):
        def run(j, carry):
            at = j * TILE
            if not isinstance(j, int):
                at = pl.multiple_of(at, TILE)
            return step(at, pl.ds(at, TILE), carry)

        if cfg["unroll"]:
            for j in range(tile_count):
                carry = run(j, carry)
            return carry
        return lax.fori_loop(0, tile_count, run, carry)

    def run_live():
        counter = [0]
        waits = {}

        def start(key, source, target):
            copy = pltpu.make_async_copy(source, target, sems.at[counter[0]])
            counter[0] += 1
            copy.start()
            waits.setdefault(key, []).append(copy)

        def ready(key):
            for copy in waits.pop(key, []):
                copy.wait()

        for b in range(blocks):
            start("x", ref["x%d" % b], x.at[pl.ds(b * block_rows, block_rows)])
        made = set()
        for op in ops:
            for name in NEEDS[op]:
                if name not in made and not (name in ("n", "r") and last and not wide and op == "decb"):
                    if name not in waits:
                        start(name, ref[name], ref["v_" + name])
            made.update(MAKES[op])
            kind = "we" if op in ("enc", "encb") else "wd"
            if kind not in waits:
                start(kind, ref[kind + "_own"], ref["v_" + kind].at[core])
                start(kind, ref[kind + "_oth"], ref["v_" + kind].at[1 - core])
            if op == "decb" and "dec" in ops:
                for b in range(blocks):
                    start("q", ref["q%d" % b], ref["v_q"].at[pl.ds(b * block_rows, block_rows)])

        outs = []

        def store(source, target):
            copy = pltpu.make_async_copy(source, target, sems.at[counter[0]])
            counter[0] += 1
            copy.start()
            outs.append(copy)

        def store_split(level, source, name):
            sem = sems.at[counter[0]]
            counter[0] += 1

            @pl.when(core == level)
            def _():
                pltpu.make_async_copy(source, ref[name + "_own"], sem).start()

            @pl.when(core != level)
            def _():
                pltpu.make_async_copy(source, ref[name + "_send"], sem).start()

            outs.append(pltpu.make_async_copy(source, ref[name + "_own"], sem))

        def normalize(level, n_ref, r_ref):
            values = x[...].astype(jnp.float32)
            inv = lax.rsqrt(jnp.mean(values * values, axis=-1, keepdims=True) + EPS)
            n_ref[level] = (values * inv).astype(jnp.bfloat16)
            r_ref[level] = jnp.broadcast_to(inv, (rows, 128))

        def activate(pre, gain_ref, level, sl):
            sigma = jax.nn.sigmoid(pre)
            gain_ref[level, :, sl] = sigma * (1.0 + pre * (1.0 - sigma))
            x[:, sl] = (x[:, sl].astype(jnp.float32) + pre * sigma).astype(jnp.bfloat16)

        def enc_level(level):
            n, we = ref["v_n"], ref["v_we"]
            normalize(level, n, ref["v_r"])
            ready("we")

            def step(at, sl, carry):
                activate(dot(n[level], we[level, :, sl]), ref["v_ga"], level, sl)
                return carry

            for_tiles(step)
            if wide:
                width = channels // dp_count
                at = pl.multiple_of(dp * width, 128)
                store_split(level, n.at[level, :, pl.ds(at, width)], "nc")

        def dec_level(level):
            n, nd, wd = ref["v_n"], ref["v_nd"], ref["v_wd"]
            normalize(level, nd, ref["v_rd"])
            ready("n")
            ready("wd")

            def step(at, sl, carry):
                pre = dot(nd[level], wd[level, :channels, sl]) + dot(
                    n[level], wd[level, channels:, sl]
                )
                activate(pre, ref["v_gb"], level, sl)
                return carry

            for_tiles(step)
            if wide:
                width = 2 * channels // dp_count
                half = dp_count // 2
                sem = sems.at[counter[0]]
                counter[0] += 1
                for is_skip, buf in ((0, nd), (1, n)):
                    index = jnp.maximum(dp - half, 0) if is_skip else jnp.minimum(dp, half - 1)
                    source = buf.at[level, :, pl.ds(pl.multiple_of(index * width, 128), width)]
                    mine = (dp >= half) if is_skip else (dp < half)

                    @pl.when(mine & (core == level))
                    def _():
                        pltpu.make_async_copy(source, ref["mc_own"], sem).start()

                    @pl.when(mine & (core != level))
                    def _():
                        pltpu.make_async_copy(source, ref["mc_send"], sem).start()

                outs.append(pltpu.make_async_copy(nd.at[level, :, pl.ds(0, width)], ref["mc_own"], sem))

        def back(grad_ref, level, w_ref, base, n_ref, finish):
            grad = grad_ref[level]

            def step(at, sl, total):
                part = dot_t(grad, w_ref[level, pl.ds(base + at, TILE), :])
                ybuf[:, sl] = part
                return total + jnp.sum(
                    part * n_ref[level, :, sl].astype(jnp.float32), axis=-1, keepdims=True
                )

            total = for_tiles(step, jnp.zeros((rows, 1), jnp.float32)) / channels

            def close(at, sl, carry):
                finish(sl, ybuf[:, sl] - n_ref[level, :, sl].astype(jnp.float32) * total)
                return carry

            for_tiles(close)

        def decb_level(level):
            n, nd, wd, u, k = ref["v_n"], ref["v_nd"], ref["v_wd"], ref["v_u"], ref["v_k"]
            ready("gb")
            u[level] = (x[...].astype(jnp.float32) * ref["v_gb"][level]).astype(jnp.bfloat16)
            if wide:
                store_split(level, u.at[level], "u")
            ready("nd")
            ready("rd")
            ready("wd")
            rd = ref["v_rd"][level, :, :1]

            def finish(sl, value):
                x[:, sl] = (x[:, sl].astype(jnp.float32) + rd * value).astype(jnp.bfloat16)

            if not (wide and level == 1 and ops[-1] == "decb"):
                back(u, level, wd, 0, nd, finish)
            if wide or not last:
                ready("n")
                ready("r")
                r = ref["v_r"][level, :, :1]

                def finish_skip(sl, value):
                    k[level, :, sl] = (r * value).astype(jnp.bfloat16)

                back(u, level, wd, channels, n, finish_skip)

        def encb_level(level):
            n, we, e, k = ref["v_n"], ref["v_we"], ref["v_e"], ref["v_k"]
            ready("ga")
            e[level] = (x[...].astype(jnp.float32) * ref["v_ga"][level]).astype(jnp.bfloat16)
            if wide:
                store_split(level, e.at[level], "e")
            if wide and level == 0:
                return
            ready("we")
            ready("n")
            ready("r")
            ready("k")
            r = ref["v_r"][level, :, :1]

            def finish(sl, value):
                x[:, sl] = (
                    x[:, sl].astype(jnp.float32) + r * value + k[level, :, sl].astype(jnp.float32)
                ).astype(jnp.bfloat16)

            back(e, level, we, 0, n, finish)

        ready("x")
        for op in ops:
            if op == "enc":
                enc_level(0)
                enc_level(1)
            if op == "dec":
                dec_level(1)
                dec_level(0)
            if op == "decb":
                if "dec" in ops:
                    ready("q")
                    x[...] = ref["v_q"][...]
                decb_level(0)
                decb_level(1)
            if op == "encb":
                encb_level(1)
                encb_level(0)
            if not wide and op == ops[-1]:
                store(x, ref["out_x"])
            for name in MAKES[op]:
                if name == "k" and ("encb" in ops or (last and not wide)):
                    continue
                store(ref["v_" + name], ref["out_" + name])
        for key in list(waits):
            ready(key)
        for copy in outs:
            copy.wait()

    if pair is None:
        run_live()
    else:
        pl.when(live)(run_live)


def run_stage(ops, pair, wide, pairs, xs, qs, weights, state, dp_count, after=()):
    block_rows, channels = xs[0].shape
    blocks = len(xs)
    rows = block_rows * blocks
    last = pair == 0
    bf16, f32 = jnp.bfloat16, jnp.float32
    kinds = {
        "n": ((2, rows, channels), bf16), "r": ((2, rows, 128), f32), "ga": ((2, rows, channels), f32),
        "nd": ((2, rows, channels), bf16), "rd": ((2, rows, 128), f32), "gb": ((2, rows, channels), f32),
        "k": ((2, rows, channels), bf16),
        "nc": ((rows, channels // dp_count), bf16), "mc": ((rows, 2 * channels // dp_count), bf16),
        "u": ((rows, channels), bf16), "e": ((rows, channels), bf16),
    }
    names, args = [], []
    for b, value in enumerate(xs):
        names.append("x%d" % b)
        args.append(value)
    if "dec" in ops and "decb" in ops:
        for b, value in enumerate(qs):
            names.append("q%d" % b)
            args.append(value)
    for kind, users in (("we", ("enc", "encb")), ("wd", ("dec", "decb"))):
        if any(op in users for op in ops):
            names += [kind + "_own", kind + "_oth"]
            args += list(weights[kind])
    made = set()
    for op in ops:
        for name in NEEDS[op]:
            if name not in made and name not in names:
                if name == "k" and "decb" in ops:
                    continue
                names.append(name)
                args.append(state[name])
        made.update(MAKES[op])
    for i, value in enumerate(after):
        names.append("after%d" % i)
        args.append(value)
    outs = []
    if not wide:
        outs.append(("out_x", None, ((rows, channels), bf16)))
    for op in ops:
        for name in MAKES[op]:
            if name == "k" and ("encb" in ops or (last and not wide)):
                continue
            outs.append(("out_" + name, name, kinds[name]))
        if wide:
            for name in SENDS[op]:
                for tail in ("_own", "_send"):
                    outs.append((name + tail, name + tail, kinds[name]))
    aliases = {}
    for i, (_, key, _) in enumerate(outs):
        if key is not None and key in state:
            if key in names:
                aliases[names.index(key)] = i
            else:
                aliases[len(args)] = i
                names.append("prior_" + key)
                args.append(state[key])
    in_count = len(args)
    names += [o[0] for o in outs]
    scratch = {"v_x": ((rows, channels), bf16), "v_y": ((rows, channels), f32)}
    if "dec" in ops and "decb" in ops:
        scratch["v_q"] = ((rows, channels), bf16)
    for op in ops:
        for name in NEEDS[op] + MAKES[op]:
            scratch["v_" + name] = kinds[name]
        if op in ("enc", "encb"):
            scratch["v_we"] = ((2, channels, channels), bf16)
        else:
            scratch["v_wd"] = ((2, 2 * channels, channels), bf16)
        if op == "decb":
            scratch["v_u"] = ((2, rows, channels), bf16)
        if op == "encb":
            scratch["v_e"] = ((2, rows, channels), bf16)
    names += list(scratch) + ["sems"]
    cfg = dict(ops=ops, pair=pair, wide=wide, last=last, blocks=blocks, names=names, dp_count=dp_count,
               unroll=pairs <= 2)
    any_spec = pl.BlockSpec(memory_space=pl.ANY)
    flops = 2 * rows * channels * channels * 4 * len(ops)
    results = pl.pallas_call(
        functools.partial(stage_kernel, cfg),
        name=("wide_" if wide else "chain_") + "_".join(ops),
        out_shape=[jax.ShapeDtypeStruct(*o[2]) for o in outs],
        in_specs=[any_spec] * in_count,
        out_specs=[any_spec] * len(outs),
        scratch_shapes=[pltpu.VMEM(*s) for s in scratch.values()] + [pltpu.SemaphoreType.DMA((64,))],
        input_output_aliases=aliases,
        compiler_params=pltpu.CompilerParams(vmem_limit_bytes=VMEM_LIMIT),
        cost_estimate=pl.CostEstimate(
            flops=flops, bytes_accessed=8 * 1024 * 1024, transcendentals=0
        ),
    )(*args)
    state = dict(state)
    x_out = None
    for (name, key, _), value in zip(outs, results):
        if key is None:
            x_out = value
        else:
            state[key] = value
    return x_out, state


def wgrad_kernel(a_own, a_oth, b_own, b_oth, out):
    for j in range(0, out.shape[1], TILE):
        sl = slice(j, j + TILE)
        out[:, sl] = dot_rows(a_own[...], b_own[:, sl]) + dot_rows(a_oth[...], b_oth[:, sl])


def wgrad(a_own, a_oth, b_own, b_oth):
    width, channels = a_own.shape[1], b_own.shape[1]
    vmem = pl.BlockSpec(memory_space=pltpu.VMEM)
    return pl.pallas_call(
        wgrad_kernel,
        out_shape=jax.ShapeDtypeStruct((width, channels), jnp.float32),
        in_specs=[vmem] * 4,
        out_specs=vmem,
        compiler_params=pltpu.CompilerParams(vmem_limit_bytes=VMEM_LIMIT),
        cost_estimate=pl.CostEstimate(
            flops=4 * a_own.shape[0] * width * channels, bytes_accessed=4 * 1024 * 1024, transcendentals=0
        ),
    )(a_own, a_oth, b_own, b_oth)


def body(inputs, cotangent, enc_weights, dec_weights):
    section_count = lax.axis_size("section")
    dp_count = lax.axis_size("dp")
    core = lax.rem(lax.axis_index("section"), 2)
    pairs = section_count // 2
    batches, row_count, channels = inputs.shape
    half = batches * row_count // 2

    def my_rows(values):
        flat = values.reshape(2, half, channels)
        return lax.dynamic_index_in_dim(flat, core, 0, keepdims=False)

    def swap(value):
        return lax.ppermute(value, "section", [(i, i ^ 1) for i in range(section_count)])

    def over_dp(value):
        return [value] + [
            lax.ppermute(value, "dp", [(i, (i + k) % dp_count) for i in range(dp_count)])
            for k in range(1, dp_count)
        ]

    def hop(value, source, target, reach):
        return [
            lax.ppermute(
                value,
                ("section", "dp"),
                [
                    ((2 * source + c) * dp_count + d, (2 * target + c) * dp_count + (d + k) % dp_count)
                    for c in range(2)
                    for d in range(dp_count)
                ],
            )
            for k in range(reach)
        ]

    we, wd = enc_weights[0], dec_weights[0]
    weights = {"we": (we, swap(we)), "wd": (wd, swap(wd))}
    x0, cot = my_rows(inputs), my_rows(cotangent)
    x_all, cot_all = (over_dp(x0), over_dp(cot)) if pairs <= 2 else ([], [])

    visits = [("enc", k) for k in range(pairs)]
    visits += [("dec", k) for k in reversed(range(pairs))]
    visits += [("decb", k) for k in range(pairs)]
    visits += [("encb", k) for k in reversed(range(pairs))]
    stages = []
    for op, k in visits:
        if pairs <= 2 and stages and stages[-1][1] == k:
            stages[-1] = (stages[-1][0] + (op,), k)
        else:
            stages.append(((op,), k))

    chain, wide = {}, {}
    if pairs <= 2:
        arrived, waiting = x_all, None
        for i, (ops, k) in enumerate(stages[:-1]):
            x_out, chain = run_stage(
                ops, k, False, pairs, arrived[:1], [cot], weights, chain, dp_count
            )
            if waiting is not None:
                w_ops, w_k, w_x = waiting
                _, wide = run_stage(
                    w_ops, w_k, True, pairs, w_x, cot_all, weights, wide, dp_count, after=(x_out,)
                )
            waiting = (ops, k, arrived)
            arrived = hop(x_out, k, stages[i + 1][1], dp_count)
        for w_ops, w_k, w_x in (waiting, stages[-1] + (arrived,)):
            _, wide = run_stage(w_ops, w_k, True, pairs, w_x, cot_all, weights, wide, dp_count)
    else:
        my_pair = lax.div(lax.axis_index("section"), 2)
        arrived = x0
        for i, (ops, k) in enumerate(stages):
            if i % pairs == 0:
                entry = arrived
            else:
                entry = jnp.where(my_pair == k, arrived, entry)
            if i % pairs == pairs - 1:
                _, wide = run_stage(
                    ops, None, True, pairs, over_dp(entry), [], weights, wide, dp_count
                )
            if i == len(stages) - 1:
                break
            x_out, chain = run_stage(ops, k, False, pairs, [arrived], [], weights, chain, dp_count)
            target = stages[i + 1][1]
            if stages[i + 1] == (("decb",), 0):
                arrived = cot
            elif target == k:
                arrived = x_out
            else:
                arrived = hop(x_out, k, target, 1)[0]

    other = {name: swap(wide[name + "_send"]) for name in ("nc", "mc", "u", "e")}
    enc_grads = wgrad(wide["nc_own"], other["nc"], wide["e_own"], other["e"])
    dec_grads = wgrad(wide["mc_own"], other["mc"], wide["u_own"], other["u"])
    return (enc_grads[None], dec_grads[None])


def solution(mesh):
    in_specs = (
        P(None, ("group", "dp"), None),
        P(None, ("group", "dp"), None),
        P("section", None, None),
        P("section", None, None),
    )
    out_specs = (P(("group", "section"), "dp", None), P(("group", "section"), "dp", None))
    return jax.shard_map(body, mesh=mesh, in_specs=in_specs, out_specs=out_specs, check_vma=False)
```

time: 388 us -> 145 us (0.37)
  waiting for transfers between devices: 186 us -> 26.6 us
  matrix products: 57.2 us -> 0 us
  Pallas kernels: 0 us -> 45.8 us
  other arithmetic: 33.8 us -> 0 us
  starting transfers between devices: 77.8 us -> 63.6 us
  between operations: 14.2 us -> 1.31 us
  local copies, waits for them, and re-layouts: 14.3 us -> 6.77 us
    reduce_scatter x2 -> x0, waiting for transfers between devices: 117 us -> none  [the longest x1 76.4 us: body(): lax.psum_scatter(jnp.stack([decode_wgrad(merged(dec_inputs, 0), merged(sk...]
    dot_general x18 -> x0, matrix products: 57.2 us -> none  [the longest x8 27.1 us: transpose_dot(): lax.dot_general(left, right, (((1,), (1,)), ((), ())), preferred_element_...]
    pallas_call x0 -> x11, Pallas kernels: none -> 45.8 us  [the longest x9 39.6 us: run_stage(): pl.pallas_call(functools.partial(stage_kernel, cfg), name=('wide_' if wid...]
    ppermute x28, waiting for transfers between devices: 68.5 us -> 26.6 us  [the longest x16 15.6 us: hop(): lax.ppermute(value, ('section', 'dp'), [((2 * source + c) * dp_count + d,...]
    ppermute x28, starting transfers between devices: 77.7 us -> 63.6 us  [the longest x16 51.3 us: hop(): lax.ppermute(value, ('section', 'dp'), [((2 * source + c) * dp_count + d,...]
    dynamic_slice x49 -> x0, local copies, waits for them, and re-layouts: 12.3 us -> none  [pick(): return lax.dynamic_index_in_dim(buffer, position, 0, keepdims=False)]
    select_n x28 -> x0, other arithmetic: 12.2 us -> none  [the longest x7 6.11 us: climb_step(): incoming = jnp.where(section_index == 0, pick(cotangent, micro_slot), inbox)]
    convert_element_type x7 -> x0, other arithmetic: 9.55 us -> none  [the longest x4 3.83 us: return_all(): grads = summed.astype(jnp.bfloat16)]
  transfers between devices with their start and end apart: 30 -> 28, of which waited for: 23 -> 6; matrix products, arithmetic and copies ran while one was open for 7% -> 1% of each run, Pallas kernels for 0% -> 29%
where the time goes in v1:
time: 145 us; the launch traced here: 144 us
  starting transfers between devices  63.6 us (44%)
  Pallas kernels  45.8 us (32%)
  waiting for transfers between devices  26.6 us (18%)
  local copies, waits for them, and re-layouts  6.77 us (5%)
    ppermute x16, starting transfers between devices, hop(): lax.ppermute(value, ('section', 'dp'), [((2 * source + c) * dp_count + d,...  51.3 us
    pallas_call x9, Pallas kernels, run_stage(): pl.pallas_call(functools.partial(stage_kernel, cfg), name=('wide_' if wid...  39.6 us
    ppermute x16, waiting for transfers between devices, hop(): lax.ppermute(value, ('section', 'dp'), [((2 * source + c) * dp_count + d,...  15.6 us
    ppermute x6, starting transfers between devices, over_dp(): lax.ppermute(value, 'dp', [(i, (i + k) % dp_count) for i in range(dp_coun...  10.9 us
    ppermute x6, waiting for transfers between devices, swap(): lax.ppermute(value, 'section', [(i, i ^ 1) for i in range(section_count)])  10.5 us
    pallas_call x2, Pallas kernels, wgrad(): pl.pallas_call(wgrad_kernel, out_shape=jax.ShapeDtypeStruct((width, chann...  6.24 us
    unnamed x72, local copies, waits for them, and re-layouts  5.44 us
  transfers between devices with their start and end apart: 28, of which 6 were waited for; matrix products, arithmetic and copies ran while one was open for 1% of the time, Pallas kernels for 29%

profile of v1, /device:TPU:0, one launch (start us, length us, event | category | flops | bytes accessed | tf_op | source)
XLA Modules:
  0.0 144.0 jit_solution(7508977691201800275)
XLA Ops:
  2.3 8.8 %collective-permute-done.refs_2_.refs_5_ = bf16[1024,1024]{1,0:T(8,128)(2,1)S(1)} collective-permute-done((bf16[1024,1024]{1,0:T(8,128)(2,1)}, bf16[1024,1024]{1,0:T(8,128)(2,1)S(1)}, u32[]{:S(2)}, u32[]{:S(2)}) %collective-permute-start) | collective-permute-done | bytes 2097184 | tf_op jit(solution)/shard_map/ppermute | solution.py:425
  11.1 1.3 copy-done.1
  12.4 4.9 %chain_enc.1 = (bf16[64,1024]{1,0:T(8,128)(2,1)}, bf16[2,64,1024]{2,1,0:T(8,128)(2,1)}, f32[2,64,128]{2,1,0:T(8,128)}, f32[2,64,1024]{2,1,0:T(8,128)}) custom-call(bf16[64,1024]{1,0:T(8,128)(2,1)} %dynamic-slice_bitcast_fusion.1.refs_0_, bf16[1024,1024]{1,0:T(8,128)(2,1)} %bitcast.19, bf16[1024,1024]{1,0:T(8,128)(2,1)} %copy-done.1), custom_call_target="tpu_custom_call" | custom-call | flops 536870912 | bytes 8388608 | tf_op jit(solution)/shard_map/chain_enc/pallas_call | solution.py:368
  17.3 1.3 collective-permute-start.1
  18.6 3.6 %collective-permute-done.1.refs_0_ = bf16[64,1024]{1,0:T(8,128)(2,1)S(1)} collective-permute-done((bf16[64,1024]{1,0:T(8,128)(2,1)}, bf16[64,1024]{1,0:T(8,128)(2,1)S(1)}, u32[]{:S(2)}, u32[]{:S(2)}) %collective-permute-start.1) | collective-permute-done | bytes 131104 | tf_op jit(solution)/shard_map/ppermute | solution.py:435
  23.4 1.3 collective-permute-start.6
  24.8 2.9 %collective-permute-start.7 = (bf16[64,1024]{1,0:T(8,128)(2,1)S(1)}, bf16[64,1024]{1,0:T(8,128)(2,1)S(1)}, u32[]{:S(2)}, u32[]{:S(2)}) collective-permute-start(bf16[64,1024]{1,0:T(8,128)(2,1)S(1)} %copy-done.5), channel_id=1, source_target_pairs={{0,1},{1,2},{2,3},{3,0},{4,5},{5,6},{6,7},{7,4},{8,9},{9,10},{10,1... | collective-permute-start | bytes 393224 | tf_op jit(solution)/shard_map/ppermute | solution.py:429
  27.7 2.6 %collective-permute-start.8 = (bf16[64,1024]{1,0:T(8,128)(2,1)S(1)}, bf16[64,1024]{1,0:T(8,128)(2,1)S(1)}, u32[]{:S(2)}, u32[]{:S(2)}) collective-permute-start(bf16[64,1024]{1,0:T(8,128)(2,1)S(1)} %copy-done.5), channel_id=1, source_target_pairs={{0,2},{1,3},{2,0},{3,1},{4,6},{5,7},{6,4},{7,5},{8,10},{9,11},{10,... | collective-permute-start | bytes 393224 | tf_op jit(solution)/shard_map/ppermute | solution.py:429
  30.3 1.3 collective-permute-start.9
  33.0 5.3 %collective-permute-done.6.refs_0_ = bf16[64,1024]{1,0:T(8,128)(2,1)S(1)} collective-permute-done((bf16[64,1024]{1,0:T(8,128)(2,1)}, bf16[64,1024]{1,0:T(8,128)(2,1)S(1)}, u32[]{:S(2)}, u32[]{:S(2)}) %collective-permute-start.6) | collective-permute-done | bytes 131104 | tf_op jit(solution)/shard_map/ppermute | solution.py:435
  38.3 6.2 %collective-permute-start.2 = (bf16[64,1024]{1,0:T(8,128)(2,1)S(1)}, bf16[64,1024]{1,0:T(8,128)(2,1)S(1)}, u32[]{:S(2)}, u32[]{:S(2)}) collective-permute-start(bf16[64,1024]{1,0:T(8,128)(2,1)S(1)} %copy-done.27), channel_id=1, source_target_pairs={{0,9},{1,10},{2,11},{3,8},{4,13},{5,14},{6,15},{7,12},{16,25},{17,... | collective-permute-start | bytes 393224 | tf_op jit(solution)/shard_map/ppermute | solution.py:435
  44.5 8.2 %chain_dec_decb.1 = (bf16[64,1024]{1,0:T(8,128)(2,1)}, bf16[2,64,1024]{2,1,0:T(8,128)(2,1)}, f32[2,64,128]{2,1,0:T(8,128)}, f32[2,64,1024]{2,1,0:T(8,128)}) custom-call(bf16[64,1024]{1,0:T(8,128)(2,1)} %copy-done.8, bf16[64,1024]{1,0:T(8,128)(2,1)} %dynamic-slice_bitcast_fusion.refs_1_.refs_4_, ...), custom_call_target="tpu_custom_call", output_to_operand_aliasing={{1}: (6, {}), {2}: (7, {}), {3}: (8, {})} | custom-call | flops 1073741824 | bytes 8388608 | tf_op jit(solution)/shard_map/chain_dec_decb/pallas_call | solution.py:368
  52.7 1.3 collective-permute-start.3
  54.0 1.8 %collective-permute-start.4 = (bf16[64,1024]{1,0:T(8,128)(2,1)S(1)}, bf16[64,1024]{1,0:T(8,128)(2,1)S(1)}, u32[]{:S(2)}, u32[]{:S(2)}) collective-permute-start(bf16[64,1024]{1,0:T(8,128)(2,1)S(1)} %copy-done.27), channel_id=1, source_target_pairs={{0,11},{1,8},{2,9},{3,10},{4,15},{5,12},{6,13},{7,14},{16,27},{17,... | collective-permute-start | bytes 393224 | tf_op jit(solution)/shard_map/ppermute | solution.py:435
  55.9 1.4 collective-permute-start.11
  57.4 6.3 %wide_enc.1 = (bf16[2,256,1024]{2,1,0:T(8,128)(2,1)}, f32[2,256,128]{2,1,0:T(8,128)}, f32[2,256,1024]{2,1,0:T(8,128)}, bf16[256,256]{1,0:T(8,128)(2,1)}, bf16[256,256]{1,0:T(8,128)(2,1)}) custom-call(bf16[64,1024]{1,0:T(8,128)(2,1)} %dynamic-slice_bitcast_fusion.1.refs_0_, bf16[64,1024]{1,0:T(8,128)(2,1)} %copy-done.33, bf16[64,1024]{1,0:T(8,128)(2,1)} %copy-done.34, ...), custom_call_target="tpu_custom_call" | custom-call | flops 2147483648 | bytes 8388608 | tf_op jit(solution)/shard_map/wide_enc/pallas_call | solution.py:368
  63.7 3.2 %collective-permute-start.20 = (bf16[64,1024]{1,0:T(8,128)(2,1)}, bf16[64,1024]{1,0:T(8,128)(2,1)S(1)}, u32[]{:S(2)}, u32[]{:S(2)}) collective-permute-start(bf16[64,1024]{1,0:T(8,128)(2,1)} %dynamic-slice_bitcast_fusion.refs_1_.refs_4_), channel_id=1, source_target_pairs={{0,2},{1,3},{2,0},{3,1},{4,6},{5,7},{6,4},{7,5},{8,10},{9,11},{10,... | collective-permute-start | bytes 393224 | tf_op jit(solution)/shard_map/ppermute | solution.py:429
  68.4 1.3 collective-permute-start.17
  69.7 1.3 collective-permute-start.18
  72.9 24.7 %collective-permute-start.22 = (bf16[64,1024]{1,0:T(8,128)(2,1)S(1)}, bf16[64,1024]{1,0:T(8,128)(2,1)S(1)}, u32[]{:S(2)}, u32[]{:S(2)}) collective-permute-start(bf16[64,1024]{1,0:T(8,128)(2,1)S(1)} %copy-done.9), channel_id=1, source_target_pairs={{0,9},{1,10},{2,11},{3,8},{4,13},{5,14},{6,15},{7,12},{16,25},{17,... | collective-permute-start | bytes 393224 | tf_op jit(solution)/shard_map/ppermute | solution.py:435
  97.6 2.1 %collective-permute-start.23 = (bf16[64,1024]{1,0:T(8,128)(2,1)S(1)}, bf16[64,1024]{1,0:T(8,128)(2,1)S(1)}, u32[]{:S(2)}, u32[]{:S(2)}) collective-permute-start(bf16[64,1024]{1,0:T(8,128)(2,1)S(1)} %copy-done.9), channel_id=1, source_target_pairs={{0,10},{1,11},{2,8},{3,9},{4,14},{5,15},{6,12},{7,13},{16,26},{17,... | collective-permute-start | bytes 393224 | tf_op jit(solution)/shard_map/ppermute | solution.py:435
  99.7 2.2 %collective-permute-start.24 = (bf16[64,1024]{1,0:T(8,128)(2,1)S(1)}, bf16[64,1024]{1,0:T(8,128)(2,1)S(1)}, u32[]{:S(2)}, u32[]{:S(2)}) collective-permute-start(bf16[64,1024]{1,0:T(8,128)(2,1)S(1)} %copy-done.9), channel_id=1, source_target_pairs={{0,11},{1,8},{2,9},{3,10},{4,15},{5,12},{6,13},{7,14},{16,27},{17,... | collective-permute-start | bytes 393224 | tf_op jit(solution)/shard_map/ppermute | solution.py:435
  101.9 1.3 collective-permute-start.12
  103.3 1.3 collective-permute-start.13
  104.6 11.1 %wide_dec_decb.1 = (bf16[2,256,1024]{2,1,0:T(8,128)(2,1)}, f32[2,256,128]{2,1,0:T(8,128)}, f32[2,256,1024]{2,1,0:T(8,128)}, bf16[256,512]{1,0:T(8,128)(2,1)}, bf...) custom-call(bf16[64,1024]{1,0:T(8,128)(2,1)} %copy-done.8, ...), custom_call_target="tpu_custom_call", output_to_operand_aliasing={{0}: (13, {}), {1}: (14, {}), {2}: (15, {}), {3}: (16, {}),... | custom-call | flops 4294967296 | bytes 8388608 | tf_op jit(solution)/shard_map/wide_dec_decb/pallas_call | solution.py:368
  115.8 1.3 collective-permute-start.14
  117.1 1.3 collective-permute-start.15
  119.8 6.6 %collective-permute-done.14.refs_2_ = bf16[64,1024]{1,0:T(8,128)(2,1)S(1)} collective-permute-done((bf16[64,1024]{1,0:T(8,128)(2,1)S(1)}, bf16[64,1024]{1,0:T(8,128)(2,1)S(1)}, u32[]{:S(2)}, u32[]{:S(2)}) %collective-permute-start.14) | collective-permute-done | bytes 131104 | tf_op jit(solution)/shard_map/ppermute | solution.py:435
  127.1 6.6 %wide_encb.1 = (bf16[256,1024]{1,0:T(8,128)(2,1)}, bf16[256,1024]{1,0:T(8,128)(2,1)}) custom-call(bf16[64,1024]{1,0:T(8,128)(2,1)} %copy-done.12, bf16[64,1024]{1,0:T(8,128)(2,1)} %copy-done.13, bf16[64,1024]{1,0:T(8,128)(2,1)} %copy-done.20, bf16[64,1024]{1,0:T(8,128)(2,1)} %copy-done.21, ...), custom_call_target="tpu_custom_call", output_to_operand_aliasing={{0}: (10, {}), {1}: (11, {})} | custom-call | flops 2147483648 | bytes 8388608 | tf_op jit(solution)/shard_map/wide_encb/pallas_call | solution.py:368
  134.4 1.7 %collective-permute-done.26.a_oth = bf16[256,512]{1,0:T(8,128)(2,1)S(1)} collective-permute-done((bf16[256,512]{1,0:T(8,128)(2,1)S(1)}, bf16[256,512]{1,0:T(8,128)(2,1)S(1)}, u32[]{:S(2)}, u32[]{:S(2)}) %collective-permute-start.26) | collective-permute-done | bytes 262176 | tf_op jit(solution)/shard_map/ppermute | solution.py:425
  136.9 3.4 %shard_map.60 = f32[512,1024]{1,0:T(8,128)} custom-call(bf16[256,512]{1,0:T(8,128)(2,1)} %get-tuple-element.86.a_own, bf16[256,512]{1,0:T(8,128)(2,1)} %copy-done.7, bf16[256,1024]{1,0:T(8,128)(2,1)} %get-tuple-element.88.b_own, bf16[256,1024]{1,0:T(8,128)(2,1)} %copy-done.4), custom_call_target="tpu_custom_call" | custom-call | flops 536870912 | bytes 4194304 | tf_op jit(solution)/shard_map/pallas_call | solution.py:400
  141.2 2.8 %shard_map.59 = f32[256,1024]{1,0:T(8,128)} custom-call(bf16[256,256]{1,0:T(8,128)(2,1)} %get-tuple-element.62.a_own, bf16[256,256]{1,0:T(8,128)(2,1)} %copy-done.22, bf16[256,1024]{1,0:T(8,128)(2,1)} %get-tuple-element.84.b_own, bf16[256,1024]{1,0:T(8,128)(2,1)} %copy-done.6), custom_call_target="tpu_custom_call" | custom-call | flops 268435456 | bytes 4194304 | tf_op jit(solution)/shard_map/pallas_call | solution.py:400
  (109 shorter events, 11.9 us)
Async XLA Ops:
  0.6 21.6 %collective-permute-start.5 = (bf16[2048,1024]{1,0:T(8,128)(2,1)}, bf16[2048,1024]{1,0:T(8,128)(2,1)}, u32[]{:S(2)}, u32[]{:S(2)}) collective-permute-start(bf16[2048,1024]{1,0:T(8,128)(2,1)} %bitcast.11), channel_id=1, source_target_pairs={{0,4},{4,0},{8,12},{12,8},{1,5},{5,1},{9,13},{13,9},{2,6},{6,2},{1... | collective-permute-start | bytes 12582920 | tf_op jit(solution)/shard_map/ppermute | solution.py:425
  1.2 9.9 %collective-permute-start = (bf16[1024,1024]{1,0:T(8,128)(2,1)}, bf16[1024,1024]{1,0:T(8,128)(2,1)S(1)}, u32[]{:S(2)}, u32[]{:S(2)}) collective-permute-start(bf16[1024,1024]{1,0:T(8,128)(2,1)} %bitcast.18), channel_id=1, source_target_pairs={{0,4},{4,0},{8,12},{12,8},{1,5},{5,1},{9,13},{13,9},{2,6},{6,2},{1... | collective-permute-start | bytes 6291464 | tf_op jit(solution)/shard_map/ppermute | solution.py:425
  17.3 4.9 %collective-permute-start.1 = (bf16[64,1024]{1,0:T(8,128)(2,1)}, bf16[64,1024]{1,0:T(8,128)(2,1)S(1)}, u32[]{:S(2)}, u32[]{:S(2)}) collective-permute-start(bf16[64,1024]{1,0:T(8,128)(2,1)} %get-tuple-element.46), channel_id=1, source_target_pairs={{0,8},{1,9},{2,10},{3,11},{4,12},{5,13},{6,14},{7,15},{16,24},{17,... | collective-permute-start | bytes 393224 | tf_op jit(solution)/shard_map/ppermute | solution.py:435
  22.9 15.4 %copy-start.27 = (bf16[64,1024]{1,0:T(8,128)(2,1)S(1)}, bf16[64,1024]{1,0:T(8,128)(2,1)}, u32[]{:S(2)}) copy-start(bf16[64,1024]{1,0:T(8,128)(2,1)} %get-tuple-element.46) | copy-start | bytes 393220
  23.4 14.8 %collective-permute-start.6 = (bf16[64,1024]{1,0:T(8,128)(2,1)}, bf16[64,1024]{1,0:T(8,128)(2,1)S(1)}, u32[]{:S(2)}, u32[]{:S(2)}) collective-permute-start(bf16[64,1024]{1,0:T(8,128)(2,1)} %get-tuple-element.50.refs_6_), channel_id=1, source_target_pairs={{8,0},{9,1},{10,2},{11,3},{12,4},{13,5},{14,6},{15,7},{24,16},{25,... | collective-permute-start | bytes 393224 | tf_op jit(solution)/shard_map/ppermute | solution.py:435
  24.8 27.9 %collective-permute-start.7 = (bf16[64,1024]{1,0:T(8,128)(2,1)S(1)}, bf16[64,1024]{1,0:T(8,128)(2,1)S(1)}, u32[]{:S(2)}, u32[]{:S(2)}) collective-permute-start(bf16[64,1024]{1,0:T(8,128)(2,1)S(1)} %copy-done.5), channel_id=1, source_target_pairs={{0,1},{1,2},{2,3},{3,0},{4,5},{5,6},{6,7},{7,4},{8,9},{9,10},{10,1... | collective-permute-start | bytes 393224 | tf_op jit(solution)/shard_map/ppermute | solution.py:429
  27.7 26.3 %collective-permute-start.8 = (bf16[64,1024]{1,0:T(8,128)(2,1)S(1)}, bf16[64,1024]{1,0:T(8,128)(2,1)S(1)}, u32[]{:S(2)}, u32[]{:S(2)}) collective-permute-start(bf16[64,1024]{1,0:T(8,128)(2,1)S(1)} %copy-done.5), channel_id=1, source_target_pairs={{0,2},{1,3},{2,0},{3,1},{4,6},{5,7},{6,4},{7,5},{8,10},{9,11},{10,... | collective-permute-start | bytes 393224 | tf_op jit(solution)/shard_map/ppermute | solution.py:429
  30.3 25.6 %collective-permute-start.9 = (bf16[64,1024]{1,0:T(8,128)(2,1)S(1)}, bf16[64,1024]{1,0:T(8,128)(2,1)S(1)}, u32[]{:S(2)}, u32[]{:S(2)}) collective-permute-start(bf16[64,1024]{1,0:T(8,128)(2,1)S(1)} %copy-done.5), channel_id=1, source_target_pairs={{0,3},{1,0},{2,1},{3,2},{4,7},{5,4},{6,5},{7,6},{8,11},{9,8},{10,9... | collective-permute-start | bytes 393224 | tf_op jit(solution)/shard_map/ppermute | solution.py:429
  32.3 31.4 %collective-permute-start.19 = (bf16[64,1024]{1,0:T(8,128)(2,1)}, bf16[64,1024]{1,0:T(8,128)(2,1)S(1)}, u32[]{:S(2)}, u32[]{:S(2)}) collective-permute-start(bf16[64,1024]{1,0:T(8,128)(2,1)} %dynamic-slice_bitcast_fusion.refs_1_.refs_4_), channel_id=1, source_target_pairs={{0,1},{1,2},{2,3},{3,0},{4,5},{5,6},{6,7},{7,4},{8,9},{9,10},{10,1... | collective-permute-start | bytes 393224 | tf_op jit(solution)/shard_map/ppermute | solution.py:429
  38.3 28.6 %collective-permute-start.2 = (bf16[64,1024]{1,0:T(8,128)(2,1)S(1)}, bf16[64,1024]{1,0:T(8,128)(2,1)S(1)}, u32[]{:S(2)}, u32[]{:S(2)}) collective-permute-start(bf16[64,1024]{1,0:T(8,128)(2,1)S(1)} %copy-done.27), channel_id=1, source_target_pairs={{0,9},{1,10},{2,11},{3,8},{4,13},{5,14},{6,15},{7,12},{16,25},{17,... | collective-permute-start | bytes 393224 | tf_op jit(solution)/shard_map/ppermute | solution.py:435
  52.7 14.4 %collective-permute-start.3 = (bf16[64,1024]{1,0:T(8,128)(2,1)S(1)}, bf16[64,1024]{1,0:T(8,128)(2,1)S(1)}, u32[]{:S(2)}, u32[]{:S(2)}) collective-permute-start(bf16[64,1024]{1,0:T(8,128)(2,1)S(1)} %copy-done.27), channel_id=1, source_target_pairs={{0,10},{1,11},{2,8},{3,9},{4,14},{5,15},{6,12},{7,13},{16,26},{17,... | collective-permute-start | bytes 393224 | tf_op jit(solution)/shard_map/ppermute | solution.py:435
  54.0 14.4 %collective-permute-start.4 = (bf16[64,1024]{1,0:T(8,128)(2,1)S(1)}, bf16[64,1024]{1,0:T(8,128)(2,1)S(1)}, u32[]{:S(2)}, u32[]{:S(2)}) collective-permute-start(bf16[64,1024]{1,0:T(8,128)(2,1)S(1)} %copy-done.27), channel_id=1, source_target_pairs={{0,11},{1,8},{2,9},{3,10},{4,15},{5,12},{6,13},{7,14},{16,27},{17,... | collective-permute-start | bytes 393224 | tf_op jit(solution)/shard_map/ppermute | solution.py:435
  55.9 11.2 %copy-start.25 = (bf16[64,1024]{1,0:T(8,128)(2,1)S(1)}, bf16[64,1024]{1,0:T(8,128)(2,1)}, u32[]{:S(2)}) copy-start(bf16[64,1024]{1,0:T(8,128)(2,1)} %get-tuple-element.50.refs_6_) | copy-start | bytes 393220
  55.9 13.8 %collective-permute-start.11 = (bf16[64,1024]{1,0:T(8,128)(2,1)}, bf16[64,1024]{1,0:T(8,128)(2,1)S(1)}, u32[]{:S(2)}, u32[]{:S(2)}) collective-permute-start(bf16[64,1024]{1,0:T(8,128)(2,1)} %get-tuple-element.56.refs_8_), channel_id=1, source_target_pairs={{0,8},{1,9},{2,10},{3,11},{4,12},{5,13},{6,14},{7,15},{16,24},{17,... | collective-permute-start | bytes 393224 | tf_op jit(solution)/shard_map/ppermute | solution.py:435
  63.7 9.2 %collective-permute-start.20 = (bf16[64,1024]{1,0:T(8,128)(2,1)}, bf16[64,1024]{1,0:T(8,128)(2,1)S(1)}, u32[]{:S(2)}, u32[]{:S(2)}) collective-permute-start(bf16[64,1024]{1,0:T(8,128)(2,1)} %dynamic-slice_bitcast_fusion.refs_1_.refs_4_), channel_id=1, source_target_pairs={{0,2},{1,3},{2,0},{3,1},{4,6},{5,7},{6,4},{7,5},{8,10},{9,11},{10,... | collective-permute-start | bytes 393224 | tf_op jit(solution)/shard_map/ppermute | solution.py:429
  66.9 30.7 %collective-permute-start.21 = (bf16[64,1024]{1,0:T(8,128)(2,1)}, bf16[64,1024]{1,0:T(8,128)(2,1)S(1)}, u32[]{:S(2)}, u32[]{:S(2)}) collective-permute-start(bf16[64,1024]{1,0:T(8,128)(2,1)} %dynamic-slice_bitcast_fusion.refs_1_.refs_4_), channel_id=1, source_target_pairs={{0,3},{1,0},{2,1},{3,2},{4,7},{5,4},{6,5},{7,6},{8,11},{9,8},{10,9... | collective-permute-start | bytes 393224 | tf_op jit(solution)/shard_map/ppermute | solution.py:429
  67.1 32.6 %collective-permute-start.16 = (bf16[64,1024]{1,0:T(8,128)(2,1)S(1)}, bf16[64,1024]{1,0:T(8,128)(2,1)S(1)}, u32[]{:S(2)}, u32[]{:S(2)}) collective-permute-start(bf16[64,1024]{1,0:T(8,128)(2,1)S(1)} %copy-done.25), channel_id=1, source_target_pairs={{8,1},{9,2},{10,3},{11,0},{12,5},{13,6},{14,7},{15,4},{24,17},{25,... | collective-permute-start | bytes 393224 | tf_op jit(solution)/shard_map/ppermute | solution.py:435
  68.4 33.5 %collective-permute-start.17 = (bf16[64,1024]{1,0:T(8,128)(2,1)S(1)}, bf16[64,1024]{1,0:T(8,128)(2,1)S(1)}, u32[]{:S(2)}, u32[]{:S(2)}) collective-permute-start(bf16[64,1024]{1,0:T(8,128)(2,1)S(1)} %copy-done.25), channel_id=1, source_target_pairs={{8,2},{9,3},{10,0},{11,1},{12,6},{13,7},{14,4},{15,5},{24,18},{25,... | collective-permute-start | bytes 393224 | tf_op jit(solution)/shard_map/ppermute | solution.py:435
  69.7 33.5 %collective-permute-start.18 = (bf16[64,1024]{1,0:T(8,128)(2,1)S(1)}, bf16[64,1024]{1,0:T(8,128)(2,1)S(1)}, u32[]{:S(2)}, u32[]{:S(2)}) collective-permute-start(bf16[64,1024]{1,0:T(8,128)(2,1)S(1)} %copy-done.25), channel_id=1, source_target_pairs={{8,3},{9,0},{10,1},{11,2},{12,7},{13,4},{14,5},{15,6},{24,19},{25,... | collective-permute-start | bytes 393224 | tf_op jit(solution)/shard_map/ppermute | solution.py:435
  72.9 31.6 %copy-start.28 = (bf16[64,1024]{1,0:T(8,128)(2,1)}, bf16[64,1024]{1,0:T(8,128)(2,1)S(1)}, u32[]{:S(2)}) copy-start(bf16[64,1024]{1,0:T(8,128)(2,1)S(1)} %collective-permute-done.20.refs_6_) | copy-start | bytes 393220
  72.9 42.9 %collective-permute-start.22 = (bf16[64,1024]{1,0:T(8,128)(2,1)S(1)}, bf16[64,1024]{1,0:T(8,128)(2,1)S(1)}, u32[]{:S(2)}, u32[]{:S(2)}) collective-permute-start(bf16[64,1024]{1,0:T(8,128)(2,1)S(1)} %copy-done.9), channel_id=1, source_target_pairs={{0,9},{1,10},{2,11},{3,8},{4,13},{5,14},{6,15},{7,12},{16,25},{17,... | collective-permute-start | bytes 393224 | tf_op jit(solution)/shard_map/ppermute | solution.py:435
  97.6 19.5 %collective-permute-start.23 = (bf16[64,1024]{1,0:T(8,128)(2,1)S(1)}, bf16[64,1024]{1,0:T(8,128)(2,1)S(1)}, u32[]{:S(2)}, u32[]{:S(2)}) collective-permute-start(bf16[64,1024]{1,0:T(8,128)(2,1)S(1)} %copy-done.9), channel_id=1, source_target_pairs={{0,10},{1,11},{2,8},{3,9},{4,14},{5,15},{6,12},{7,13},{16,26},{17,... | collective-permute-start | bytes 393224 | tf_op jit(solution)/shard_map/ppermute | solution.py:435
  99.7 18.7 %collective-permute-start.24 = (bf16[64,1024]{1,0:T(8,128)(2,1)S(1)}, bf16[64,1024]{1,0:T(8,128)(2,1)S(1)}, u32[]{:S(2)}, u32[]{:S(2)}) collective-permute-start(bf16[64,1024]{1,0:T(8,128)(2,1)S(1)} %copy-done.9), channel_id=1, source_target_pairs={{0,11},{1,8},{2,9},{3,10},{4,15},{5,12},{6,13},{7,14},{16,27},{17,... | collective-permute-start | bytes 393224 | tf_op jit(solution)/shard_map/ppermute | solution.py:435
  101.9 17.8 %collective-permute-start.12 = (bf16[64,1024]{1,0:T(8,128)(2,1)}, bf16[64,1024]{1,0:T(8,128)(2,1)S(1)}, u32[]{:S(2)}, u32[]{:S(2)}) collective-permute-start(bf16[64,1024]{1,0:T(8,128)(2,1)} %chain_decb_encb.1.refs_12_), channel_id=1, source_target_pairs={{8,0},{9,1},{10,2},{11,3},{12,4},{13,5},{14,6},{15,7},{24,16},{25,... | collective-permute-start | bytes 393224 | tf_op jit(solution)/shard_map/ppermute | solution.py:435
  103.3 16.5 %collective-permute-start.13 = (bf16[64,1024]{1,0:T(8,128)(2,1)}, bf16[64,1024]{1,0:T(8,128)(2,1)S(1)}, u32[]{:S(2)}, u32[]{:S(2)}) collective-permute-start(bf16[64,1024]{1,0:T(8,128)(2,1)} %chain_decb_encb.1.refs_12_), channel_id=1, source_target_pairs={{8,1},{9,2},{10,3},{11,0},{12,5},{13,6},{14,7},{15,4},{24,17},{25,... | collective-permute-start | bytes 393224 | tf_op jit(solution)/shard_map/ppermute | solution.py:435
  104.6 11.2 %copy-start.10 = (bf16[64,1024]{1,0:T(8,128)(2,1)S(1)}, bf16[64,1024]{1,0:T(8,128)(2,1)}, u32[]{:S(2)}) copy-start(bf16[64,1024]{1,0:T(8,128)(2,1)} %chain_decb_encb.1.refs_12_) | copy-start | bytes 393220
  115.8 10.6 %collective-permute-start.14 = (bf16[64,1024]{1,0:T(8,128)(2,1)S(1)}, bf16[64,1024]{1,0:T(8,128)(2,1)S(1)}, u32[]{:S(2)}, u32[]{:S(2)}) collective-permute-start(bf16[64,1024]{1,0:T(8,128)(2,1)S(1)} %copy-done.10), channel_id=1, source_target_pairs={{8,2},{9,3},{10,0},{11,1},{12,6},{13,7},{14,4},{15,5},{24,18},{25,... | collective-permute-start | bytes 393224 | tf_op jit(solution)/shard_map/ppermute | solution.py:435
  117.1 9.3 %collective-permute-start.15 = (bf16[64,1024]{1,0:T(8,128)(2,1)S(1)}, bf16[64,1024]{1,0:T(8,128)(2,1)S(1)}, u32[]{:S(2)}, u32[]{:S(2)}) collective-permute-start(bf16[64,1024]{1,0:T(8,128)(2,1)S(1)} %copy-done.10), channel_id=1, source_target_pairs={{8,3},{9,0},{10,1},{11,2},{12,7},{13,4},{14,5},{15,6},{24,19},{25,... | collective-permute-start | bytes 393224 | tf_op jit(solution)/shard_map/ppermute | solution.py:435
  119.7 16.4 %collective-permute-start.27 = (bf16[256,1024]{1,0:T(8,128)(2,1)}, bf16[256,1024]{1,0:T(8,128)(2,1)S(1)}, u32[]{:S(2)}, u32[]{:S(2)}) collective-permute-start(bf16[256,1024]{1,0:T(8,128)(2,1)} %get-tuple-element.89), channel_id=1, source_target_pairs={{0,4},{4,0},{8,12},{12,8},{1,5},{5,1},{9,13},{13,9},{2,6},{6,2},{1... | collective-permute-start | bytes 1572872 | tf_op jit(solution)/shard_map/ppermute | solution.py:425
  133.7 6.7 %collective-permute-start.25 = (bf16[256,1024]{1,0:T(8,128)(2,1)}, bf16[256,1024]{1,0:T(8,128)(2,1)S(1)}, u32[]{:S(2)}, u32[]{:S(2)}) collective-permute-start(bf16[256,1024]{1,0:T(8,128)(2,1)} %get-tuple-element.85), channel_id=1, source_target_pairs={{0,4},{4,0},{8,12},{12,8},{1,5},{5,1},{9,13},{13,9},{2,6},{6,2},{1... | collective-permute-start | bytes 1572872 | tf_op jit(solution)/shard_map/ppermute | solution.py:425
  133.8 2.3 %collective-permute-start.26 = (bf16[256,512]{1,0:T(8,128)(2,1)S(1)}, bf16[256,512]{1,0:T(8,128)(2,1)S(1)}, u32[]{:S(2)}, u32[]{:S(2)}) collective-permute-start(bf16[256,512]{1,0:T(8,128)(2,1)S(1)} %copy-done.24), channel_id=1, source_target_pairs={{0,4},{4,0},{8,12},{12,8},{1,5},{5,1},{9,13},{13,9},{2,6},{6,2},{1... | collective-permute-start | bytes 786440 | tf_op jit(solution)/shard_map/ppermute | solution.py:425
  134.3 6.1 %collective-permute-start.10 = (bf16[256,256]{1,0:T(8,128)(2,1)S(1)}, bf16[256,256]{1,0:T(8,128)(2,1)S(1)}, u32[]{:S(2)}, u32[]{:S(2)}) collective-permute-start(bf16[256,256]{1,0:T(8,128)(2,1)S(1)} %copy-done.19), channel_id=1, source_target_pairs={{0,4},{4,0},{8,12},{12,8},{1,5},{5,1},{9,13},{13,9},{2,6},{6,2},{1... | collective-permute-start | bytes 393224 | tf_op jit(solution)/shard_map/ppermute | solution.py:425
  (32 other events, 103.4 us)

commit v2 on v0

v2 whole, which is shorter than its diff:
```python
import functools

import jax
import jax.numpy as jnp
from jax import lax
from jax.experimental import pallas as pl
from jax.experimental.pallas import tpu as pltpu
from jax.sharding import PartitionSpec as P

EPS = 1e-06
TILE = 256
VMEM_LIMIT = 22 * 1024 * 1024
WIDE_LIMIT = 40 * 1024 * 1024


def dot(left, right):
    return lax.dot_general(
        left, right, (((1,), (0,)), ((), ())), preferred_element_type=jnp.float32
    )


def dot_t(left, right):
    return lax.dot_general(
        left, right, (((1,), (1,)), ((), ())), preferred_element_type=jnp.float32
    )


def dot_rows(left, right):
    return lax.dot_general(
        left, right, (((0,), (0,)), ((), ())), preferred_element_type=jnp.float32
    )


NEEDS = {
    "enc": (),
    "dec": ("n",),
    "decb": ("n", "r", "nd", "rd", "gb"),
    "encb": ("n", "r", "ga", "k"),
}
MAKES = {
    "enc": ("n", "r", "ga"),
    "dec": ("nd", "rd", "gb"),
    "decb": ("k",),
    "encb": (),
}
VMEM = pl.BlockSpec(memory_space=pltpu.VMEM)
ANY = pl.BlockSpec(memory_space=pl.ANY)


def own_kernel(own, both, sem):
    core = lax.rem(lax.axis_index("section"), 2)
    copy = pltpu.make_async_copy(own, both.at[core], sem)
    copy.start()
    copy.wait()


def other_kernel(before, other, both, sem):
    core = lax.rem(lax.axis_index("section"), 2)
    copy = pltpu.make_async_copy(other, both.at[1 - core], sem)
    copy.start()
    copy.wait()


def load_own(own):
    return pl.pallas_call(
        own_kernel,
        name="load_own",
        out_shape=jax.ShapeDtypeStruct((2,) + own.shape, own.dtype),
        in_specs=[pl.BlockSpec(memory_space=pltpu.HBM)],
        out_specs=VMEM,
        scratch_shapes=[pltpu.SemaphoreType.DMA],
        compiler_params=pltpu.CompilerParams(vmem_limit_bytes=VMEM_LIMIT),
    )(own)


def load_other(both, other):
    return pl.pallas_call(
        other_kernel,
        name="load_other",
        out_shape=jax.ShapeDtypeStruct(both.shape, both.dtype),
        in_specs=[VMEM, ANY],
        out_specs=VMEM,
        input_output_aliases={0: 0},
        scratch_shapes=[pltpu.SemaphoreType.DMA],
        compiler_params=pltpu.CompilerParams(vmem_limit_bytes=VMEM_LIMIT),
    )(both, other)


def stage_kernel(cfg, *refs):
    ops, pair, wide, dp_count = cfg["ops"], cfg["pair"], cfg["wide"], cfg["dp_count"]
    ref = dict(zip(cfg["names"], refs))
    section = lax.axis_index("section")
    core = lax.rem(section, 2)
    dp = lax.axis_index("dp")
    x = ref["out_x"] if "out_x" in ref else ref["work_x"]
    ybuf = ref.get("ybuf")
    rows, channels = x.shape
    tile_count = channels // TILE
    skip_k = cfg["skip_k"]

    def for_tiles(step, carry=0):
        def run(j, carry):
            at = j * TILE
            if not isinstance(j, int):
                at = pl.multiple_of(at, TILE)
            return step(at, pl.ds(at, TILE), carry)

        if cfg["unroll"]:
            for j in range(tile_count):
                carry = run(j, carry)
            return carry
        return lax.fori_loop(0, tile_count, run, carry)

    def by_core(level, name, cols, value):
        @pl.when(core == level)
        def _():
            ref[name + "_own"][:, cols] = value

        @pl.when(core != level)
        def _():
            ref[name + "_send"][:, cols] = value

    def normalize(level, n_ref, r_ref):
        values = x[...].astype(jnp.float32)
        inv = lax.rsqrt(jnp.mean(values * values, axis=-1, keepdims=True) + EPS)
        n_ref[level] = (values * inv).astype(jnp.bfloat16)
        r_ref[level] = jnp.broadcast_to(inv, (rows, 128))

    def activate(pre, gain_ref, level, sl):
        sigma = jax.nn.sigmoid(pre)
        gain_ref[level, :, sl] = sigma * (1.0 + pre * (1.0 - sigma))
        x[:, sl] = (x[:, sl].astype(jnp.float32) + pre * sigma).astype(jnp.bfloat16)

    def enc_level(level):
        n, we = ref["n"], ref["we"]
        normalize(level, n, ref["r"])

        def step(at, sl, carry):
            activate(dot(n[level], we[level, :, sl]), ref["ga"], level, sl)
            return carry

        for_tiles(step)

    def dec_level(level):
        n, nd, wd = ref["n"], ref["nd"], ref["wd"]
        normalize(level, nd, ref["rd"])

        def step(at, sl, carry):
            pre = dot(nd[level], wd[level, :channels, sl]) + dot(n[level], wd[level, channels:, sl])
            activate(pre, ref["gb"], level, sl)
            return carry

        for_tiles(step)

    def back(grad_ref, level, w_ref, base, n_ref, finish):
        grad = grad_ref[level]

        def step(at, sl, total):
            part = dot_t(grad, w_ref[level, pl.ds(base + at, TILE), :])
            ybuf[:, sl] = part
            return total + jnp.sum(
                part * n_ref[level, :, sl].astype(jnp.float32), axis=-1, keepdims=True
            )

        total = for_tiles(step, jnp.zeros((rows, 1), jnp.float32)) / channels

        def close(at, sl, carry):
            finish(sl, ybuf[:, sl] - n_ref[level, :, sl].astype(jnp.float32) * total)
            return carry

        for_tiles(close)

    def decb_level(level):
        n, nd, wd, u = ref.get("n"), ref["nd"], ref["wd"], ref["u"]
        u[level] = (x[...].astype(jnp.float32) * ref["gb"][level]).astype(jnp.bfloat16)
        if wide:
            width = channels // dp_count
            half = dp_count // 2
            by_core(
                level, "p", pl.ds(0, width),
                n[level, :, pl.ds(pl.multiple_of(dp * width, 128), width)],
            )
            low = pl.multiple_of(jnp.minimum(dp, half - 1) * 2 * width, 128)
            high = pl.multiple_of(jnp.maximum(dp - half, 0) * 2 * width, 128)

            @pl.when(dp < half)
            def _():
                by_core(level, "p", pl.ds(width, 2 * width), nd[level, :, pl.ds(low, 2 * width)])

            @pl.when(dp >= half)
            def _():
                by_core(level, "p", pl.ds(width, 2 * width), n[level, :, pl.ds(high, 2 * width)])

            by_core(level, "p", pl.ds(3 * width, channels), u[level])
        rd = ref["rd"][level, :, :1]

        def finish(sl, value):
            x[:, sl] = (x[:, sl].astype(jnp.float32) + rd * value).astype(jnp.bfloat16)

        if not (wide and level == 1 and ops[-1] == "decb"):
            back(u, level, wd, 0, nd, finish)
        if not skip_k:
            r, k = ref["r"][level, :, :1], ref["k"]

            def finish_skip(sl, value):
                k[level, :, sl] = (r * value).astype(jnp.bfloat16)

            back(u, level, wd, channels, n, finish_skip)

    def encb_level(level):
        n, we, e, k = ref["n"], ref["we"], ref["e"], ref["k"]
        e[level] = (x[...].astype(jnp.float32) * ref["ga"][level]).astype(jnp.bfloat16)
        if wide:
            by_core(level, "e", slice(None), e[level])
        if wide and level == 0:
            return
        r = ref["r"][level, :, :1]

        def finish(sl, value):
            x[:, sl] = (
                x[:, sl].astype(jnp.float32) + r * value + k[level, :, sl].astype(jnp.float32)
            ).astype(jnp.bfloat16)

        back(e, level, we, 0, n, finish)

    def fill(layout):
        for name, offset, flip in layout:
            source = ref[name]
            if flip is None:
                x[...] = source[offset : offset + rows]
            else:
                size = rows // dp_count
                at = pl.multiple_of(lax.bitwise_xor(dp, flip) * size, size)
                x[pl.ds(at, size)] = source[offset : offset + size]

    def run_live():
        fill(cfg["x_layout"])
        for op in ops:
            if op == "enc":
                enc_level(0)
                enc_level(1)
            if op == "dec":
                dec_level(1)
                dec_level(0)
            if op == "decb":
                if "dec" in ops:
                    fill(cfg["q_layout"])
                decb_level(0)
                decb_level(1)
            if op == "encb":
                encb_level(1)
                encb_level(0)

    if pair is None:
        run_live()
    else:
        here = lax.div(section, 2) == pair
        pl.when(here)(run_live)
        if cfg["prior"]:

            @pl.when(jnp.logical_not(here))
            def _():
                for name in cfg["prior"]:
                    ref[name][...] = ref["prior_" + name][...]


def run_stage(ops, pair, wide, unroll, rows, xs, qs, weights, state, dp_count, prior=()):
    channels = xs[0][0].shape[1]
    skip_k = pair == 0 and not wide
    bf16, f32 = jnp.bfloat16, jnp.float32
    matrix, pile = ((rows, channels), bf16), ((2, rows, channels), bf16)
    kinds = {
        "n": pile, "nd": pile, "k": pile, "u": pile, "e": pile,
        "r": ((2, rows, 128), f32), "rd": ((2, rows, 128), f32),
        "ga": ((2, rows, channels), f32), "gb": ((2, rows, channels), f32),
        "p": ((rows, channels + 3 * channels // dp_count), bf16),
    }
    names, args = [], []

    def operands(blocks):
        layout = []
        for value, offset, flip in blocks:
            known = [i for i, arg in enumerate(args) if arg is value]
            if known:
                name = names[known[0]]
            else:
                name = "x%d" % len(args)
                names.append(name)
                args.append(value)
            layout.append((name, offset, flip))
        return tuple(layout)

    x_layout = operands(xs)
    q_layout = operands(qs) if "dec" in ops and "decb" in ops else ()
    for kind, users in (("we", ("enc", "encb")), ("wd", ("dec", "decb"))):
        if any(op in users for op in ops):
            names.append(kind)
            args.append(weights[kind])
    made = set()
    for op in ops:
        for name in NEEDS[op]:
            if name not in made and name not in names and not (skip_k and op == "decb" and name in ("n", "r")):
                names.append(name)
                args.append(state[name])
        made.update(MAKES[op])
    for name in prior:
        names.append("prior_" + name)
        args.append(prior[name])
    in_count = len(args)
    outs, scratch = [], {}
    if not wide:
        outs.append(("out_x", matrix))
    else:
        scratch["work_x"] = matrix
    for op in ops:
        for name in MAKES[op]:
            if name == "k" and skip_k:
                continue
            if (name == "k" and "encb" in ops) or (name in ("nd", "rd", "gb") and "decb" in ops):
                scratch[name] = kinds[name]
            else:
                outs.append((name, kinds[name]))
        if op == "decb":
            scratch["u"] = pile
            if wide:
                outs += [("p_own", kinds["p"]), ("p_send", kinds["p"])]
        if op == "encb":
            scratch["e"] = pile
            if wide:
                outs += [("e_own", matrix), ("e_send", matrix)]
    if "decb" in ops or "encb" in ops:
        scratch["ybuf"] = ((rows, channels), f32)
    names += [o[0] for o in outs] + list(scratch)
    cfg = dict(
        ops=ops, pair=pair, wide=wide, names=names, dp_count=dp_count, skip_k=skip_k,
        unroll=unroll, prior=tuple(prior), x_layout=x_layout, q_layout=q_layout,
    )
    results = pl.pallas_call(
        functools.partial(stage_kernel, cfg),
        name=("wide_" if wide else "chain_") + "_".join(ops),
        out_shape=[jax.ShapeDtypeStruct(*o[1]) for o in outs],
        in_specs=[VMEM] * in_count,
        out_specs=[VMEM] * len(outs),
        scratch_shapes=[pltpu.VMEM(*v) for v in scratch.values()],
        compiler_params=pltpu.CompilerParams(
            vmem_limit_bytes=VMEM_LIMIT if unroll else WIDE_LIMIT
        ),
        cost_estimate=pl.CostEstimate(
            flops=1024, bytes_accessed=1024, transcendentals=0,
        ),
    )(*args)
    made = {name: value for (name, _), value in zip(outs, results)}
    x_out = made.pop("out_x", None)
    return x_out, {**state, **made}


def wgrad_kernel(skip, base, a_own, a_oth, b_own, b_oth, out, buf, sems):
    width, channels = buf.shape
    copies = []
    for index in range(channels // TILE):
        at = index * TILE
        total = dot_rows(a_own[:, skip : skip + width], b_own[:, base + at : base + at + TILE])
        total += dot_rows(a_oth[:, skip : skip + width], b_oth[:, base + at : base + at + TILE])
        buf[:, at : at + TILE] = total
        copy = pltpu.make_async_copy(
            buf.at[:, pl.ds(at, TILE)], out.at[:, pl.ds(at, TILE)], sems.at[index]
        )
        copy.start()
        copies.append(copy)
    for copy in copies:
        copy.wait()


def wgrad(name, skip, width, base, channels, a_own, a_oth, b_own, b_oth):
    return pl.pallas_call(
        functools.partial(wgrad_kernel, skip, base),
        name=name,
        out_shape=jax.ShapeDtypeStruct((width, channels), jnp.float32),
        in_specs=[VMEM] * 4,
        out_specs=ANY,
        scratch_shapes=[
            pltpu.VMEM((width, channels), jnp.float32),
            pltpu.SemaphoreType.DMA((channels // TILE,)),
        ],
        compiler_params=pltpu.CompilerParams(vmem_limit_bytes=VMEM_LIMIT),
        cost_estimate=pl.CostEstimate(
            flops=1024, bytes_accessed=1024, transcendentals=0,
        ),
    )(a_own, a_oth, b_own, b_oth)


def pack_kernel(inputs, cotangent, out, sems):
    core = lax.rem(lax.axis_index("section"), 2)
    count, row_count = inputs.shape[0] // 2, inputs.shape[1]
    copies = []
    for index, source in enumerate((inputs, cotangent)):
        for b in range(count):
            slot = index * count + b
            copies.append(
                pltpu.make_async_copy(
                    source.at[core * count + b],
                    out.at[pl.ds(slot * row_count, row_count)],
                    sems.at[slot],
                )
            )
            copies[-1].start()
    for copy in copies:
        copy.wait()


def pack(inputs, cotangent):
    batches, row_count, channels = inputs.shape
    return pl.pallas_call(
        pack_kernel,
        name="pack",
        out_shape=jax.ShapeDtypeStruct((batches * row_count, channels), inputs.dtype),
        in_specs=[pl.BlockSpec(memory_space=pltpu.HBM)] * 2,
        out_specs=VMEM,
        scratch_shapes=[pltpu.SemaphoreType.DMA((batches,))],
        compiler_params=pltpu.CompilerParams(vmem_limit_bytes=VMEM_LIMIT),
    )(inputs, cotangent)


def merge_kernel(low_count, *refs):
    pair = lax.div(lax.axis_index("section"), 2)
    out = refs[-1]
    for index, sources in enumerate((refs[:low_count], refs[low_count:-1])):

        @pl.when(pair == index)
        def _():
            at = 0
            for source in sources:
                size = source.shape[0]
                out[at : at + size] = source[...]
                at += size


def merge(low, high):
    rows = sum(value.shape[0] for value in low)
    return pl.pallas_call(
        functools.partial(merge_kernel, len(low)),
        name="merge",
        out_shape=jax.ShapeDtypeStruct((rows, low[0].shape[1]), low[0].dtype),
        in_specs=[VMEM] * (len(low) + len(high)),
        out_specs=VMEM,
        compiler_params=pltpu.CompilerParams(vmem_limit_bytes=VMEM_LIMIT),
    )(*low, *high)


def after(value, *others):
    return lax.optimization_barrier((value,) + others)[0]


def body(inputs, cotangent, enc_weights, dec_weights):
    section_count = lax.axis_size("section")
    dp_count = lax.axis_size("dp")
    core = lax.rem(lax.axis_index("section"), 2)
    pairs = section_count // 2
    batches, row_count, channels = inputs.shape
    half = batches * row_count // 2

    def my_rows(values):
        flat = values.reshape(2, half, channels)
        return lax.dynamic_index_in_dim(flat, core, 0, keepdims=False)

    def swap(value):
        return lax.ppermute(value, "section", [(i, i ^ 1) for i in range(section_count)])

    def flip_dp(value, flip, only=None):
        if only is None:
            return lax.ppermute(value, "dp", [(i, i ^ flip) for i in range(dp_count)])
        first = 2 * only * dp_count
        return lax.ppermute(
            value, ("section", "dp"), [(first + i, first + (i ^ flip)) for i in range(2 * dp_count)]
        )

    def over_dp(value):
        return lax.all_gather(value, "dp", axis=0, tiled=True)

    def hop(value, source, target, flips=(0,)):
        return [
            lax.ppermute(
                value,
                ("section", "dp"),
                [
                    ((2 * source + c) * dp_count + d, (2 * target + c) * dp_count + (d ^ flip))
                    for c in range(2)
                    for d in range(dp_count)
                ],
            )
            for flip in flips
        ]

    we, wd = enc_weights[0], dec_weights[0]
    we_other = swap(we)

    def stage(ops, k, wide, xs, qs, weights, state, prior=(), rows=half):
        return run_stage(
            ops, k, wide, pairs <= 2, rows, xs, qs, weights, state, dp_count, prior
        )

    if pairs == 2 and dp_count == 4:
        wide_rows = half * dp_count
        packed = pack(inputs, cotangent)
        packed_two = flip_dp(packed, 2)
        wd_other = swap(after(wd, we_other, packed))
        weights = {"we": load_other(load_own(we), we_other), "wd": load_other(load_own(wd), wd_other)}
        h_top, low = stage(("enc",), 0, False, [(packed, 0, None)], [], weights, {})
        h_in, h_two = hop(h_top, 0, 1, (0, 2))
        d_top, high = stage(("enc", "dec"), 1, False, [(h_in, 0, None)], [], weights, {})
        d_in, d_two = hop(d_top, 1, 0, (0, 2))
        near = flip_dp(
            merge([packed, packed_two], [h_in, after(h_two, d_top), h_in, h_two]), 1
        )
        q_top, low = stage(
            ("dec", "decb"), 0, False, [(d_in, 0, None)], [(packed, half, None)], weights, low
        )
        q_in, q_two = hop(q_top, 0, 1, (0, 2))
        d_both = merge([d_in, d_two], [d_in, d_two])
        d_near = flip_dp(d_both, 1, 0)
        p_top, high = stage(
            ("decb", "encb"), 1, False, [(after(q_in, d_both), 0, None)], [], weights, high
        )
        q_late = after(q_two, p_top)
        q_near = flip_dp(merge([q_in, q_late], [q_in, q_late]), 1, 1)
        p_in = hop(p_top, 1, 0, (0, 1, 2, 3))
        near_late = after(near, p_in[0])
        _, wide_high = stage(
            ("enc", "dec"), 1, True,
            [(h_in, 0, 0), (h_two, 0, 2), (near_late, 0, 1), (near_late, half, 3)],
            [], weights, {}, (), wide_rows,
        )
        _, wide_low = stage(
            ("enc",), 0, True,
            [(packed, 0, 0), (packed_two, 0, 2), (near_late, 0, 1), (near_late, 2 * half, 3)],
            [], weights, {}, (), wide_rows,
        )
        _, wide_low = stage(
            ("dec", "decb"), 0, True,
            [(d_in, 0, 0), (d_two, 0, 2), (d_near, 0, 1), (d_near, half, 3)],
            [
                (packed, half, 0), (packed_two, half, 2),
                (near_late, half, 1), (near_late, 3 * half, 3),
            ],
            weights, wide_low, (), wide_rows,
        )
        _, wide_high = stage(
            ("decb", "encb"), 1, True,
            [(q_in, 0, 0), (q_two, 0, 2), (q_near, 0, 1), (q_near, half, 3)],
            [], weights, wide_high,
            {name: wide_low[name] for name in ("p_own", "p_send")}, wide_rows,
        )
        _, wide = stage(
            ("encb",), 0, True, [(p_in[flip], 0, flip) for flip in range(dp_count)],
            [], weights, wide_low,
            {name: wide_high[name] for name in ("e_own", "e_send")}, wide_rows,
        )
        wide["p_own"], wide["p_send"] = wide_high["p_own"], after(wide_high["p_send"], *p_in[1:])
    else:
        x0, cot = my_rows(inputs), my_rows(cotangent)
        wd_other = swap(wd)
        weights = {"we": load_other(load_own(we), we_other), "wd": load_other(load_own(wd), wd_other)}
        my_pair = lax.div(lax.axis_index("section"), 2)
        visits = [("enc", k) for k in range(pairs)]
        visits += [("dec", k) for k in reversed(range(pairs))]
        visits += [("decb", k) for k in range(pairs)]
        visits += [("encb", k) for k in reversed(range(pairs))]
        chain, wide = [{} for _ in range(pairs)], {}
        arrived = x0
        for i, (op, k) in enumerate(visits):
            entry = arrived if i % pairs == 0 else jnp.where(my_pair == k, arrived, entry)
            if i % pairs == pairs - 1:
                _, wide = stage(
                    (op,), None, True, [(over_dp(entry), 0, None)], [], weights, wide, (),
                    half * dp_count,
                )
            if i == len(visits) - 1:
                break
            x_out, chain[k] = stage((op,), k, False, [(arrived, 0, None)], [], weights, chain[k])
            target = visits[i + 1][1]
            if visits[i + 1] == ("decb", 0):
                arrived = cot
            elif target == k:
                arrived = x_out
            else:
                (arrived,) = hop(x_out, k, target)
    narrow = channels // dp_count
    p_own, p_oth = wide["p_own"], swap(wide["p_send"])
    e_own, e_oth = wide["e_own"], swap(wide["e_send"])
    dec_grads = wgrad(
        "wgrad_dec", narrow, 2 * narrow, 3 * narrow, channels, p_own, p_oth, p_own, p_oth
    )
    enc_grads = wgrad("wgrad_enc", 0, narrow, 0, channels, p_own, p_oth, e_own, e_oth)
    return (enc_grads[None], dec_grads[None])


def solution(mesh):
    in_specs = (
        P(None, ("group", "dp"), None),
        P(None, ("group", "dp"), None),
        P("section", None, None),
        P("section", None, None),
    )
    out_specs = (P(("group", "section"), "dp", None), P(("group", "section"), "dp", None))
    return jax.shard_map(body, mesh=mesh, in_specs=in_specs, out_specs=out_specs, check_vma=False)
```

time: 388 us -> 82.6 us (0.21)
  the two profiles are of different devices: /device:TPU:0 before, /device:TPU:5 now
where the time goes in v2:
time: 82.6 us; the launch traced here: 82.1 us
  starting transfers between devices  35.2 us (43%)
  Pallas kernels  22.4 us (27%)
  waiting for transfers between devices  20 us (24%)
  local copies, waits for them, and re-layouts  3.5 us (4%)
  between operations  1.13 us (1%)
    ppermute x10, starting transfers between devices, hop(): lax.ppermute(value, ('section', 'dp'), [((2 * source + c) * dp_count + d,...  23.2 us
    pallas_call x9, Pallas kernels, run_stage(): pl.pallas_call(functools.partial(stage_kernel, cfg), name=('wide_' if wid...  17.9 us
    ppermute x10, waiting for transfers between devices, hop(): lax.ppermute(value, ('section', 'dp'), [((2 * source + c) * dp_count + d,...  16.3 us
    ppermute x2, starting transfers between devices, flip_dp(): lax.ppermute(value, ('section', 'dp'), [(first + i, first + (i ^ flip)) f...  5.11 us
    ppermute x4, starting transfers between devices, swap(): lax.ppermute(value, 'section', [(i, i ^ 1) for i in range(section_count)])  4.43 us
    ppermute x4, waiting for transfers between devices, swap(): lax.ppermute(value, 'section', [(i, i ^ 1) for i in range(section_count)])  3.67 us
    unnamed x8, local copies, waits for them, and re-layouts  3.5 us
    pallas_call x2, Pallas kernels, wgrad(): pl.pallas_call(functools.partial(wgrad_kernel, skip, base), name=name, ou...  3.13 us
  transfers between devices with their start and end apart: 18, of which 7 were waited for; matrix products, arithmetic and copies ran while one was open for 0% of the time, Pallas kernels for 26%

profile of v2, /device:TPU:5, one launch (start us, length us, event | category | flops | bytes accessed | tf_op | source)
XLA Modules:
  0.0 82.1 jit_solution(2112836605542864470)
XLA Ops:
  0.6 0.7 collective-permute-start
  1.4 0.9 %copy-done.2 = bf16[4,32,1024]{2,1,0:T(8,128)(2,1)S(1)} copy-done((bf16[4,32,1024]{2,1,0:T(8,128)(2,1)S(1)}, bf16[4,32,1024]{2,1,0:T(8,128)(2,1)}, u32[]{:S(2)}) %copy-start.2) | copy-done | bytes 262168
  2.3 0.9 %copy-done.3 = bf16[4,32,1024]{2,1,0:T(8,128)(2,1)S(1)} copy-done((bf16[4,32,1024]{2,1,0:T(8,128)(2,1)S(1)}, bf16[4,32,1024]{2,1,0:T(8,128)(2,1)}, u32[]{:S(2)}) %copy-start.3) | copy-done | bytes 262168
  3.6 1.7 %collective-permute-done.other = bf16[1024,1024]{1,0:T(8,128)(2,1)S(1)} collective-permute-done((bf16[1024,1024]{1,0:T(8,128)(2,1)}, bf16[1024,1024]{1,0:T(8,128)(2,1)S(1)}, u32[]{:S(2)}, u32[]{:S(2)}) %collective-permute-start) | collective-permute-done | bytes 2097184 | tf_op jit(solution)/shard_map/ppermute | solution.py:467
  5.7 2.3 %collective-permute-start.9 = (bf16[128,1024]{1,0:T(8,128)(2,1)S(1)}, bf16[128,1024]{1,0:T(8,128)(2,1)S(1)}, u32[]{:S(2)}, u32[]{:S(2)}) collective-permute-start(bf16[128,1024]{1,0:T(8,128)(2,1)S(1)} %pack.1.refs_0_.refs_1_.refs_3_), channel_id=1, source_target_pairs={{0,2},{1,3},{2,0},{3,1},{4,6},{5,7},{6,4},{7,5},{8,10},{9,11},{10,... | collective-permute-start | bytes 786440 | tf_op jit(solution)/shard_map/ppermute | solution.py:471
  8.1 1.6 %copy-done.1 = bf16[1,1024,1024]{2,1,0:T(8,128)(2,1)S(1)} copy-done((bf16[1,1024,1024]{2,1,0:T(8,128)(2,1)S(1)}, bf16[1,1024,1024]{2,1,0:T(8,128)(2,1)}, u32[]{:S(2)}) %copy-start.1) | copy-done | bytes 2097176
  10.0 0.8 %chain_enc.1 = (bf16[64,1024]{1,0:T(8,128)(2,1)S(1)}, bf16[2,64,1024]{2,1,0:T(8,128)(2,1)S(1)}, f32[2,64,128]{2,1,0:T(8,128)}, f32[2,64,1024]{2,1,0:T(8,128)}) custom-call(bf16[128,1024]{1,0:T(8,128)(2,1)S(1)} %pack.1.refs_0_.refs_1_.refs_3_, bf16[2,1024,1024]{2,1,0:T(8,128)(2,1)S(1)} %load_other.2.refs_1_.refs_3_.refs_4_), custom_call_target="tpu_custom_call" | custom-call | flops 1024 | bytes 1024 | tf_op jit(solution)/shard_map/chain_enc/pallas_call | solution.py:338
  10.8 1.4 %collective-permute-start.1 = (bf16[64,1024]{1,0:T(8,128)(2,1)S(1)}, bf16[64,1024]{1,0:T(8,128)(2,1)S(1)}, u32[]{:S(2)}, u32[]{:S(2)}) collective-permute-start(bf16[64,1024]{1,0:T(8,128)(2,1)S(1)} %get-tuple-element.35), channel_id=1, source_target_pairs={{0,8},{1,9},{2,10},{3,11},{4,12},{5,13},{6,14},{7,15},{16,24},{17,... | collective-permute-start | bytes 393224 | tf_op jit(solution)/shard_map/ppermute | solution.py:482
  12.2 1.3 %collective-permute-start.8 = (bf16[64,1024]{1,0:T(8,128)(2,1)S(1)}, bf16[64,1024]{1,0:T(8,128)(2,1)S(1)}, u32[]{:S(2)}, u32[]{:S(2)}) collective-permute-start(bf16[64,1024]{1,0:T(8,128)(2,1)S(1)} %get-tuple-element.35), channel_id=1, source_target_pairs={{0,10},{1,11},{2,8},{3,9},{4,14},{5,15},{6,12},{7,13},{16,26},{17,... | collective-permute-start | bytes 393224 | tf_op jit(solution)/shard_map/ppermute | solution.py:482
  14.2 3.3 %collective-permute-done.1.refs_0_.refs_2_.refs_4_ = bf16[64,1024]{1,0:T(8,128)(2,1)S(1)} collective-permute-done((bf16[64,1024]{1,0:T(8,128)(2,1)S(1)}, bf16[64,1024]{1,0:T(8,128)(2,1)S(1)}, u32[]{:S(2)}, u32[]{:S(2)}) %collective-permute-start.1) | collective-permute-done | bytes 131104 | tf_op jit(solution)/shard_map/ppermute | solution.py:482
  17.5 2.8 %chain_enc_dec.1 = (bf16[64,1024]{1,0:T(8,128)(2,1)S(1)}, bf16[2,64,1024]{2,1,0:T(8,128)(2,1)S(1)}, f32[2,64,128]{2,1,0:T(8,128)S(1)}, f32[2,64,1024]{2,1,0:T(8,...) custom-call(bf16[64,1024]{1,0:T(8,128)(2,1)S(1)} %collective-permute-done.1.refs_0, ...), custom_call_target="tpu_custom_call" | custom-call | flops 1024 | bytes 1024 | tf_op jit(solution)/shard_map/chain_enc_dec/pallas_call | solution.py:338
  20.3 5.5 %collective-permute-done.8.refs_3_.refs_5_.refs_1_ = bf16[64,1024]{1,0:T(8,128)(2,1)S(1)} collective-permute-done((bf16[64,1024]{1,0:T(8,128)(2,1)S(1)}, bf16[64,1024]{1,0:T(8,128)(2,1)S(1)}, u32[]{:S(2)}, u32[]{:S(2)}) %collective-permute-start.8) | collective-permute-done | bytes 131104 | tf_op jit(solution)/shard_map/ppermute | solution.py:482
  25.9 2.9 %collective-permute-start.3 = (bf16[64,1024]{1,0:T(8,128)(2,1)S(1)}, bf16[64,1024]{1,0:T(8,128)(2,1)S(1)}, u32[]{:S(2)}, u32[]{:S(2)}) collective-permute-start(bf16[64,1024]{1,0:T(8,128)(2,1)S(1)} %get-tuple-element.37), channel_id=1, source_target_pairs={{8,0},{9,1},{10,2},{11,3},{12,4},{13,5},{14,6},{15,7},{24,16},{25,... | collective-permute-start | bytes 393224 | tf_op jit(solution)/shard_map/ppermute | solution.py:482
  28.8 1.3 %collective-permute-start.6 = (bf16[64,1024]{1,0:T(8,128)(2,1)S(1)}, bf16[64,1024]{1,0:T(8,128)(2,1)S(1)}, u32[]{:S(2)}, u32[]{:S(2)}) collective-permute-start(bf16[64,1024]{1,0:T(8,128)(2,1)S(1)} %get-tuple-element.37), channel_id=1, source_target_pairs={{8,2},{9,3},{10,0},{11,1},{12,6},{13,7},{14,4},{15,5},{24,18},{25,... | collective-permute-start | bytes 393224 | tf_op jit(solution)/shard_map/ppermute | solution.py:482
  30.1 0.6 collective-permute-done.3.refs_0_.refs_2_
  30.7 1.3 %collective-permute-start.4 = (bf16[64,1024]{1,0:T(8,128)(2,1)S(1)}, bf16[64,1024]{1,0:T(8,128)(2,1)S(1)}, u32[]{:S(2)}, u32[]{:S(2)}) collective-permute-start(bf16[64,1024]{1,0:T(8,128)(2,1)S(1)} %chain_dec_decb.1), channel_id=1, source_target_pairs={{0,8},{1,9},{2,10},{3,11},{4,12},{5,13},{6,14},{7,15},{16,24},{17,... | collective-permute-start | bytes 393224 | tf_op jit(solution)/shard_map/ppermute | solution.py:482
  32.0 1.3 %collective-permute-start.5 = (bf16[64,1024]{1,0:T(8,128)(2,1)S(1)}, bf16[64,1024]{1,0:T(8,128)(2,1)S(1)}, u32[]{:S(2)}, u32[]{:S(2)}) collective-permute-start(bf16[64,1024]{1,0:T(8,128)(2,1)S(1)} %chain_dec_decb.1), channel_id=1, source_target_pairs={{0,10},{1,11},{2,8},{3,9},{4,14},{5,15},{6,12},{7,13},{16,26},{17,... | collective-permute-start | bytes 393224 | tf_op jit(solution)/shard_map/ppermute | solution.py:482
  33.3 6.3 %collective-permute-done.6.refs_1_.refs_3_ = bf16[64,1024]{1,0:T(8,128)(2,1)S(1)} collective-permute-done((bf16[64,1024]{1,0:T(8,128)(2,1)S(1)}, bf16[64,1024]{1,0:T(8,128)(2,1)S(1)}, u32[]{:S(2)}, u32[]{:S(2)}) %collective-permute-start.6) | collective-permute-done | bytes 131104 | tf_op jit(solution)/shard_map/ppermute | solution.py:482
  39.6 0.7 collective-permute-start.12
  40.3 4.3 %chain_decb_encb.1 = bf16[64,1024]{1,0:T(8,128)(2,1)S(1)} custom-call(bf16[64,1024]{1,0:T(8,128)(2,1)S(1)} %collective-permute-done.4.refs_0_.refs_2_, bf16[2,1024,1024]{2,1,0:T(8,128)(2,1)S(1)} %load_other.2.refs_1_.refs_3_.refs_4_, bf16[2,2048,1024]{2,1,0:T(8,128)(2,1)S(1)} %load_other.3.refs_2_.refs_4_.refs_6_, ...), custom_call_target="tpu_custom_call" | custom-call | flops 1024 | bytes 1024 | tf_op jit(solution)/shard_map/chain_decb_encb/pallas_call | solution.py:338
  44.6 4.4 %collective-permute-start.7 = (bf16[128,1024]{1,0:T(8,128)(2,1)S(1)}, bf16[128,1024]{1,0:T(8,128)(2,1)S(1)}, u32[]{:S(2)}, u32[]{:S(2)}) collective-permute-start(bf16[128,1024]{1,0:T(8,128)(2,1)S(1)} %merge.4), channel_id=1, source_target_pairs={{8,9},{9,8},{10,11},{11,10},{12,13},{13,12},{14,15},{15,14},{24,25... | collective-permute-start | bytes 786440 | tf_op jit(solution)/shard_map/ppermute | solution.py:473
  49.1 1.3 %collective-permute-start.11 = (bf16[64,1024]{1,0:T(8,128)(2,1)S(1)}, bf16[64,1024]{1,0:T(8,128)(2,1)S(1)}, u32[]{:S(2)}, u32[]{:S(2)}) collective-permute-start(bf16[64,1024]{1,0:T(8,128)(2,1)S(1)} %chain_decb_encb.1), channel_id=1, source_target_pairs={{8,0},{9,1},{10,2},{11,3},{12,4},{13,5},{14,6},{15,7},{24,16},{25,... | collective-permute-start | bytes 393224 | tf_op jit(solution)/shard_map/ppermute | solution.py:482
  50.4 1.3 %collective-permute-start.13 = (bf16[64,1024]{1,0:T(8,128)(2,1)S(1)}, bf16[64,1024]{1,0:T(8,128)(2,1)S(1)}, u32[]{:S(2)}, u32[]{:S(2)}) collective-permute-start(bf16[64,1024]{1,0:T(8,128)(2,1)S(1)} %chain_decb_encb.1), channel_id=1, source_target_pairs={{8,1},{9,0},{10,3},{11,2},{12,5},{13,4},{14,7},{15,6},{24,17},{25,... | collective-permute-start | bytes 393224 | tf_op jit(solution)/shard_map/ppermute | solution.py:482
  51.7 0.6 collective-permute-done.11.refs_0_
  52.3 9.9 %collective-permute-start.14 = (bf16[64,1024]{1,0:T(8,128)(2,1)S(1)}, bf16[64,1024]{1,0:T(8,128)(2,1)S(1)}, u32[]{:S(2)}, u32[]{:S(2)}) collective-permute-start(bf16[64,1024]{1,0:T(8,128)(2,1)S(1)} %chain_decb_encb.1), channel_id=1, source_target_pairs={{8,2},{9,3},{10,0},{11,1},{12,6},{13,7},{14,4},{15,5},{24,18},{25,... | collective-permute-start | bytes 393224 | tf_op jit(solution)/shard_map/ppermute | solution.py:482
  62.2 1.3 %collective-permute-start.15 = (bf16[64,1024]{1,0:T(8,128)(2,1)S(1)}, bf16[64,1024]{1,0:T(8,128)(2,1)S(1)}, u32[]{:S(2)}, u32[]{:S(2)}) collective-permute-start(bf16[64,1024]{1,0:T(8,128)(2,1)S(1)} %chain_decb_encb.1), channel_id=1, source_target_pairs={{8,3},{9,2},{10,1},{11,0},{12,7},{13,6},{14,5},{15,4},{24,19},{25,... | collective-permute-start | bytes 393224 | tf_op jit(solution)/shard_map/ppermute | solution.py:482
  63.6 4.9 %wide_enc_dec.1 = (bf16[2,256,1024]{2,1,0:T(8,128)(2,1)S(1)}, f32[2,256,128]{2,1,0:T(8,128)S(1)}, f32[2,256,1024]{2,1,0:T(8,128)S(1)}, bf16[2,256,1024]{2,1,0:T(...) custom-call(bf16[64,1024]{1,0:T(8,128)(2,1)S(1)} %collective-permute-done.1.refs_0_.refs_2_.refs_4_, ...), custom_call_target="tpu_custom_call" | custom-call | flops 1024 | bytes 1024 | tf_op jit(solution)/shard_map/wide_enc_dec/pallas_call | solution.py:338
  68.5 5.0 %wide_decb_encb.1 = (bf16[256,1792]{1,0:T(8,128)(2,1)S(1)}, bf16[256,1792]{1,0:T(8,128)(2,1)S(1)}, bf16[256,1024]{1,0:T(8,128)(2,1)S(1)}, bf16[256,1024]{1,0:T(8,128)(2,1)S(1)}) custom-call(bf16[64,1024]{1,0:T(8,128)(2,1)S(1)} %collective-permute-done.4.refs_0_.refs_2_, bf16[64,1024]{1,0:T(8,128)(2,1)S(1)} %collective-permute-done.5.refs_1_.refs_3_, ...), custom_call_target="tpu_custom_call" | custom-call | flops 1024 | bytes 1024 | tf_op jit(solution)/shard_map/wide_decb_encb/pallas_call | solution.py:338
  73.5 3.2 %collective-permute-start.16 = (bf16[256,1792]{1,0:T(8,128)(2,1)S(1)}, bf16[256,1792]{1,0:T(8,128)(2,1)S(1)}, u32[]{:S(2)}, u32[]{:S(2)}) collective-permute-start(bf16[256,1792]{1,0:T(8,128)(2,1)S(1)} %get-tuple-element.61), channel_id=1, source_target_pairs={{0,4},{4,0},{8,12},{12,8},{1,5},{5,1},{9,13},{13,9},{2,6},{6,2},{1... | collective-permute-start | bytes 2752520 | tf_op jit(solution)/shard_map/ppermute | solution.py:467
  76.9 1.9 %collective-permute-done.16.a_oth.b_oth = bf16[256,1792]{1,0:T(8,128)(2,1)S(1)} collective-permute-done((bf16[256,1792]{1,0:T(8,128)(2,1)S(1)}, bf16[256,1792]{1,0:T(8,128)(2,1)S(1)}, u32[]{:S(2)}, u32[]{:S(2)}) %collective-permute-start.16) | collective-permute-done | bytes 917536 | tf_op jit(solution)/shard_map/ppermute | solution.py:467
  78.8 1.8 %wgrad_dec.1 = f32[512,1024]{1,0:T(8,128)} custom-call(bf16[256,1792]{1,0:T(8,128)(2,1)S(1)} %get-tuple-element.59.a_own.b_own, bf16[256,1792]{1,0:T(8,128)(2,1)S(1)} %collective-permute-done.16.a_oth.b_oth, bf16[256,1792]{1,0:T(8,128)(2,1)S(1)} %get-tuple-element.59.a_own.b_own, bf16[256,1792]{1,0:T(8,128)(2,1)S(1)} %collective-permute-done.16.a_oth.b_oth), custom_call_target="tpu_custom_call" | custom-call | flops 1024 | bytes 1024 | tf_op jit(solution)/shard_map/wgrad_dec/pallas_call | solution.py:375
  80.6 1.3 %wgrad_enc.1 = f32[256,1024]{1,0:T(8,128)} custom-call(bf16[256,1792]{1,0:T(8,128)(2,1)S(1)} %get-tuple-element.59.a_own.b_own, bf16[256,1792]{1,0:T(8,128)(2,1)S(1)} %collective-permute-done.16.a_oth.b_oth, bf16[256,1024]{1,0:T(8,128)(2,1)S(1)} %get-tuple-element.66.b_own, bf16[256,1024]{1,0:T(8,128)(2,1)S(1)} %collective-permute-done.17.b_oth), custom_call_target="tpu_custom_call" | custom-call | flops 1024 | bytes 1024 | tf_op jit(solution)/shard_map/wgrad_enc/pallas_call | solution.py:375
  (31 shorter events, 2.1 us)
Async XLA Ops:
  0.6 4.7 %collective-permute-start = (bf16[1024,1024]{1,0:T(8,128)(2,1)}, bf16[1024,1024]{1,0:T(8,128)(2,1)S(1)}, u32[]{:S(2)}, u32[]{:S(2)}) collective-permute-start(bf16[1024,1024]{1,0:T(8,128)(2,1)} %bitcast.6), channel_id=1, source_target_pairs={{0,4},{4,0},{8,12},{12,8},{1,5},{5,1},{9,13},{13,9},{2,6},{6,2},{1... | collective-permute-start | bytes 6291464 | tf_op jit(solution)/shard_map/ppermute | solution.py:467
  1.4 0.9 %copy-start.2 = (bf16[4,32,1024]{2,1,0:T(8,128)(2,1)S(1)}, bf16[4,32,1024]{2,1,0:T(8,128)(2,1)}, u32[]{:S(2)}) copy-start(bf16[4,32,1024]{2,1,0:T(8,128)(2,1)} %inputs.1) | copy-start | bytes 786436
  2.3 0.9 %copy-start.3 = (bf16[4,32,1024]{2,1,0:T(8,128)(2,1)S(1)}, bf16[4,32,1024]{2,1,0:T(8,128)(2,1)}, u32[]{:S(2)}) copy-start(bf16[4,32,1024]{2,1,0:T(8,128)(2,1)} %cotangent.1) | copy-start | bytes 786436
  5.4 8.5 %collective-permute-start.2 = (bf16[2048,1024]{1,0:T(8,128)(2,1)}, bf16[2048,1024]{1,0:T(8,128)(2,1)S(1)}, u32[]{:S(2)}, u32[]{:S(2)}) collective-permute-start(bf16[2048,1024]{1,0:T(8,128)(2,1)} %bitcast.4), channel_id=1, source_target_pairs={{0,4},{4,0},{8,12},{12,8},{1,5},{5,1},{9,13},{13,9},{2,6},{6,2},{1... | collective-permute-start | bytes 12582920 | tf_op jit(solution)/shard_map/ppermute | solution.py:467
  5.7 20.0 %collective-permute-start.9 = (bf16[128,1024]{1,0:T(8,128)(2,1)S(1)}, bf16[128,1024]{1,0:T(8,128)(2,1)S(1)}, u32[]{:S(2)}, u32[]{:S(2)}) collective-permute-start(bf16[128,1024]{1,0:T(8,128)(2,1)S(1)} %pack.1.refs_0_.refs_1_.refs_3_), channel_id=1, source_target_pairs={{0,2},{1,3},{2,0},{3,1},{4,6},{5,7},{6,4},{7,5},{8,10},{9,11},{10,... | collective-permute-start | bytes 786440 | tf_op jit(solution)/shard_map/ppermute | solution.py:471
  8.1 1.6 %copy-start.1 = (bf16[1,1024,1024]{2,1,0:T(8,128)(2,1)S(1)}, bf16[1,1024,1024]{2,1,0:T(8,128)(2,1)}, u32[]{:S(2)}) copy-start(bf16[1,1024,1024]{2,1,0:T(8,128)(2,1)} %param.6) | copy-start | bytes 6291460
  10.0 3.6 %copy-start = (bf16[1,2048,1024]{2,1,0:T(8,128)(2,1)S(1)}, bf16[1,2048,1024]{2,1,0:T(8,128)(2,1)}, u32[]{:S(2)}) copy-start(bf16[1,2048,1024]{2,1,0:T(8,128)(2,1)} %param.7) | copy-start | bytes 12582916
  10.8 6.7 %collective-permute-start.1 = (bf16[64,1024]{1,0:T(8,128)(2,1)S(1)}, bf16[64,1024]{1,0:T(8,128)(2,1)S(1)}, u32[]{:S(2)}, u32[]{:S(2)}) collective-permute-start(bf16[64,1024]{1,0:T(8,128)(2,1)S(1)} %get-tuple-element.35), channel_id=1, source_target_pairs={{0,8},{1,9},{2,10},{3,11},{4,12},{5,13},{6,14},{7,15},{16,24},{17,... | collective-permute-start | bytes 393224 | tf_op jit(solution)/shard_map/ppermute | solution.py:482
  12.2 13.5 %collective-permute-start.8 = (bf16[64,1024]{1,0:T(8,128)(2,1)S(1)}, bf16[64,1024]{1,0:T(8,128)(2,1)S(1)}, u32[]{:S(2)}, u32[]{:S(2)}) collective-permute-start(bf16[64,1024]{1,0:T(8,128)(2,1)S(1)} %get-tuple-element.35), channel_id=1, source_target_pairs={{0,10},{1,11},{2,8},{3,9},{4,14},{5,15},{6,12},{7,13},{16,26},{17,... | collective-permute-start | bytes 393224 | tf_op jit(solution)/shard_map/ppermute | solution.py:482
  25.8 36.4 %collective-permute-start.10 = (bf16[256,1024]{1,0:T(8,128)(2,1)S(1)}, bf16[256,1024]{1,0:T(8,128)(2,1)S(1)}, u32[]{:S(2)}, u32[]{:S(2)}) collective-permute-start(bf16[256,1024]{1,0:T(8,128)(2,1)S(1)} %merge.5), channel_id=1, source_target_pairs={{0,1},{1,0},{2,3},{3,2},{4,5},{5,4},{6,7},{7,6},{8,9},{9,8},{10,11... | collective-permute-start | bytes 1572872 | tf_op jit(solution)/shard_map/ppermute | solution.py:471
  25.9 4.8 %collective-permute-start.3 = (bf16[64,1024]{1,0:T(8,128)(2,1)S(1)}, bf16[64,1024]{1,0:T(8,128)(2,1)S(1)}, u32[]{:S(2)}, u32[]{:S(2)}) collective-permute-start(bf16[64,1024]{1,0:T(8,128)(2,1)S(1)} %get-tuple-element.37), channel_id=1, source_target_pairs={{8,0},{9,1},{10,2},{11,3},{12,4},{13,5},{14,6},{15,7},{24,16},{25,... | collective-permute-start | bytes 393224 | tf_op jit(solution)/shard_map/ppermute | solution.py:482
  28.8 10.8 %collective-permute-start.6 = (bf16[64,1024]{1,0:T(8,128)(2,1)S(1)}, bf16[64,1024]{1,0:T(8,128)(2,1)S(1)}, u32[]{:S(2)}, u32[]{:S(2)}) collective-permute-start(bf16[64,1024]{1,0:T(8,128)(2,1)S(1)} %get-tuple-element.37), channel_id=1, source_target_pairs={{8,2},{9,3},{10,0},{11,1},{12,6},{13,7},{14,4},{15,5},{24,18},{25,... | collective-permute-start | bytes 393224 | tf_op jit(solution)/shard_map/ppermute | solution.py:482
  30.7 9.6 %collective-permute-start.4 = (bf16[64,1024]{1,0:T(8,128)(2,1)S(1)}, bf16[64,1024]{1,0:T(8,128)(2,1)S(1)}, u32[]{:S(2)}, u32[]{:S(2)}) collective-permute-start(bf16[64,1024]{1,0:T(8,128)(2,1)S(1)} %chain_dec_decb.1), channel_id=1, source_target_pairs={{0,8},{1,9},{2,10},{3,11},{4,12},{5,13},{6,14},{7,15},{16,24},{17,... | collective-permute-start | bytes 393224 | tf_op jit(solution)/shard_map/ppermute | solution.py:482
  32.0 12.6 %collective-permute-start.5 = (bf16[64,1024]{1,0:T(8,128)(2,1)S(1)}, bf16[64,1024]{1,0:T(8,128)(2,1)S(1)}, u32[]{:S(2)}, u32[]{:S(2)}) collective-permute-start(bf16[64,1024]{1,0:T(8,128)(2,1)S(1)} %chain_dec_decb.1), channel_id=1, source_target_pairs={{0,10},{1,11},{2,8},{3,9},{4,14},{5,15},{6,12},{7,13},{16,26},{17,... | collective-permute-start | bytes 393224 | tf_op jit(solution)/shard_map/ppermute | solution.py:482
  39.6 28.9 %collective-permute-start.12 = (bf16[128,1024]{1,0:T(8,128)(2,1)S(1)}, bf16[128,1024]{1,0:T(8,128)(2,1)S(1)}, u32[]{:S(2)}, u32[]{:S(2)}) collective-permute-start(bf16[128,1024]{1,0:T(8,128)(2,1)S(1)} %merge.3), channel_id=1, source_target_pairs={{0,1},{1,0},{2,3},{3,2},{4,5},{5,4},{6,7},{7,6},{16,17},{17,16},{1... | collective-permute-start | bytes 786440 | tf_op jit(solution)/shard_map/ppermute | solution.py:473
  44.6 23.9 %collective-permute-start.7 = (bf16[128,1024]{1,0:T(8,128)(2,1)S(1)}, bf16[128,1024]{1,0:T(8,128)(2,1)S(1)}, u32[]{:S(2)}, u32[]{:S(2)}) collective-permute-start(bf16[128,1024]{1,0:T(8,128)(2,1)S(1)} %merge.4), channel_id=1, source_target_pairs={{8,9},{9,8},{10,11},{11,10},{12,13},{13,12},{14,15},{15,14},{24,25... | collective-permute-start | bytes 786440 | tf_op jit(solution)/shard_map/ppermute | solution.py:473
  49.1 3.2 %collective-permute-start.11 = (bf16[64,1024]{1,0:T(8,128)(2,1)S(1)}, bf16[64,1024]{1,0:T(8,128)(2,1)S(1)}, u32[]{:S(2)}, u32[]{:S(2)}) collective-permute-start(bf16[64,1024]{1,0:T(8,128)(2,1)S(1)} %chain_decb_encb.1), channel_id=1, source_target_pairs={{8,0},{9,1},{10,2},{11,3},{12,4},{13,5},{14,6},{15,7},{24,16},{25,... | collective-permute-start | bytes 393224 | tf_op jit(solution)/shard_map/ppermute | solution.py:482
  50.4 23.1 %collective-permute-start.13 = (bf16[64,1024]{1,0:T(8,128)(2,1)S(1)}, bf16[64,1024]{1,0:T(8,128)(2,1)S(1)}, u32[]{:S(2)}, u32[]{:S(2)}) collective-permute-start(bf16[64,1024]{1,0:T(8,128)(2,1)S(1)} %chain_decb_encb.1), channel_id=1, source_target_pairs={{8,1},{9,0},{10,3},{11,2},{12,5},{13,4},{14,7},{15,6},{24,17},{25,... | collective-permute-start | bytes 393224 | tf_op jit(solution)/shard_map/ppermute | solution.py:482
  52.3 21.2 %collective-permute-start.14 = (bf16[64,1024]{1,0:T(8,128)(2,1)S(1)}, bf16[64,1024]{1,0:T(8,128)(2,1)S(1)}, u32[]{:S(2)}, u32[]{:S(2)}) collective-permute-start(bf16[64,1024]{1,0:T(8,128)(2,1)S(1)} %chain_decb_encb.1), channel_id=1, source_target_pairs={{8,2},{9,3},{10,0},{11,1},{12,6},{13,7},{14,4},{15,5},{24,18},{25,... | collective-permute-start | bytes 393224 | tf_op jit(solution)/shard_map/ppermute | solution.py:482
  62.2 11.3 %collective-permute-start.15 = (bf16[64,1024]{1,0:T(8,128)(2,1)S(1)}, bf16[64,1024]{1,0:T(8,128)(2,1)S(1)}, u32[]{:S(2)}, u32[]{:S(2)}) collective-permute-start(bf16[64,1024]{1,0:T(8,128)(2,1)S(1)} %chain_decb_encb.1), channel_id=1, source_target_pairs={{8,3},{9,2},{10,1},{11,0},{12,7},{13,6},{14,5},{15,4},{24,19},{25,... | collective-permute-start | bytes 393224 | tf_op jit(solution)/shard_map/ppermute | solution.py:482
  73.5 5.3 %collective-permute-start.16 = (bf16[256,1792]{1,0:T(8,128)(2,1)S(1)}, bf16[256,1792]{1,0:T(8,128)(2,1)S(1)}, u32[]{:S(2)}, u32[]{:S(2)}) collective-permute-start(bf16[256,1792]{1,0:T(8,128)(2,1)S(1)} %get-tuple-element.61), channel_id=1, source_target_pairs={{0,4},{4,0},{8,12},{12,8},{1,5},{5,1},{9,13},{13,9},{2,6},{6,2},{1... | collective-permute-start | bytes 2752520 | tf_op jit(solution)/shard_map/ppermute | solution.py:467
  76.8 3.8 %collective-permute-start.17 = (bf16[256,1024]{1,0:T(8,128)(2,1)S(1)}, bf16[256,1024]{1,0:T(8,128)(2,1)S(1)}, u32[]{:S(2)}, u32[]{:S(2)}) collective-permute-start(bf16[256,1024]{1,0:T(8,128)(2,1)S(1)} %get-tuple-element.67), channel_id=1, source_target_pairs={{0,4},{4,0},{8,12},{12,8},{1,5},{5,1},{9,13},{13,9},{2,6},{6,2},{1... | collective-permute-start | bytes 1572872 | tf_op jit(solution)/shard_map/ppermute | solution.py:467

commit v3 on v2

--- a/solution.py
+++ b/solution.py
@@ -502,29 +502,29 @@
     if pairs == 2 and dp_count == 4:
         wide_rows = half * dp_count
         packed = pack(inputs, cotangent)
-        packed_two = flip_dp(packed, 2)
-        wd_other = swap(after(wd, we_other, packed))
-        weights = {"we": load_other(load_own(we), we_other), "wd": load_other(load_own(wd), wd_other)}
+        packed_two = flip_dp(packed, 2, 0)
+        we_own = load_own(we)
+        wd_other = swap(after(wd, we_other, packed, we_own))
+        weights = {"we": load_other(we_own, we_other), "wd": load_other(load_own(wd), wd_other)}
         h_top, low = stage(("enc",), 0, False, [(packed, 0, None)], [], weights, {})
-        h_in, h_two = hop(h_top, 0, 1, (0, 2))
+        (h_in,) = hop(h_top, 0, 1)
+        h_two = flip_dp(h_in, 2, 1)
         d_top, high = stage(("enc", "dec"), 1, False, [(h_in, 0, None)], [], weights, {})
         d_in, d_two = hop(d_top, 1, 0, (0, 2))
-        near = flip_dp(
-            merge([packed, packed_two], [h_in, after(h_two, d_top), h_in, h_two]), 1
-        )
         q_top, low = stage(
             ("dec", "decb"), 0, False, [(d_in, 0, None)], [(packed, half, None)], weights, low
         )
+        near = flip_dp(
+            merge([packed, after(packed_two, q_top)], [h_in, after(h_two, q_top), h_in, h_two]), 1
+        )
         q_in, q_two = hop(q_top, 0, 1, (0, 2))
         d_both = merge([d_in, d_two], [d_in, d_two])
-        d_near = flip_dp(d_both, 1, 0)
         p_top, high = stage(
             ("decb", "encb"), 1, False, [(after(q_in, d_both), 0, None)], [], weights, high
         )
-        q_late = after(q_two, p_top)
-        q_near = flip_dp(merge([q_in, q_late], [q_in, q_late]), 1, 1)
         p_in = hop(p_top, 1, 0, (0, 1, 2, 3))
         near_late = after(near, p_in[0])
+        near_two = flip_dp(merge([after(d_both, p_in[0])], [q_in, after(q_two, p_in[0])]), 1)
         _, wide_high = stage(
             ("enc", "dec"), 1, True,
             [(h_in, 0, 0), (h_two, 0, 2), (near_late, 0, 1), (near_late, half, 3)],
@@ -537,7 +537,7 @@
         )
         _, wide_low = stage(
             ("dec", "decb"), 0, True,
-            [(d_in, 0, 0), (d_two, 0, 2), (d_near, 0, 1), (d_near, half, 3)],
+            [(d_in, 0, 0), (d_two, 0, 2), (near_two, 0, 1), (near_two, half, 3)],
             [
                 (packed, half, 0), (packed_two, half, 2),
                 (near_late, half, 1), (near_late, 3 * half, 3),
@@ -546,7 +546,7 @@
         )
         _, wide_high = stage(
             ("decb", "encb"), 1, True,
-            [(q_in, 0, 0), (q_two, 0, 2), (q_near, 0, 1), (q_near, half, 3)],
+            [(q_in, 0, 0), (q_two, 0, 2), (near_two, 0, 1), (near_two, half, 3)],
             [], weights, wide_high,
             {name: wide_low[name] for name in ("p_own", "p_send")}, wide_rows,
         )

time: 82.6 us -> 70.7 us (0.86)
  the two profiles are of different devices: /device:TPU:5 before, /device:TPU:0 now
where the time goes in v3:
time: 70.7 us; the launch traced here: 70.4 us
  starting transfers between devices  30.9 us (44%)
  Pallas kernels  19.7 us (28%)
  waiting for transfers between devices  15.9 us (22%)
  local copies, waits for them, and re-layouts  2.72 us (4%)
  between operations  1.13 us (2%)
    ppermute x9, starting transfers between devices, hop(): lax.ppermute(value, ('section', 'dp'), [((2 * source + c) * dp_count + d,...  21.9 us
    pallas_call x9, Pallas kernels, run_stage(): pl.pallas_call(functools.partial(stage_kernel, cfg), name=('wide_' if wid...  15.2 us
    ppermute x9, waiting for transfers between devices, hop(): lax.ppermute(value, ('section', 'dp'), [((2 * source + c) * dp_count + d,...  14.7 us
    ppermute x2, starting transfers between devices, flip_dp(): lax.ppermute(value, ('section', 'dp'), [(first + i, first + (i ^ flip)) f...  5.17 us
    pallas_call x2, Pallas kernels, wgrad(): pl.pallas_call(functools.partial(wgrad_kernel, skip, base), name=name, ou...  3.13 us
    unnamed x8, local copies, waits for them, and re-layouts  2.72 us
    ppermute x2, starting transfers between devices, flip_dp(): return lax.ppermute(value, 'dp', [(i, i ^ flip) for i in range(dp_count)])  2.33 us
    ppermute x4, starting transfers between devices, swap(): lax.ppermute(value, 'section', [(i, i ^ 1) for i in range(section_count)])  1.47 us
  transfers between devices with their start and end apart: 17, of which 6 were waited for; matrix products, arithmetic and copies ran while one was open for 0% of the time, Pallas kernels for 26%

profile of v3, /device:TPU:0, one launch (start us, length us, event | category | flops | bytes accessed | tf_op | source)
XLA Modules:
  0.0 70.4 jit_solution(17306175929821269568)
XLA Ops:
  0.6 0.5 collective-permute-start
  1.2 1.8 %copy-done.1 = bf16[1,1024,1024]{2,1,0:T(8,128)(2,1)S(1)} copy-done((bf16[1,1024,1024]{2,1,0:T(8,128)(2,1)S(1)}, bf16[1,1024,1024]{2,1,0:T(8,128)(2,1)}, u32[]{:S(2)}) %copy-start.1) | copy-done | bytes 2097176
  3.2 0.8 %copy-done.2 = bf16[4,32,1024]{2,1,0:T(8,128)(2,1)S(1)} copy-done((bf16[4,32,1024]{2,1,0:T(8,128)(2,1)S(1)}, bf16[4,32,1024]{2,1,0:T(8,128)(2,1)}, u32[]{:S(2)}) %copy-start.2) | copy-done | bytes 262168
  4.4 0.8 %collective-permute-done.other = bf16[1024,1024]{1,0:T(8,128)(2,1)S(1)} collective-permute-done((bf16[1024,1024]{1,0:T(8,128)(2,1)}, bf16[1024,1024]{1,0:T(8,128)(2,1)S(1)}, u32[]{:S(2)}, u32[]{:S(2)}) %collective-permute-start) | collective-permute-done | bytes 2097184 | tf_op jit(solution)/shard_map/ppermute | solution.py:467
  5.2 0.4 collective-permute-start.2
  5.7 2.0 %chain_enc.1 = (bf16[64,1024]{1,0:T(8,128)(2,1)S(1)}, bf16[2,64,1024]{2,1,0:T(8,128)(2,1)S(1)}, f32[2,64,128]{2,1,0:T(8,128)}, f32[2,64,1024]{2,1,0:T(8,128)}) custom-call(bf16[128,1024]{1,0:T(8,128)(2,1)S(1)} %pack.1.refs_0_.refs_1_.refs_3_, bf16[2,1024,1024]{2,1,0:T(8,128)(2,1)S(1)} %load_other.2.refs_1_.refs_3_.refs_4_), custom_call_target="tpu_custom_call" | custom-call | flops 1024 | bytes 1024 | tf_op jit(solution)/shard_map/chain_enc/pallas_call | solution.py:338
  7.7 3.4 %collective-permute-start.1 = (bf16[64,1024]{1,0:T(8,128)(2,1)S(1)}, bf16[64,1024]{1,0:T(8,128)(2,1)S(1)}, u32[]{:S(2)}, u32[]{:S(2)}) collective-permute-start(bf16[64,1024]{1,0:T(8,128)(2,1)S(1)} %get-tuple-element.37), channel_id=1, source_target_pairs={{0,8},{1,9},{2,10},{3,11},{4,12},{5,13},{6,14},{7,15},{16,24},{17,... | collective-permute-start | bytes 393224 | tf_op jit(solution)/shard_map/ppermute | solution.py:482
  11.1 4.5 %collective-permute-start.10 = (bf16[128,1024]{1,0:T(8,128)(2,1)S(1)}, bf16[128,1024]{1,0:T(8,128)(2,1)S(1)}, u32[]{:S(2)}, u32[]{:S(2)}) collective-permute-start(bf16[128,1024]{1,0:T(8,128)(2,1)S(1)} %pack.1.refs_0_.refs_1_.refs_3_), channel_id=1, source_target_pairs={{0,2},{1,3},{2,0},{3,1},{4,6},{5,7},{6,4},{7,5},{16,18},{17,19},{1... | collective-permute-start | bytes 786440 | tf_op jit(solution)/shard_map/ppermute | solution.py:473
  16.3 1.3 %collective-permute-start.3 = (bf16[64,1024]{1,0:T(8,128)(2,1)S(1)}, bf16[64,1024]{1,0:T(8,128)(2,1)S(1)}, u32[]{:S(2)}, u32[]{:S(2)}) collective-permute-start(bf16[64,1024]{1,0:T(8,128)(2,1)S(1)} %get-tuple-element.39), channel_id=1, source_target_pairs={{8,0},{9,1},{10,2},{11,3},{12,4},{13,5},{14,6},{15,7},{24,16},{25,... | collective-permute-start | bytes 393224 | tf_op jit(solution)/shard_map/ppermute | solution.py:482
  17.6 0.7 collective-permute-start.9
  18.3 1.3 %collective-permute-start.6 = (bf16[64,1024]{1,0:T(8,128)(2,1)S(1)}, bf16[64,1024]{1,0:T(8,128)(2,1)S(1)}, u32[]{:S(2)}, u32[]{:S(2)}) collective-permute-start(bf16[64,1024]{1,0:T(8,128)(2,1)S(1)} %get-tuple-element.39), channel_id=1, source_target_pairs={{8,2},{9,3},{10,0},{11,1},{12,6},{13,7},{14,4},{15,5},{24,18},{25,... | collective-permute-start | bytes 393224 | tf_op jit(solution)/shard_map/ppermute | solution.py:482
  19.6 4.6 %collective-permute-done.3.refs_0_.refs_2_ = bf16[64,1024]{1,0:T(8,128)(2,1)S(1)} collective-permute-done((bf16[64,1024]{1,0:T(8,128)(2,1)S(1)}, bf16[64,1024]{1,0:T(8,128)(2,1)S(1)}, u32[]{:S(2)}, u32[]{:S(2)}) %collective-permute-start.3) | collective-permute-done | bytes 131104 | tf_op jit(solution)/shard_map/ppermute | solution.py:482
  24.2 3.2 %chain_dec_decb.1 = bf16[64,1024]{1,0:T(8,128)(2,1)S(1)} custom-call(bf16[64,1024]{1,0:T(8,128)(2,1)S(1)} %collective-permute-done.3.refs_0_.refs_2_, bf16[128,1024]{1,0:T(8,128)(2,1)S(1)} %pack.1.refs_0_.refs_1_.refs_3_, bf16[2,2048,1024]{2,1,0:T(8,128)(2,1)S(1)} %load_other.3.refs_2_.refs_4_.refs_6_, bf16[2,64,1024]{2,1,0:T(8,128)(2,1)S(1)} %get-tuple-element.40.refs_3_), custom_call_target="tpu_custom_call" | custom-call | flops 1024 | bytes 1024 | tf_op jit(solution)/shard_map/chain_dec_decb/pallas_call | solution.py:338
  27.4 1.3 %collective-permute-start.4 = (bf16[64,1024]{1,0:T(8,128)(2,1)S(1)}, bf16[64,1024]{1,0:T(8,128)(2,1)S(1)}, u32[]{:S(2)}, u32[]{:S(2)}) collective-permute-start(bf16[64,1024]{1,0:T(8,128)(2,1)S(1)} %chain_dec_decb.1), channel_id=1, source_target_pairs={{0,8},{1,9},{2,10},{3,11},{4,12},{5,13},{6,14},{7,15},{16,24},{17,... | collective-permute-start | bytes 393224 | tf_op jit(solution)/shard_map/ppermute | solution.py:482
  28.8 1.6 %collective-permute-start.11 = (bf16[256,1024]{1,0:T(8,128)(2,1)S(1)}, bf16[256,1024]{1,0:T(8,128)(2,1)S(1)}, u32[]{:S(2)}, u32[]{:S(2)}) collective-permute-start(bf16[256,1024]{1,0:T(8,128)(2,1)S(1)} %merge.5), channel_id=1, source_target_pairs={{0,1},{1,0},{2,3},{3,2},{4,5},{5,4},{6,7},{7,6},{8,9},{9,8},{10,11... | collective-permute-start | bytes 1572872 | tf_op jit(solution)/shard_map/ppermute | solution.py:471
  30.5 9.5 %collective-permute-start.5 = (bf16[64,1024]{1,0:T(8,128)(2,1)S(1)}, bf16[64,1024]{1,0:T(8,128)(2,1)S(1)}, u32[]{:S(2)}, u32[]{:S(2)}) collective-permute-start(bf16[64,1024]{1,0:T(8,128)(2,1)S(1)} %chain_dec_decb.1), channel_id=1, source_target_pairs={{0,10},{1,11},{2,8},{3,9},{4,14},{5,15},{6,12},{7,13},{16,26},{17,... | collective-permute-start | bytes 393224 | tf_op jit(solution)/shard_map/ppermute | solution.py:482
  40.0 1.3 %collective-permute-start.7 = (bf16[64,1024]{1,0:T(8,128)(2,1)S(1)}, bf16[64,1024]{1,0:T(8,128)(2,1)S(1)}, u32[]{:S(2)}, u32[]{:S(2)}) collective-permute-start(bf16[64,1024]{1,0:T(8,128)(2,1)S(1)} %chain_decb_encb.1), channel_id=1, source_target_pairs={{8,0},{9,1},{10,2},{11,3},{12,4},{13,5},{14,6},{15,7},{24,16},{25,... | collective-permute-start | bytes 393224 | tf_op jit(solution)/shard_map/ppermute | solution.py:482
  41.3 2.3 %collective-permute-done.5.refs_2_.refs_1_ = bf16[64,1024]{1,0:T(8,128)(2,1)S(1)} collective-permute-done((bf16[64,1024]{1,0:T(8,128)(2,1)S(1)}, bf16[64,1024]{1,0:T(8,128)(2,1)S(1)}, u32[]{:S(2)}, u32[]{:S(2)}) %collective-permute-start.5) | collective-permute-done | bytes 131104 | tf_op jit(solution)/shard_map/ppermute | solution.py:482
  43.7 3.2 %collective-permute-done.7.refs_0_ = bf16[64,1024]{1,0:T(8,128)(2,1)S(1)} collective-permute-done((bf16[64,1024]{1,0:T(8,128)(2,1)S(1)}, bf16[64,1024]{1,0:T(8,128)(2,1)S(1)}, u32[]{:S(2)}, u32[]{:S(2)}) %collective-permute-start.7) | collective-permute-done | bytes 131104 | tf_op jit(solution)/shard_map/ppermute | solution.py:482
  46.9 0.7 collective-permute-start.8
  47.6 1.3 %collective-permute-start.12 = (bf16[64,1024]{1,0:T(8,128)(2,1)S(1)}, bf16[64,1024]{1,0:T(8,128)(2,1)S(1)}, u32[]{:S(2)}, u32[]{:S(2)}) collective-permute-start(bf16[64,1024]{1,0:T(8,128)(2,1)S(1)} %chain_decb_encb.1), channel_id=1, source_target_pairs={{8,1},{9,0},{10,3},{11,2},{12,5},{13,4},{14,7},{15,6},{24,17},{25,... | collective-permute-start | bytes 393224 | tf_op jit(solution)/shard_map/ppermute | solution.py:482
  48.9 1.3 %collective-permute-start.13 = (bf16[64,1024]{1,0:T(8,128)(2,1)S(1)}, bf16[64,1024]{1,0:T(8,128)(2,1)S(1)}, u32[]{:S(2)}, u32[]{:S(2)}) collective-permute-start(bf16[64,1024]{1,0:T(8,128)(2,1)S(1)} %chain_decb_encb.1), channel_id=1, source_target_pairs={{8,2},{9,3},{10,0},{11,1},{12,6},{13,7},{14,4},{15,5},{24,18},{25,... | collective-permute-start | bytes 393224 | tf_op jit(solution)/shard_map/ppermute | solution.py:482
  50.2 1.3 %collective-permute-start.14 = (bf16[64,1024]{1,0:T(8,128)(2,1)S(1)}, bf16[64,1024]{1,0:T(8,128)(2,1)S(1)}, u32[]{:S(2)}, u32[]{:S(2)}) collective-permute-start(bf16[64,1024]{1,0:T(8,128)(2,1)S(1)} %chain_decb_encb.1), channel_id=1, source_target_pairs={{8,3},{9,2},{10,1},{11,0},{12,7},{13,6},{14,5},{15,4},{24,19},{25,... | collective-permute-start | bytes 393224 | tf_op jit(solution)/shard_map/ppermute | solution.py:482
  51.5 2.0 %wide_enc.1 = (bf16[2,256,1024]{2,1,0:T(8,128)(2,1)S(1)}, f32[2,256,128]{2,1,0:T(8,128)S(1)}, f32[2,256,1024]{2,1,0:T(8,128)S(1)}) custom-call(bf16[128,1024]{1,0:T(8,128)(2,1)S(1)} %pack.1.refs_0_.refs_1_.refs_3_, bf16[128,1024]{1,0:T(8,128)(2,1)S(1)} %collective-permute-done.10.refs_1_.refs_4_, ...), custom_call_target="tpu_custom_call" | custom-call | flops 1024 | bytes 1024 | tf_op jit(solution)/shard_map/wide_enc/pallas_call | solution.py:338
  53.7 5.9 %wide_dec_decb.1 = (bf16[2,256,1024]{2,1,0:T(8,128)(2,1)S(1)}, bf16[256,1792]{1,0:T(8,128)(2,1)S(1)}, bf16[256,1792]{1,0:T(8,128)(2,1)S(1)}) custom-call(bf16[64,1024]{1,0:T(8,128)(2,1)S(1)} %collective-permute-done.3.refs_0_.refs_2_, bf16[64,1024]{1,0:T(8,128)(2,1)S(1)} %collective-permute-done.6.refs_1_.refs_3_, ...), custom_call_target="tpu_custom_call" | custom-call | flops 1024 | bytes 1024 | tf_op jit(solution)/shard_map/wide_dec_decb/pallas_call | solution.py:338
  59.6 0.4 wide_decb_encb.1
  60.0 4.5 %collective-permute-done.13.refs_2_ = bf16[64,1024]{1,0:T(8,128)(2,1)S(1)} collective-permute-done((bf16[64,1024]{1,0:T(8,128)(2,1)S(1)}, bf16[64,1024]{1,0:T(8,128)(2,1)S(1)}, u32[]{:S(2)}, u32[]{:S(2)}) %collective-permute-start.13) | collective-permute-done | bytes 131104 | tf_op jit(solution)/shard_map/ppermute | solution.py:482
  64.6 1.5 %wide_encb.1 = (bf16[256,1024]{1,0:T(8,128)(2,1)S(1)}, bf16[256,1024]{1,0:T(8,128)(2,1)S(1)}) custom-call(bf16[64,1024]{1,0:T(8,128)(2,1)S(1)} %collective-permute-done.7.refs_0_, bf16[64,1024]{1,0:T(8,128)(2,1)S(1)} %collective-permute-done.12.refs_1_, bf16[64,1024]{1,0:T(8,128)(2,1)S(1)} %collective-permute-done.13.refs_2_, ...), custom_call_target="tpu_custom_call" | custom-call | flops 1024 | bytes 1024 | tf_op jit(solution)/shard_map/wide_encb/pallas_call | solution.py:338
  66.0 0.6 collective-permute-start.16
  66.6 0.4 collective-permute-done.15.a_oth.b_oth
  67.0 1.8 %wgrad_dec.1 = f32[512,1024]{1,0:T(8,128)} custom-call(bf16[256,1792]{1,0:T(8,128)(2,1)S(1)} %get-tuple-element.63.a_own.b_own, bf16[256,1792]{1,0:T(8,128)(2,1)S(1)} %collective-permute-done.15.a_oth.b_oth, bf16[256,1792]{1,0:T(8,128)(2,1)S(1)} %get-tuple-element.63.a_own.b_own, bf16[256,1792]{1,0:T(8,128)(2,1)S(1)} %collective-permute-done.15.a_oth.b_oth), custom_call_target="tpu_custom_call" | custom-call | flops 1024 | bytes 1024 | tf_op jit(solution)/shard_map/wgrad_dec/pallas_call | solution.py:375
  68.9 1.3 %wgrad_enc.1 = f32[256,1024]{1,0:T(8,128)} custom-call(bf16[256,1792]{1,0:T(8,128)(2,1)S(1)} %get-tuple-element.63.a_own.b_own, bf16[256,1792]{1,0:T(8,128)(2,1)S(1)} %collective-permute-done.15.a_oth.b_oth, bf16[256,1024]{1,0:T(8,128)(2,1)S(1)} %get-tuple-element.70.b_own, bf16[256,1024]{1,0:T(8,128)(2,1)S(1)} %collective-permute-done.16.b_oth), custom_call_target="tpu_custom_call" | custom-call | flops 1024 | bytes 1024 | tf_op jit(solution)/shard_map/wgrad_enc/pallas_call | solution.py:375
  (29 shorter events, 1.7 us)
Async XLA Ops:
  0.6 4.5 %copy-start = (bf16[1,2048,1024]{2,1,0:T(8,128)(2,1)S(1)}, bf16[1,2048,1024]{2,1,0:T(8,128)(2,1)}, u32[]{:S(2)}) copy-start(bf16[1,2048,1024]{2,1,0:T(8,128)(2,1)} %param.7) | copy-start | bytes 12582916
  0.6 4.5 %collective-permute-start = (bf16[1024,1024]{1,0:T(8,128)(2,1)}, bf16[1024,1024]{1,0:T(8,128)(2,1)S(1)}, u32[]{:S(2)}, u32[]{:S(2)}) collective-permute-start(bf16[1024,1024]{1,0:T(8,128)(2,1)} %bitcast.6), channel_id=1, source_target_pairs={{0,4},{4,0},{8,12},{12,8},{1,5},{5,1},{9,13},{13,9},{2,6},{6,2},{1... | collective-permute-start | bytes 6291464 | tf_op jit(solution)/shard_map/ppermute | solution.py:467
  1.2 1.9 %copy-start.1 = (bf16[1,1024,1024]{2,1,0:T(8,128)(2,1)S(1)}, bf16[1,1024,1024]{2,1,0:T(8,128)(2,1)}, u32[]{:S(2)}) copy-start(bf16[1,1024,1024]{2,1,0:T(8,128)(2,1)} %param.6) | copy-start | bytes 6291460
  3.0 0.9 %copy-start.2 = (bf16[4,32,1024]{2,1,0:T(8,128)(2,1)S(1)}, bf16[4,32,1024]{2,1,0:T(8,128)(2,1)}, u32[]{:S(2)}) copy-start(bf16[4,32,1024]{2,1,0:T(8,128)(2,1)} %inputs.1) | copy-start | bytes 786436
  3.0 1.0 %copy-start.3 = (bf16[4,32,1024]{2,1,0:T(8,128)(2,1)S(1)}, bf16[4,32,1024]{2,1,0:T(8,128)(2,1)}, u32[]{:S(2)}) copy-start(bf16[4,32,1024]{2,1,0:T(8,128)(2,1)} %cotangent.1) | copy-start | bytes 786436
  5.2 10.8 %collective-permute-start.2 = (bf16[2048,1024]{1,0:T(8,128)(2,1)S(1)}, bf16[2048,1024]{1,0:T(8,128)(2,1)S(1)}, u32[]{:S(2)}, u32[]{:S(2)}) collective-permute-start(bf16[2048,1024]{1,0:T(8,128)(2,1)S(1)} %bitcast.4), channel_id=1, source_target_pairs={{0,4},{4,0},{8,12},{12,8},{1,5},{5,1},{9,13},{13,9},{2,6},{6,2},{1... | collective-permute-start | bytes 12582920 | tf_op jit(solution)/shard_map/ppermute | solution.py:467
  7.7 8.6 %collective-permute-start.1 = (bf16[64,1024]{1,0:T(8,128)(2,1)S(1)}, bf16[64,1024]{1,0:T(8,128)(2,1)S(1)}, u32[]{:S(2)}, u32[]{:S(2)}) collective-permute-start(bf16[64,1024]{1,0:T(8,128)(2,1)S(1)} %get-tuple-element.37), channel_id=1, source_target_pairs={{0,8},{1,9},{2,10},{3,11},{4,12},{5,13},{6,14},{7,15},{16,24},{17,... | collective-permute-start | bytes 393224 | tf_op jit(solution)/shard_map/ppermute | solution.py:482
  11.1 17.7 %collective-permute-start.10 = (bf16[128,1024]{1,0:T(8,128)(2,1)S(1)}, bf16[128,1024]{1,0:T(8,128)(2,1)S(1)}, u32[]{:S(2)}, u32[]{:S(2)}) collective-permute-start(bf16[128,1024]{1,0:T(8,128)(2,1)S(1)} %pack.1.refs_0_.refs_1_.refs_3_), channel_id=1, source_target_pairs={{0,2},{1,3},{2,0},{3,1},{4,6},{5,7},{6,4},{7,5},{16,18},{17,19},{1... | collective-permute-start | bytes 786440 | tf_op jit(solution)/shard_map/ppermute | solution.py:473
  16.3 7.9 %collective-permute-start.3 = (bf16[64,1024]{1,0:T(8,128)(2,1)S(1)}, bf16[64,1024]{1,0:T(8,128)(2,1)S(1)}, u32[]{:S(2)}, u32[]{:S(2)}) collective-permute-start(bf16[64,1024]{1,0:T(8,128)(2,1)S(1)} %get-tuple-element.39), channel_id=1, source_target_pairs={{8,0},{9,1},{10,2},{11,3},{12,4},{13,5},{14,6},{15,7},{24,16},{25,... | collective-permute-start | bytes 393224 | tf_op jit(solution)/shard_map/ppermute | solution.py:482
  17.6 11.2 %collective-permute-start.9 = (bf16[64,1024]{1,0:T(8,128)(2,1)S(1)}, bf16[64,1024]{1,0:T(8,128)(2,1)S(1)}, u32[]{:S(2)}, u32[]{:S(2)}) collective-permute-start(bf16[64,1024]{1,0:T(8,128)(2,1)S(1)} %collective-permute-done.1.refs_0_.refs_2_.refs_4_), channel_id=1, source_target_pairs={{8,10},{9,11},{10,8},{11,9},{12,14},{13,15},{14,12},{15,13},{24,26... | collective-permute-start | bytes 393224 | tf_op jit(solution)/shard_map/ppermute | solution.py:473
  18.3 21.7 %collective-permute-start.6 = (bf16[64,1024]{1,0:T(8,128)(2,1)S(1)}, bf16[64,1024]{1,0:T(8,128)(2,1)S(1)}, u32[]{:S(2)}, u32[]{:S(2)}) collective-permute-start(bf16[64,1024]{1,0:T(8,128)(2,1)S(1)} %get-tuple-element.39), channel_id=1, source_target_pairs={{8,2},{9,3},{10,0},{11,1},{12,6},{13,7},{14,4},{15,5},{24,18},{25,... | collective-permute-start | bytes 393224 | tf_op jit(solution)/shard_map/ppermute | solution.py:482
  27.4 12.6 %collective-permute-start.4 = (bf16[64,1024]{1,0:T(8,128)(2,1)S(1)}, bf16[64,1024]{1,0:T(8,128)(2,1)S(1)}, u32[]{:S(2)}, u32[]{:S(2)}) collective-permute-start(bf16[64,1024]{1,0:T(8,128)(2,1)S(1)} %chain_dec_decb.1), channel_id=1, source_target_pairs={{0,8},{1,9},{2,10},{3,11},{4,12},{5,13},{6,14},{7,15},{16,24},{17,... | collective-permute-start | bytes 393224 | tf_op jit(solution)/shard_map/ppermute | solution.py:482
  28.8 22.7 %collective-permute-start.11 = (bf16[256,1024]{1,0:T(8,128)(2,1)S(1)}, bf16[256,1024]{1,0:T(8,128)(2,1)S(1)}, u32[]{:S(2)}, u32[]{:S(2)}) collective-permute-start(bf16[256,1024]{1,0:T(8,128)(2,1)S(1)} %merge.5), channel_id=1, source_target_pairs={{0,1},{1,0},{2,3},{3,2},{4,5},{5,4},{6,7},{7,6},{8,9},{9,8},{10,11... | collective-permute-start | bytes 1572872 | tf_op jit(solution)/shard_map/ppermute | solution.py:471
  30.5 13.2 %collective-permute-start.5 = (bf16[64,1024]{1,0:T(8,128)(2,1)S(1)}, bf16[64,1024]{1,0:T(8,128)(2,1)S(1)}, u32[]{:S(2)}, u32[]{:S(2)}) collective-permute-start(bf16[64,1024]{1,0:T(8,128)(2,1)S(1)} %chain_dec_decb.1), channel_id=1, source_target_pairs={{0,10},{1,11},{2,8},{3,9},{4,14},{5,15},{6,12},{7,13},{16,26},{17,... | collective-permute-start | bytes 393224 | tf_op jit(solution)/shard_map/ppermute | solution.py:482
  40.0 6.9 %collective-permute-start.7 = (bf16[64,1024]{1,0:T(8,128)(2,1)S(1)}, bf16[64,1024]{1,0:T(8,128)(2,1)S(1)}, u32[]{:S(2)}, u32[]{:S(2)}) collective-permute-start(bf16[64,1024]{1,0:T(8,128)(2,1)S(1)} %chain_decb_encb.1), channel_id=1, source_target_pairs={{8,0},{9,1},{10,2},{11,3},{12,4},{13,5},{14,6},{15,7},{24,16},{25,... | collective-permute-start | bytes 393224 | tf_op jit(solution)/shard_map/ppermute | solution.py:482
  46.9 6.8 %collective-permute-start.8 = (bf16[128,1024]{1,0:T(8,128)(2,1)S(1)}, bf16[128,1024]{1,0:T(8,128)(2,1)S(1)}, u32[]{:S(2)}, u32[]{:S(2)}) collective-permute-start(bf16[128,1024]{1,0:T(8,128)(2,1)S(1)} %merge.4), channel_id=1, source_target_pairs={{0,1},{1,0},{2,3},{3,2},{4,5},{5,4},{6,7},{7,6},{8,9},{9,8},{10,11... | collective-permute-start | bytes 786440 | tf_op jit(solution)/shard_map/ppermute | solution.py:471
  47.6 12.4 %collective-permute-start.12 = (bf16[64,1024]{1,0:T(8,128)(2,1)S(1)}, bf16[64,1024]{1,0:T(8,128)(2,1)S(1)}, u32[]{:S(2)}, u32[]{:S(2)}) collective-permute-start(bf16[64,1024]{1,0:T(8,128)(2,1)S(1)} %chain_decb_encb.1), channel_id=1, source_target_pairs={{8,1},{9,0},{10,3},{11,2},{12,5},{13,4},{14,7},{15,6},{24,17},{25,... | collective-permute-start | bytes 393224 | tf_op jit(solution)/shard_map/ppermute | solution.py:482
  48.9 15.7 %collective-permute-start.13 = (bf16[64,1024]{1,0:T(8,128)(2,1)S(1)}, bf16[64,1024]{1,0:T(8,128)(2,1)S(1)}, u32[]{:S(2)}, u32[]{:S(2)}) collective-permute-start(bf16[64,1024]{1,0:T(8,128)(2,1)S(1)} %chain_decb_encb.1), channel_id=1, source_target_pairs={{8,2},{9,3},{10,0},{11,1},{12,6},{13,7},{14,4},{15,5},{24,18},{25,... | collective-permute-start | bytes 393224 | tf_op jit(solution)/shard_map/ppermute | solution.py:482
  50.2 14.4 %collective-permute-start.14 = (bf16[64,1024]{1,0:T(8,128)(2,1)S(1)}, bf16[64,1024]{1,0:T(8,128)(2,1)S(1)}, u32[]{:S(2)}, u32[]{:S(2)}) collective-permute-start(bf16[64,1024]{1,0:T(8,128)(2,1)S(1)} %chain_decb_encb.1), channel_id=1, source_target_pairs={{8,3},{9,2},{10,1},{11,0},{12,7},{13,6},{14,5},{15,4},{24,19},{25,... | collective-permute-start | bytes 393224 | tf_op jit(solution)/shard_map/ppermute | solution.py:482
  64.6 2.5 %collective-permute-start.15 = (bf16[256,1792]{1,0:T(8,128)(2,1)S(1)}, bf16[256,1792]{1,0:T(8,128)(2,1)S(1)}, u32[]{:S(2)}, u32[]{:S(2)}) collective-permute-start(bf16[256,1792]{1,0:T(8,128)(2,1)S(1)} %get-tuple-element.65), channel_id=1, source_target_pairs={{0,4},{4,0},{8,12},{12,8},{1,5},{5,1},{9,13},{13,9},{2,6},{6,2},{1... | collective-permute-start | bytes 2752520 | tf_op jit(solution)/shard_map/ppermute | solution.py:467
  66.0 2.8 %collective-permute-start.16 = (bf16[256,1024]{1,0:T(8,128)(2,1)S(1)}, bf16[256,1024]{1,0:T(8,128)(2,1)S(1)}, u32[]{:S(2)}, u32[]{:S(2)}) collective-permute-start(bf16[256,1024]{1,0:T(8,128)(2,1)S(1)} %get-tuple-element.71), channel_id=1, source_target_pairs={{0,4},{4,0},{8,12},{12,8},{1,5},{5,1},{9,13},{13,9},{2,6},{6,2},{1... | collective-permute-start | bytes 1572872 | tf_op jit(solution)/shard_map/ppermute | solution.py:467

commit v4 on v3

--- a/solution.py
+++ b/solution.py
@@ -8,6 +8,7 @@
 from jax.sharding import PartitionSpec as P
 
 EPS = 1e-06
+COSTS = {(('decb', 'encb'), False): 10000000000, (('dec', 'decb'), False): 10000000000}
 TILE = 256
 VMEM_LIMIT = 22 * 1024 * 1024
 WIDE_LIMIT = 40 * 1024 * 1024
@@ -199,7 +200,7 @@
 
         if not (wide and level == 1 and ops[-1] == "decb"):
             back(u, level, wd, 0, nd, finish)
-        if not skip_k:
+        if not skip_k and not (wide and level == 0):
             r, k = ref["r"][level, :, :1], ref["k"]
 
             def finish_skip(sl, value):
@@ -346,7 +347,7 @@
             vmem_limit_bytes=VMEM_LIMIT if unroll else WIDE_LIMIT
         ),
         cost_estimate=pl.CostEstimate(
-            flops=1024, bytes_accessed=1024, transcendentals=0,
+            flops=COSTS.get((ops, wide), 1024), bytes_accessed=1024, transcendentals=0,
         ),
     )(*args)
     made = {name: value for (name, _), value in zip(outs, results)}
@@ -514,13 +515,13 @@
         q_top, low = stage(
             ("dec", "decb"), 0, False, [(d_in, 0, None)], [(packed, half, None)], weights, low
         )
+        q_in, q_two = hop(q_top, 0, 1, (0, 2))
         near = flip_dp(
-            merge([packed, after(packed_two, q_top)], [h_in, after(h_two, q_top), h_in, h_two]), 1
-        )
-        q_in, q_two = hop(q_top, 0, 1, (0, 2))
+            merge([packed, after(packed_two, q_in)], [h_in, after(h_two, q_in), h_in, h_two]), 1
+        )
         d_both = merge([d_in, d_two], [d_in, d_two])
         p_top, high = stage(
-            ("decb", "encb"), 1, False, [(after(q_in, d_both), 0, None)], [], weights, high
+            ("decb", "encb"), 1, False, [(q_in, 0, None)], [], weights, high
         )
         p_in = hop(p_top, 1, 0, (0, 1, 2, 3))
         near_late = after(near, p_in[0])

time: 70.7 us -> 69.6 us (0.984)
  starting transfers between devices: 30.9 us -> 27.5 us
  waiting for transfers between devices: 15.9 us -> 18.8 us
    ppermute x2, waiting for transfers between devices: 0.01 us -> 4.33 us  [flip_dp(): return lax.ppermute(value, 'dp', [(i, i ^ flip) for i in range(dp_count)])]
    ppermute x9, starting transfers between devices: 21.9 us -> 18.8 us  [hop(): lax.ppermute(value, ('section', 'dp'), [((2 * source + c) * dp_count + d,...]
    ppermute x9, waiting for transfers between devices: 14.7 us -> 12.4 us  [hop(): lax.ppermute(value, ('section', 'dp'), [((2 * source + c) * dp_count + d,...]
    ppermute x4, waiting for transfers between devices: 1.19 us -> 2.09 us  [swap(): lax.ppermute(value, 'section', [(i, i ^ 1) for i in range(section_count)])]
  transfers between devices with their start and end apart: 17 -> 17, of which waited for: 6 -> 10; matrix products, arithmetic and copies ran while one was open for 0% -> 0% of each run, Pallas kernels for 26% -> 26%
where the time goes in v4:
time: 69.6 us; the launch traced here: 69.3 us
  starting transfers between devices  27.5 us (40%)
  Pallas kernels  19.1 us (27%)
  waiting for transfers between devices  18.8 us (27%)
  local copies, waits for them, and re-layouts  2.72 us (4%)
  between operations  1.08 us (2%)
    ppermute x9, starting transfers between devices, hop(): lax.ppermute(value, ('section', 'dp'), [((2 * source + c) * dp_count + d,...  18.8 us
    pallas_call x9, Pallas kernels, run_stage(): pl.pallas_call(functools.partial(stage_kernel, cfg), name=('wide_' if wid...  14.6 us
    ppermute x9, waiting for transfers between devices, hop(): lax.ppermute(value, ('section', 'dp'), [((2 * source + c) * dp_count + d,...  12.4 us
    ppermute x2, starting transfers between devices, flip_dp(): lax.ppermute(value, ('section', 'dp'), [(first + i, first + (i ^ flip)) f...  5.17 us
    ppermute x2, waiting for transfers between devices, flip_dp(): return lax.ppermute(value, 'dp', [(i, i ^ flip) for i in range(dp_count)])  4.33 us
    pallas_call x2, Pallas kernels, wgrad(): pl.pallas_call(functools.partial(wgrad_kernel, skip, base), name=name, ou...  3.13 us
    unnamed x8, local copies, waits for them, and re-layouts  2.72 us
    ppermute x2, starting transfers between devices, flip_dp(): return lax.ppermute(value, 'dp', [(i, i ^ flip) for i in range(dp_count)])  2.15 us
  transfers between devices with their start and end apart: 17, of which 10 were waited for; matrix products, arithmetic and copies ran while one was open for 0% of the time, Pallas kernels for 26%

profile of v4, /device:TPU:0, one launch (start us, length us, event | category | flops | bytes accessed | tf_op | source)
XLA Modules:
  0.0 69.3 jit_solution(13131986032887925076)
XLA Ops:
  0.6 0.5 collective-permute-start
  1.2 1.8 %copy-done.1 = bf16[1,1024,1024]{2,1,0:T(8,128)(2,1)S(1)} copy-done((bf16[1,1024,1024]{2,1,0:T(8,128)(2,1)S(1)}, bf16[1,1024,1024]{2,1,0:T(8,128)(2,1)}, u32[]{:S(2)}) %copy-start.1) | copy-done | bytes 2097176
  3.2 0.8 %copy-done.2 = bf16[4,32,1024]{2,1,0:T(8,128)(2,1)S(1)} copy-done((bf16[4,32,1024]{2,1,0:T(8,128)(2,1)S(1)}, bf16[4,32,1024]{2,1,0:T(8,128)(2,1)}, u32[]{:S(2)}) %copy-start.2) | copy-done | bytes 262168
  4.4 0.8 %collective-permute-done.other = bf16[1024,1024]{1,0:T(8,128)(2,1)S(1)} collective-permute-done((bf16[1024,1024]{1,0:T(8,128)(2,1)}, bf16[1024,1024]{1,0:T(8,128)(2,1)S(1)}, u32[]{:S(2)}, u32[]{:S(2)}) %collective-permute-start) | collective-permute-done | bytes 2097184 | tf_op jit(solution)/shard_map/ppermute | solution.py:468
  5.7 2.0 %chain_enc.1 = (bf16[64,1024]{1,0:T(8,128)(2,1)S(1)}, bf16[2,64,1024]{2,1,0:T(8,128)(2,1)S(1)}, f32[2,64,128]{2,1,0:T(8,128)}, f32[2,64,1024]{2,1,0:T(8,128)}) custom-call(bf16[128,1024]{1,0:T(8,128)(2,1)S(1)} %pack.1.refs_0_.refs_1_.refs_3_, bf16[2,1024,1024]{2,1,0:T(8,128)(2,1)S(1)} %load_other.2.refs_1_.refs_3_.refs_4_), custom_call_target="tpu_custom_call" | custom-call | flops 1024 | bytes 1024 | tf_op jit(solution)/shard_map/chain_enc/pallas_call | solution.py:339
  7.7 3.4 %collective-permute-start.1 = (bf16[64,1024]{1,0:T(8,128)(2,1)S(1)}, bf16[64,1024]{1,0:T(8,128)(2,1)S(1)}, u32[]{:S(2)}, u32[]{:S(2)}) collective-permute-start(bf16[64,1024]{1,0:T(8,128)(2,1)S(1)} %get-tuple-element.36), channel_id=1, source_target_pairs={{0,8},{1,9},{2,10},{3,11},{4,12},{5,13},{6,14},{7,15},{16,24},{17,... | collective-permute-start | bytes 393224 | tf_op jit(solution)/shard_map/ppermute | solution.py:483
  11.4 0.9 %collective-permute-done.2.other = bf16[2048,1024]{1,0:T(8,128)(2,1)S(1)} collective-permute-done((bf16[2048,1024]{1,0:T(8,128)(2,1)S(1)}, bf16[2048,1024]{1,0:T(8,128)(2,1)S(1)}, u32[]{:S(2)}, u32[]{:S(2)}) %collective-permute-start.2) | collective-permute-done | bytes 4194336 | tf_op jit(solution)/shard_map/ppermute | solution.py:468
  12.6 1.7 %collective-permute-done.1.refs_0_.refs_2_.refs_4_ = bf16[64,1024]{1,0:T(8,128)(2,1)S(1)} collective-permute-done((bf16[64,1024]{1,0:T(8,128)(2,1)S(1)}, bf16[64,1024]{1,0:T(8,128)(2,1)S(1)}, u32[]{:S(2)}, u32[]{:S(2)}) %collective-permute-start.1) | collective-permute-done | bytes 131104 | tf_op jit(solution)/shard_map/ppermute | solution.py:483
  14.4 1.3 %collective-permute-start.3 = (bf16[64,1024]{1,0:T(8,128)(2,1)S(1)}, bf16[64,1024]{1,0:T(8,128)(2,1)S(1)}, u32[]{:S(2)}, u32[]{:S(2)}) collective-permute-start(bf16[64,1024]{1,0:T(8,128)(2,1)S(1)} %get-tuple-element.38), channel_id=1, source_target_pairs={{8,0},{9,1},{10,2},{11,3},{12,4},{13,5},{14,6},{15,7},{24,16},{25,... | collective-permute-start | bytes 393224 | tf_op jit(solution)/shard_map/ppermute | solution.py:483
  15.6 4.5 %collective-permute-start.10 = (bf16[128,1024]{1,0:T(8,128)(2,1)S(1)}, bf16[128,1024]{1,0:T(8,128)(2,1)S(1)}, u32[]{:S(2)}, u32[]{:S(2)}) collective-permute-start(bf16[128,1024]{1,0:T(8,128)(2,1)S(1)} %pack.1.refs_0_.refs_1_.refs_3_), channel_id=1, source_target_pairs={{0,2},{1,3},{2,0},{3,1},{4,6},{5,7},{6,4},{7,5},{16,18},{17,19},{1... | collective-permute-start | bytes 786440 | tf_op jit(solution)/shard_map/ppermute | solution.py:474
  20.1 0.7 collective-permute-start.9
  20.8 3.3 %collective-permute-done.3.refs_0_.refs_2_ = bf16[64,1024]{1,0:T(8,128)(2,1)S(1)} collective-permute-done((bf16[64,1024]{1,0:T(8,128)(2,1)S(1)}, bf16[64,1024]{1,0:T(8,128)(2,1)S(1)}, u32[]{:S(2)}, u32[]{:S(2)}) %collective-permute-start.3) | collective-permute-done | bytes 131104 | tf_op jit(solution)/shard_map/ppermute | solution.py:483
  24.2 3.2 %chain_dec_decb.1 = bf16[64,1024]{1,0:T(8,128)(2,1)S(1)} custom-call(bf16[64,1024]{1,0:T(8,128)(2,1)S(1)} %collective-permute-done.3.refs_0_.refs_2_, bf16[128,1024]{1,0:T(8,128)(2,1)S(1)} %pack.1.refs_0_.refs_1_.refs_3_, bf16[2,2048,1024]{2,1,0:T(8,128)(2,1)S(1)} %load_other.3.refs_2_.refs_4_.refs_6_, bf16[2,64,1024]{2,1,0:T(8,128)(2,1)S(1)} %get-tuple-element.39.refs_3_), custom_call_target="tpu_custom_call" | custom-call | flops 10000000000 | bytes 1024 | tf_op jit(solution)/shard_map/chain_dec_decb/pallas_call | solution.py:339
  27.4 1.3 %collective-permute-start.4 = (bf16[64,1024]{1,0:T(8,128)(2,1)S(1)}, bf16[64,1024]{1,0:T(8,128)(2,1)S(1)}, u32[]{:S(2)}, u32[]{:S(2)}) collective-permute-start(bf16[64,1024]{1,0:T(8,128)(2,1)S(1)} %chain_dec_decb.1), channel_id=1, source_target_pairs={{0,8},{1,9},{2,10},{3,11},{4,12},{5,13},{6,14},{7,15},{16,24},{17,... | collective-permute-start | bytes 393224 | tf_op jit(solution)/shard_map/ppermute | solution.py:483
  28.7 1.3 %collective-permute-start.6 = (bf16[64,1024]{1,0:T(8,128)(2,1)S(1)}, bf16[64,1024]{1,0:T(8,128)(2,1)S(1)}, u32[]{:S(2)}, u32[]{:S(2)}) collective-permute-start(bf16[64,1024]{1,0:T(8,128)(2,1)S(1)} %get-tuple-element.38), channel_id=1, source_target_pairs={{8,2},{9,3},{10,0},{11,1},{12,6},{13,7},{14,4},{15,5},{24,18},{25,... | collective-permute-start | bytes 393224 | tf_op jit(solution)/shard_map/ppermute | solution.py:483
  30.0 6.4 %collective-permute-start.5 = (bf16[64,1024]{1,0:T(8,128)(2,1)S(1)}, bf16[64,1024]{1,0:T(8,128)(2,1)S(1)}, u32[]{:S(2)}, u32[]{:S(2)}) collective-permute-start(bf16[64,1024]{1,0:T(8,128)(2,1)S(1)} %chain_dec_decb.1), channel_id=1, source_target_pairs={{0,10},{1,11},{2,8},{3,9},{4,14},{5,15},{6,12},{7,13},{16,26},{17,... | collective-permute-start | bytes 393224 | tf_op jit(solution)/shard_map/ppermute | solution.py:483
  36.5 1.6 %collective-permute-start.11 = (bf16[256,1024]{1,0:T(8,128)(2,1)S(1)}, bf16[256,1024]{1,0:T(8,128)(2,1)S(1)}, u32[]{:S(2)}, u32[]{:S(2)}) collective-permute-start(bf16[256,1024]{1,0:T(8,128)(2,1)S(1)} %merge.5), channel_id=1, source_target_pairs={{0,1},{1,0},{2,3},{3,2},{4,5},{5,4},{6,7},{7,6},{8,9},{9,8},{10,11... | collective-permute-start | bytes 1572872 | tf_op jit(solution)/shard_map/ppermute | solution.py:472
  38.1 1.3 %collective-permute-start.7 = (bf16[64,1024]{1,0:T(8,128)(2,1)S(1)}, bf16[64,1024]{1,0:T(8,128)(2,1)S(1)}, u32[]{:S(2)}, u32[]{:S(2)}) collective-permute-start(bf16[64,1024]{1,0:T(8,128)(2,1)S(1)} %chain_decb_encb.1), channel_id=1, source_target_pairs={{8,0},{9,1},{10,2},{11,3},{12,4},{13,5},{14,6},{15,7},{24,16},{25,... | collective-permute-start | bytes 393224 | tf_op jit(solution)/shard_map/ppermute | solution.py:483
  39.4 0.8 %collective-permute-done.5.refs_2_.refs_1_ = bf16[64,1024]{1,0:T(8,128)(2,1)S(1)} collective-permute-done((bf16[64,1024]{1,0:T(8,128)(2,1)S(1)}, bf16[64,1024]{1,0:T(8,128)(2,1)S(1)}, u32[]{:S(2)}, u32[]{:S(2)}) %collective-permute-start.5) | collective-permute-done | bytes 131104 | tf_op jit(solution)/shard_map/ppermute | solution.py:483
  40.2 6.0 %collective-permute-done.7.refs_0_ = bf16[64,1024]{1,0:T(8,128)(2,1)S(1)} collective-permute-done((bf16[64,1024]{1,0:T(8,128)(2,1)S(1)}, bf16[64,1024]{1,0:T(8,128)(2,1)S(1)}, u32[]{:S(2)}, u32[]{:S(2)}) %collective-permute-start.7) | collective-permute-done | bytes 131104 | tf_op jit(solution)/shard_map/ppermute | solution.py:483
  46.8 1.3 %collective-permute-start.12 = (bf16[64,1024]{1,0:T(8,128)(2,1)S(1)}, bf16[64,1024]{1,0:T(8,128)(2,1)S(1)}, u32[]{:S(2)}, u32[]{:S(2)}) collective-permute-start(bf16[64,1024]{1,0:T(8,128)(2,1)S(1)} %chain_decb_encb.1), channel_id=1, source_target_pairs={{8,1},{9,0},{10,3},{11,2},{12,5},{13,4},{14,7},{15,6},{24,17},{25,... | collective-permute-start | bytes 393224 | tf_op jit(solution)/shard_map/ppermute | solution.py:483
  48.1 1.3 %collective-permute-start.13 = (bf16[64,1024]{1,0:T(8,128)(2,1)S(1)}, bf16[64,1024]{1,0:T(8,128)(2,1)S(1)}, u32[]{:S(2)}, u32[]{:S(2)}) collective-permute-start(bf16[64,1024]{1,0:T(8,128)(2,1)S(1)} %chain_decb_encb.1), channel_id=1, source_target_pairs={{8,2},{9,3},{10,0},{11,1},{12,6},{13,7},{14,4},{15,5},{24,18},{25,... | collective-permute-start | bytes 393224 | tf_op jit(solution)/shard_map/ppermute | solution.py:483
  49.4 1.3 %collective-permute-start.14 = (bf16[64,1024]{1,0:T(8,128)(2,1)S(1)}, bf16[64,1024]{1,0:T(8,128)(2,1)S(1)}, u32[]{:S(2)}, u32[]{:S(2)}) collective-permute-start(bf16[64,1024]{1,0:T(8,128)(2,1)S(1)} %chain_decb_encb.1), channel_id=1, source_target_pairs={{8,3},{9,2},{10,1},{11,0},{12,7},{13,6},{14,5},{15,4},{24,19},{25,... | collective-permute-start | bytes 393224 | tf_op jit(solution)/shard_map/ppermute | solution.py:483
  50.7 2.5 %collective-permute-done.11.refs_2_.refs_5_ = bf16[256,1024]{1,0:T(8,128)(2,1)S(1)} collective-permute-done((bf16[256,1024]{1,0:T(8,128)(2,1)S(1)}, bf16[256,1024]{1,0:T(8,128)(2,1)S(1)}, u32[]{:S(2)}, u32[]{:S(2)}) %collective-permute-start.11) | collective-permute-done | bytes 524320 | tf_op jit(solution)/shard_map/ppermute | solution.py:472
  53.1 2.0 %wide_enc.1 = (bf16[2,256,1024]{2,1,0:T(8,128)(2,1)S(1)}, f32[2,256,128]{2,1,0:T(8,128)S(1)}, f32[2,256,1024]{2,1,0:T(8,128)S(1)}) custom-call(bf16[128,1024]{1,0:T(8,128)(2,1)S(1)} %pack.1.refs_0_.refs_1_.refs_3_, bf16[128,1024]{1,0:T(8,128)(2,1)S(1)} %collective-permute-done.10.refs_1_.refs_4_, ...), custom_call_target="tpu_custom_call" | custom-call | flops 1024 | bytes 1024 | tf_op jit(solution)/shard_map/wide_enc/pallas_call | solution.py:339
  55.3 1.9 %collective-permute-done.8.refs_2_ = bf16[128,1024]{1,0:T(8,128)(2,1)S(1)} collective-permute-done((bf16[128,1024]{1,0:T(8,128)(2,1)S(1)}, bf16[128,1024]{1,0:T(8,128)(2,1)S(1)}, u32[]{:S(2)}, u32[]{:S(2)}) %collective-permute-start.8) | collective-permute-done | bytes 262176 | tf_op jit(solution)/shard_map/ppermute | solution.py:472
  57.2 5.3 %wide_dec_decb.1 = (bf16[2,256,1024]{2,1,0:T(8,128)(2,1)S(1)}, bf16[256,1792]{1,0:T(8,128)(2,1)S(1)}, bf16[256,1792]{1,0:T(8,128)(2,1)S(1)}) custom-call(bf16[64,1024]{1,0:T(8,128)(2,1)S(1)} %collective-permute-done.3.refs_0_.refs_2_, bf16[64,1024]{1,0:T(8,128)(2,1)S(1)} %collective-permute-done.6.refs_1_.refs_3_, ...), custom_call_target="tpu_custom_call" | custom-call | flops 1024 | bytes 1024 | tf_op jit(solution)/shard_map/wide_dec_decb/pallas_call | solution.py:339
  62.9 0.6 collective-permute-done.12.refs_1_
  63.5 1.5 %wide_encb.1 = (bf16[256,1024]{1,0:T(8,128)(2,1)S(1)}, bf16[256,1024]{1,0:T(8,128)(2,1)S(1)}) custom-call(bf16[64,1024]{1,0:T(8,128)(2,1)S(1)} %collective-permute-done.7.refs_0_, bf16[64,1024]{1,0:T(8,128)(2,1)S(1)} %collective-permute-done.12.refs_1_, bf16[64,1024]{1,0:T(8,128)(2,1)S(1)} %collective-permute-done.13.refs_2_, ...), custom_call_target="tpu_custom_call" | custom-call | flops 1024 | bytes 1024 | tf_op jit(solution)/shard_map/wide_encb/pallas_call | solution.py:339
  65.0 0.6 collective-permute-start.16
  65.9 1.8 %wgrad_dec.1 = f32[512,1024]{1,0:T(8,128)} custom-call(bf16[256,1792]{1,0:T(8,128)(2,1)S(1)} %get-tuple-element.61.a_own.b_own, bf16[256,1792]{1,0:T(8,128)(2,1)S(1)} %collective-permute-done.15.a_oth.b_oth, bf16[256,1792]{1,0:T(8,128)(2,1)S(1)} %get-tuple-element.61.a_own.b_own, bf16[256,1792]{1,0:T(8,128)(2,1)S(1)} %collective-permute-done.15.a_oth.b_oth), custom_call_target="tpu_custom_call" | custom-call | flops 1024 | bytes 1024 | tf_op jit(solution)/shard_map/wgrad_dec/pallas_call | solution.py:376
  67.8 1.3 %wgrad_enc.1 = f32[256,1024]{1,0:T(8,128)} custom-call(bf16[256,1792]{1,0:T(8,128)(2,1)S(1)} %get-tuple-element.61.a_own.b_own, bf16[256,1792]{1,0:T(8,128)(2,1)S(1)} %collective-permute-done.15.a_oth.b_oth, bf16[256,1024]{1,0:T(8,128)(2,1)S(1)} %get-tuple-element.68.b_own, bf16[256,1024]{1,0:T(8,128)(2,1)S(1)} %collective-permute-done.16.b_oth), custom_call_target="tpu_custom_call" | custom-call | flops 1024 | bytes 1024 | tf_op jit(solution)/shard_map/wgrad_enc/pallas_call | solution.py:376
  (29 shorter events, 3.3 us)
Async XLA Ops:
  0.6 4.5 %copy-start = (bf16[1,2048,1024]{2,1,0:T(8,128)(2,1)S(1)}, bf16[1,2048,1024]{2,1,0:T(8,128)(2,1)}, u32[]{:S(2)}) copy-start(bf16[1,2048,1024]{2,1,0:T(8,128)(2,1)} %param.7) | copy-start | bytes 12582916
  0.6 4.5 %collective-permute-start = (bf16[1024,1024]{1,0:T(8,128)(2,1)}, bf16[1024,1024]{1,0:T(8,128)(2,1)S(1)}, u32[]{:S(2)}, u32[]{:S(2)}) collective-permute-start(bf16[1024,1024]{1,0:T(8,128)(2,1)} %bitcast.6), channel_id=1, source_target_pairs={{0,4},{4,0},{8,12},{12,8},{1,5},{5,1},{9,13},{13,9},{2,6},{6,2},{1... | collective-permute-start | bytes 6291464 | tf_op jit(solution)/shard_map/ppermute | solution.py:468
  1.2 1.9 %copy-start.1 = (bf16[1,1024,1024]{2,1,0:T(8,128)(2,1)S(1)}, bf16[1,1024,1024]{2,1,0:T(8,128)(2,1)}, u32[]{:S(2)}) copy-start(bf16[1,1024,1024]{2,1,0:T(8,128)(2,1)} %param.6) | copy-start | bytes 6291460
  3.0 0.9 %copy-start.2 = (bf16[4,32,1024]{2,1,0:T(8,128)(2,1)S(1)}, bf16[4,32,1024]{2,1,0:T(8,128)(2,1)}, u32[]{:S(2)}) copy-start(bf16[4,32,1024]{2,1,0:T(8,128)(2,1)} %inputs.1) | copy-start | bytes 786436
  3.0 1.0 %copy-start.3 = (bf16[4,32,1024]{2,1,0:T(8,128)(2,1)S(1)}, bf16[4,32,1024]{2,1,0:T(8,128)(2,1)}, u32[]{:S(2)}) copy-start(bf16[4,32,1024]{2,1,0:T(8,128)(2,1)} %cotangent.1) | copy-start | bytes 786436
  5.2 7.2 %collective-permute-start.2 = (bf16[2048,1024]{1,0:T(8,128)(2,1)S(1)}, bf16[2048,1024]{1,0:T(8,128)(2,1)S(1)}, u32[]{:S(2)}, u32[]{:S(2)}) collective-permute-start(bf16[2048,1024]{1,0:T(8,128)(2,1)S(1)} %bitcast.4), channel_id=1, source_target_pairs={{0,4},{4,0},{8,12},{12,8},{1,5},{5,1},{9,13},{13,9},{2,6},{6,2},{1... | collective-permute-start | bytes 12582920 | tf_op jit(solution)/shard_map/ppermute | solution.py:468
  7.7 6.7 %collective-permute-start.1 = (bf16[64,1024]{1,0:T(8,128)(2,1)S(1)}, bf16[64,1024]{1,0:T(8,128)(2,1)S(1)}, u32[]{:S(2)}, u32[]{:S(2)}) collective-permute-start(bf16[64,1024]{1,0:T(8,128)(2,1)S(1)} %get-tuple-element.36), channel_id=1, source_target_pairs={{0,8},{1,9},{2,10},{3,11},{4,12},{5,13},{6,14},{7,15},{16,24},{17,... | collective-permute-start | bytes 393224 | tf_op jit(solution)/shard_map/ppermute | solution.py:483
  14.4 9.8 %collective-permute-start.3 = (bf16[64,1024]{1,0:T(8,128)(2,1)S(1)}, bf16[64,1024]{1,0:T(8,128)(2,1)S(1)}, u32[]{:S(2)}, u32[]{:S(2)}) collective-permute-start(bf16[64,1024]{1,0:T(8,128)(2,1)S(1)} %get-tuple-element.38), channel_id=1, source_target_pairs={{8,0},{9,1},{10,2},{11,3},{12,4},{13,5},{14,6},{15,7},{24,16},{25,... | collective-permute-start | bytes 393224 | tf_op jit(solution)/shard_map/ppermute | solution.py:483
  15.6 20.8 %collective-permute-start.10 = (bf16[128,1024]{1,0:T(8,128)(2,1)S(1)}, bf16[128,1024]{1,0:T(8,128)(2,1)S(1)}, u32[]{:S(2)}, u32[]{:S(2)}) collective-permute-start(bf16[128,1024]{1,0:T(8,128)(2,1)S(1)} %pack.1.refs_0_.refs_1_.refs_3_), channel_id=1, source_target_pairs={{0,2},{1,3},{2,0},{3,1},{4,6},{5,7},{6,4},{7,5},{16,18},{17,19},{1... | collective-permute-start | bytes 786440 | tf_op jit(solution)/shard_map/ppermute | solution.py:474
  20.1 16.2 %collective-permute-start.9 = (bf16[64,1024]{1,0:T(8,128)(2,1)S(1)}, bf16[64,1024]{1,0:T(8,128)(2,1)S(1)}, u32[]{:S(2)}, u32[]{:S(2)}) collective-permute-start(bf16[64,1024]{1,0:T(8,128)(2,1)S(1)} %collective-permute-done.1.refs_0_.refs_2_.refs_4_), channel_id=1, source_target_pairs={{8,10},{9,11},{10,8},{11,9},{12,14},{13,15},{14,12},{15,13},{24,26... | collective-permute-start | bytes 393224 | tf_op jit(solution)/shard_map/ppermute | solution.py:474
  27.4 9.0 %collective-permute-start.4 = (bf16[64,1024]{1,0:T(8,128)(2,1)S(1)}, bf16[64,1024]{1,0:T(8,128)(2,1)S(1)}, u32[]{:S(2)}, u32[]{:S(2)}) collective-permute-start(bf16[64,1024]{1,0:T(8,128)(2,1)S(1)} %chain_dec_decb.1), channel_id=1, source_target_pairs={{0,8},{1,9},{2,10},{3,11},{4,12},{5,13},{6,14},{7,15},{16,24},{17,... | collective-permute-start | bytes 393224 | tf_op jit(solution)/shard_map/ppermute | solution.py:483
  28.7 10.7 %collective-permute-start.6 = (bf16[64,1024]{1,0:T(8,128)(2,1)S(1)}, bf16[64,1024]{1,0:T(8,128)(2,1)S(1)}, u32[]{:S(2)}, u32[]{:S(2)}) collective-permute-start(bf16[64,1024]{1,0:T(8,128)(2,1)S(1)} %get-tuple-element.38), channel_id=1, source_target_pairs={{8,2},{9,3},{10,0},{11,1},{12,6},{13,7},{14,4},{15,5},{24,18},{25,... | collective-permute-start | bytes 393224 | tf_op jit(solution)/shard_map/ppermute | solution.py:483
  30.0 10.2 %collective-permute-start.5 = (bf16[64,1024]{1,0:T(8,128)(2,1)S(1)}, bf16[64,1024]{1,0:T(8,128)(2,1)S(1)}, u32[]{:S(2)}, u32[]{:S(2)}) collective-permute-start(bf16[64,1024]{1,0:T(8,128)(2,1)S(1)} %chain_dec_decb.1), channel_id=1, source_target_pairs={{0,10},{1,11},{2,8},{3,9},{4,14},{5,15},{6,12},{7,13},{16,26},{17,... | collective-permute-start | bytes 393224 | tf_op jit(solution)/shard_map/ppermute | solution.py:483
  36.5 16.7 %collective-permute-start.11 = (bf16[256,1024]{1,0:T(8,128)(2,1)S(1)}, bf16[256,1024]{1,0:T(8,128)(2,1)S(1)}, u32[]{:S(2)}, u32[]{:S(2)}) collective-permute-start(bf16[256,1024]{1,0:T(8,128)(2,1)S(1)} %merge.5), channel_id=1, source_target_pairs={{0,1},{1,0},{2,3},{3,2},{4,5},{5,4},{6,7},{7,6},{8,9},{9,8},{10,11... | collective-permute-start | bytes 1572872 | tf_op jit(solution)/shard_map/ppermute | solution.py:472
  38.1 8.1 %collective-permute-start.7 = (bf16[64,1024]{1,0:T(8,128)(2,1)S(1)}, bf16[64,1024]{1,0:T(8,128)(2,1)S(1)}, u32[]{:S(2)}, u32[]{:S(2)}) collective-permute-start(bf16[64,1024]{1,0:T(8,128)(2,1)S(1)} %chain_decb_encb.1), channel_id=1, source_target_pairs={{8,0},{9,1},{10,2},{11,3},{12,4},{13,5},{14,6},{15,7},{24,16},{25,... | collective-permute-start | bytes 393224 | tf_op jit(solution)/shard_map/ppermute | solution.py:483
  46.3 10.9 %collective-permute-start.8 = (bf16[128,1024]{1,0:T(8,128)(2,1)S(1)}, bf16[128,1024]{1,0:T(8,128)(2,1)S(1)}, u32[]{:S(2)}, u32[]{:S(2)}) collective-permute-start(bf16[128,1024]{1,0:T(8,128)(2,1)S(1)} %merge.4), channel_id=1, source_target_pairs={{0,1},{1,0},{2,3},{3,2},{4,5},{5,4},{6,7},{7,6},{8,9},{9,8},{10,11... | collective-permute-start | bytes 786440 | tf_op jit(solution)/shard_map/ppermute | solution.py:472
  46.8 16.7 %collective-permute-start.12 = (bf16[64,1024]{1,0:T(8,128)(2,1)S(1)}, bf16[64,1024]{1,0:T(8,128)(2,1)S(1)}, u32[]{:S(2)}, u32[]{:S(2)}) collective-permute-start(bf16[64,1024]{1,0:T(8,128)(2,1)S(1)} %chain_decb_encb.1), channel_id=1, source_target_pairs={{8,1},{9,0},{10,3},{11,2},{12,5},{13,4},{14,7},{15,6},{24,17},{25,... | collective-permute-start | bytes 393224 | tf_op jit(solution)/shard_map/ppermute | solution.py:483
  48.1 15.4 %collective-permute-start.13 = (bf16[64,1024]{1,0:T(8,128)(2,1)S(1)}, bf16[64,1024]{1,0:T(8,128)(2,1)S(1)}, u32[]{:S(2)}, u32[]{:S(2)}) collective-permute-start(bf16[64,1024]{1,0:T(8,128)(2,1)S(1)} %chain_decb_encb.1), channel_id=1, source_target_pairs={{8,2},{9,3},{10,0},{11,1},{12,6},{13,7},{14,4},{15,5},{24,18},{25,... | collective-permute-start | bytes 393224 | tf_op jit(solution)/shard_map/ppermute | solution.py:483
  49.4 14.1 %collective-permute-start.14 = (bf16[64,1024]{1,0:T(8,128)(2,1)S(1)}, bf16[64,1024]{1,0:T(8,128)(2,1)S(1)}, u32[]{:S(2)}, u32[]{:S(2)}) collective-permute-start(bf16[64,1024]{1,0:T(8,128)(2,1)S(1)} %chain_decb_encb.1), channel_id=1, source_target_pairs={{8,3},{9,2},{10,1},{11,0},{12,7},{13,6},{14,5},{15,4},{24,19},{25,... | collective-permute-start | bytes 393224 | tf_op jit(solution)/shard_map/ppermute | solution.py:483
  63.5 2.5 %collective-permute-start.15 = (bf16[256,1792]{1,0:T(8,128)(2,1)S(1)}, bf16[256,1792]{1,0:T(8,128)(2,1)S(1)}, u32[]{:S(2)}, u32[]{:S(2)}) collective-permute-start(bf16[256,1792]{1,0:T(8,128)(2,1)S(1)} %get-tuple-element.63), channel_id=1, source_target_pairs={{0,4},{4,0},{8,12},{12,8},{1,5},{5,1},{9,13},{13,9},{2,6},{6,2},{1... | collective-permute-start | bytes 2752520 | tf_op jit(solution)/shard_map/ppermute | solution.py:468
  65.0 2.8 %collective-permute-start.16 = (bf16[256,1024]{1,0:T(8,128)(2,1)S(1)}, bf16[256,1024]{1,0:T(8,128)(2,1)S(1)}, u32[]{:S(2)}, u32[]{:S(2)}) collective-permute-start(bf16[256,1024]{1,0:T(8,128)(2,1)S(1)} %get-tuple-element.69), channel_id=1, source_target_pairs={{0,4},{4,0},{8,12},{12,8},{1,5},{5,1},{9,13},{13,9},{2,6},{6,2},{1... | collective-permute-start | bytes 1572872 | tf_op jit(solution)/shard_map/ppermute | solution.py:468

commit v5 on v4

--- a/solution.py
+++ b/solution.py
@@ -129,7 +129,8 @@
 
     def activate(pre, gain_ref, level, sl):
         sigma = jax.nn.sigmoid(pre)
-        gain_ref[level, :, sl] = sigma * (1.0 + pre * (1.0 - sigma))
+        if gain_ref is not None:
+            gain_ref[level, :, sl] = sigma * (1.0 + pre * (1.0 - sigma))
         x[:, sl] = (x[:, sl].astype(jnp.float32) + pre * sigma).astype(jnp.bfloat16)
 
     def enc_level(level):
@@ -137,7 +138,7 @@
         normalize(level, n, ref["r"])
 
         def step(at, sl, carry):
-            activate(dot(n[level], we[level, :, sl]), ref["ga"], level, sl)
+            activate(dot(n[level], we[level, :, sl]), ref.get("ga"), level, sl)
             return carry
 
         for_tiles(step)
@@ -315,7 +316,7 @@
         scratch["work_x"] = matrix
     for op in ops:
         for name in MAKES[op]:
-            if name == "k" and skip_k:
+            if name in ("k", "ga") and skip_k:
                 continue
             if (name == "k" and "encb" in ops) or (name in ("nd", "rd", "gb") and "decb" in ops):
                 scratch[name] = kinds[name]

time: 69.6 us -> 69.4 us (level)
  transfers between devices with their start and end apart: 17 -> 17, of which waited for: 10 -> 10; matrix products, arithmetic and copies ran while one was open for 0% -> 0% of each run, Pallas kernels for 26% -> 25%
where the time goes in v5:
time: 69.4 us; the launch traced here: 69.1 us
  starting transfers between devices  27.6 us (40%)
  Pallas kernels  18.8 us (27%)
  waiting for transfers between devices  18.8 us (27%)
  local copies, waits for them, and re-layouts  2.72 us (4%)
  between operations  1.08 us (2%)
    ppermute x9, starting transfers between devices, hop(): lax.ppermute(value, ('section', 'dp'), [((2 * source + c) * dp_count + d,...  18.8 us
    pallas_call x9, Pallas kernels, run_stage(): pl.pallas_call(functools.partial(stage_kernel, cfg), name=('wide_' if wid...  14.4 us
    ppermute x9, waiting for transfers between devices, hop(): lax.ppermute(value, ('section', 'dp'), [((2 * source + c) * dp_count + d,...  12.2 us
    ppermute x2, starting transfers between devices, flip_dp(): lax.ppermute(value, ('section', 'dp'), [(first + i, first + (i ^ flip)) f...  5.17 us
    ppermute x2, waiting for transfers between devices, flip_dp(): return lax.ppermute(value, 'dp', [(i, i ^ flip) for i in range(dp_count)])  4.31 us
    pallas_call x2, Pallas kernels, wgrad(): pl.pallas_call(functools.partial(wgrad_kernel, skip, base), name=name, ou...  3.13 us
    unnamed x8, local copies, waits for them, and re-layouts  2.72 us
    ppermute x4, waiting for transfers between devices, swap(): lax.ppermute(value, 'section', [(i, i ^ 1) for i in range(section_count)])  2.28 us
  transfers between devices with their start and end apart: 17, of which 10 were waited for; matrix products, arithmetic and copies ran while one was open for 0% of the time, Pallas kernels for 25%

profile of v5, /device:TPU:0, one launch (start us, length us, event | category | flops | bytes accessed | tf_op | source)
XLA Modules:
  0.0 69.1 jit_solution(84156833675838676)
XLA Ops:
  0.6 0.5 collective-permute-start
  1.2 1.8 %copy-done.1 = bf16[1,1024,1024]{2,1,0:T(8,128)(2,1)S(1)} copy-done((bf16[1,1024,1024]{2,1,0:T(8,128)(2,1)S(1)}, bf16[1,1024,1024]{2,1,0:T(8,128)(2,1)}, u32[]{:S(2)}) %copy-start.1) | copy-done | bytes 2097176
  3.2 0.8 %copy-done.2 = bf16[4,32,1024]{2,1,0:T(8,128)(2,1)S(1)} copy-done((bf16[4,32,1024]{2,1,0:T(8,128)(2,1)S(1)}, bf16[4,32,1024]{2,1,0:T(8,128)(2,1)}, u32[]{:S(2)}) %copy-start.2) | copy-done | bytes 262168
  4.4 0.8 %collective-permute-done.other = bf16[1024,1024]{1,0:T(8,128)(2,1)S(1)} collective-permute-done((bf16[1024,1024]{1,0:T(8,128)(2,1)}, bf16[1024,1024]{1,0:T(8,128)(2,1)S(1)}, u32[]{:S(2)}, u32[]{:S(2)}) %collective-permute-start) | collective-permute-done | bytes 2097184 | tf_op jit(solution)/shard_map/ppermute | solution.py:469
  5.7 1.8 %chain_enc.1 = (bf16[64,1024]{1,0:T(8,128)(2,1)S(1)}, bf16[2,64,1024]{2,1,0:T(8,128)(2,1)S(1)}, f32[2,64,128]{2,1,0:T(8,128)}) custom-call(bf16[128,1024]{1,0:T(8,128)(2,1)S(1)} %pack.1.refs_0_.refs_1_.refs_3_, bf16[2,1024,1024]{2,1,0:T(8,128)(2,1)S(1)} %load_other.2.refs_1_.refs_3_.refs_4_), custom_call_target="tpu_custom_call" | custom-call | flops 1024 | bytes 1024 | tf_op jit(solution)/shard_map/chain_enc/pallas_call | solution.py:340
  7.5 3.4 %collective-permute-start.1 = (bf16[64,1024]{1,0:T(8,128)(2,1)S(1)}, bf16[64,1024]{1,0:T(8,128)(2,1)S(1)}, u32[]{:S(2)}, u32[]{:S(2)}) collective-permute-start(bf16[64,1024]{1,0:T(8,128)(2,1)S(1)} %get-tuple-element.36), channel_id=1, source_target_pairs={{0,8},{1,9},{2,10},{3,11},{4,12},{5,13},{6,14},{7,15},{16,24},{17,... | collective-permute-start | bytes 393224 | tf_op jit(solution)/shard_map/ppermute | solution.py:484
  11.2 1.1 %collective-permute-done.2.other = bf16[2048,1024]{1,0:T(8,128)(2,1)S(1)} collective-permute-done((bf16[2048,1024]{1,0:T(8,128)(2,1)S(1)}, bf16[2048,1024]{1,0:T(8,128)(2,1)S(1)}, u32[]{:S(2)}, u32[]{:S(2)}) %collective-permute-start.2) | collective-permute-done | bytes 4194336 | tf_op jit(solution)/shard_map/ppermute | solution.py:469
  12.6 1.6 %collective-permute-done.1.refs_0_.refs_2_.refs_4_ = bf16[64,1024]{1,0:T(8,128)(2,1)S(1)} collective-permute-done((bf16[64,1024]{1,0:T(8,128)(2,1)S(1)}, bf16[64,1024]{1,0:T(8,128)(2,1)S(1)}, u32[]{:S(2)}, u32[]{:S(2)}) %collective-permute-start.1) | collective-permute-done | bytes 131104 | tf_op jit(solution)/shard_map/ppermute | solution.py:484
  14.2 1.3 %collective-permute-start.3 = (bf16[64,1024]{1,0:T(8,128)(2,1)S(1)}, bf16[64,1024]{1,0:T(8,128)(2,1)S(1)}, u32[]{:S(2)}, u32[]{:S(2)}) collective-permute-start(bf16[64,1024]{1,0:T(8,128)(2,1)S(1)} %get-tuple-element.38), channel_id=1, source_target_pairs={{8,0},{9,1},{10,2},{11,3},{12,4},{13,5},{14,6},{15,7},{24,16},{25,... | collective-permute-start | bytes 393224 | tf_op jit(solution)/shard_map/ppermute | solution.py:484
  15.5 4.5 %collective-permute-start.10 = (bf16[128,1024]{1,0:T(8,128)(2,1)S(1)}, bf16[128,1024]{1,0:T(8,128)(2,1)S(1)}, u32[]{:S(2)}, u32[]{:S(2)}) collective-permute-start(bf16[128,1024]{1,0:T(8,128)(2,1)S(1)} %pack.1.refs_0_.refs_1_.refs_3_), channel_id=1, source_target_pairs={{0,2},{1,3},{2,0},{3,1},{4,6},{5,7},{6,4},{7,5},{16,18},{17,19},{1... | collective-permute-start | bytes 786440 | tf_op jit(solution)/shard_map/ppermute | solution.py:475
  20.0 0.7 collective-permute-start.9
  20.6 3.3 %collective-permute-done.3.refs_0_.refs_2_ = bf16[64,1024]{1,0:T(8,128)(2,1)S(1)} collective-permute-done((bf16[64,1024]{1,0:T(8,128)(2,1)S(1)}, bf16[64,1024]{1,0:T(8,128)(2,1)S(1)}, u32[]{:S(2)}, u32[]{:S(2)}) %collective-permute-start.3) | collective-permute-done | bytes 131104 | tf_op jit(solution)/shard_map/ppermute | solution.py:484
  24.0 3.2 %chain_dec_decb.1 = bf16[64,1024]{1,0:T(8,128)(2,1)S(1)} custom-call(bf16[64,1024]{1,0:T(8,128)(2,1)S(1)} %collective-permute-done.3.refs_0_.refs_2_, bf16[128,1024]{1,0:T(8,128)(2,1)S(1)} %pack.1.refs_0_.refs_1_.refs_3_, bf16[2,2048,1024]{2,1,0:T(8,128)(2,1)S(1)} %load_other.3.refs_2_.refs_4_.refs_6_, bf16[2,64,1024]{2,1,0:T(8,128)(2,1)S(1)} %get-tuple-element.39.refs_3_), custom_call_target="tpu_custom_call" | custom-call | flops 10000000000 | bytes 1024 | tf_op jit(solution)/shard_map/chain_dec_decb/pallas_call | solution.py:340
  27.2 1.3 %collective-permute-start.4 = (bf16[64,1024]{1,0:T(8,128)(2,1)S(1)}, bf16[64,1024]{1,0:T(8,128)(2,1)S(1)}, u32[]{:S(2)}, u32[]{:S(2)}) collective-permute-start(bf16[64,1024]{1,0:T(8,128)(2,1)S(1)} %chain_dec_decb.1), channel_id=1, source_target_pairs={{0,8},{1,9},{2,10},{3,11},{4,12},{5,13},{6,14},{7,15},{16,24},{17,... | collective-permute-start | bytes 393224 | tf_op jit(solution)/shard_map/ppermute | solution.py:484
  28.5 1.3 %collective-permute-start.6 = (bf16[64,1024]{1,0:T(8,128)(2,1)S(1)}, bf16[64,1024]{1,0:T(8,128)(2,1)S(1)}, u32[]{:S(2)}, u32[]{:S(2)}) collective-permute-start(bf16[64,1024]{1,0:T(8,128)(2,1)S(1)} %get-tuple-element.38), channel_id=1, source_target_pairs={{8,2},{9,3},{10,0},{11,1},{12,6},{13,7},{14,4},{15,5},{24,18},{25,... | collective-permute-start | bytes 393224 | tf_op jit(solution)/shard_map/ppermute | solution.py:484
  29.8 6.4 %collective-permute-start.5 = (bf16[64,1024]{1,0:T(8,128)(2,1)S(1)}, bf16[64,1024]{1,0:T(8,128)(2,1)S(1)}, u32[]{:S(2)}, u32[]{:S(2)}) collective-permute-start(bf16[64,1024]{1,0:T(8,128)(2,1)S(1)} %chain_dec_decb.1), channel_id=1, source_target_pairs={{0,10},{1,11},{2,8},{3,9},{4,14},{5,15},{6,12},{7,13},{16,26},{17,... | collective-permute-start | bytes 393224 | tf_op jit(solution)/shard_map/ppermute | solution.py:484
  36.3 1.6 %collective-permute-start.11 = (bf16[256,1024]{1,0:T(8,128)(2,1)S(1)}, bf16[256,1024]{1,0:T(8,128)(2,1)S(1)}, u32[]{:S(2)}, u32[]{:S(2)}) collective-permute-start(bf16[256,1024]{1,0:T(8,128)(2,1)S(1)} %merge.5), channel_id=1, source_target_pairs={{0,1},{1,0},{2,3},{3,2},{4,5},{5,4},{6,7},{7,6},{8,9},{9,8},{10,11... | collective-permute-start | bytes 1572872 | tf_op jit(solution)/shard_map/ppermute | solution.py:473
  37.9 1.3 %collective-permute-start.7 = (bf16[64,1024]{1,0:T(8,128)(2,1)S(1)}, bf16[64,1024]{1,0:T(8,128)(2,1)S(1)}, u32[]{:S(2)}, u32[]{:S(2)}) collective-permute-start(bf16[64,1024]{1,0:T(8,128)(2,1)S(1)} %chain_decb_encb.1), channel_id=1, source_target_pairs={{8,0},{9,1},{10,2},{11,3},{12,4},{13,5},{14,6},{15,7},{24,16},{25,... | collective-permute-start | bytes 393224 | tf_op jit(solution)/shard_map/ppermute | solution.py:484
  39.3 0.8 %collective-permute-done.5.refs_2_.refs_1_ = bf16[64,1024]{1,0:T(8,128)(2,1)S(1)} collective-permute-done((bf16[64,1024]{1,0:T(8,128)(2,1)S(1)}, bf16[64,1024]{1,0:T(8,128)(2,1)S(1)}, u32[]{:S(2)}, u32[]{:S(2)}) %collective-permute-start.5) | collective-permute-done | bytes 131104 | tf_op jit(solution)/shard_map/ppermute | solution.py:484
  40.0 6.0 %collective-permute-done.7.refs_0_ = bf16[64,1024]{1,0:T(8,128)(2,1)S(1)} collective-permute-done((bf16[64,1024]{1,0:T(8,128)(2,1)S(1)}, bf16[64,1024]{1,0:T(8,128)(2,1)S(1)}, u32[]{:S(2)}, u32[]{:S(2)}) %collective-permute-start.7) | collective-permute-done | bytes 131104 | tf_op jit(solution)/shard_map/ppermute | solution.py:484
  46.6 1.3 %collective-permute-start.12 = (bf16[64,1024]{1,0:T(8,128)(2,1)S(1)}, bf16[64,1024]{1,0:T(8,128)(2,1)S(1)}, u32[]{:S(2)}, u32[]{:S(2)}) collective-permute-start(bf16[64,1024]{1,0:T(8,128)(2,1)S(1)} %chain_decb_encb.1), channel_id=1, source_target_pairs={{8,1},{9,0},{10,3},{11,2},{12,5},{13,4},{14,7},{15,6},{24,17},{25,... | collective-permute-start | bytes 393224 | tf_op jit(solution)/shard_map/ppermute | solution.py:484
  47.9 1.3 %collective-permute-start.13 = (bf16[64,1024]{1,0:T(8,128)(2,1)S(1)}, bf16[64,1024]{1,0:T(8,128)(2,1)S(1)}, u32[]{:S(2)}, u32[]{:S(2)}) collective-permute-start(bf16[64,1024]{1,0:T(8,128)(2,1)S(1)} %chain_decb_encb.1), channel_id=1, source_target_pairs={{8,2},{9,3},{10,0},{11,1},{12,6},{13,7},{14,4},{15,5},{24,18},{25,... | collective-permute-start | bytes 393224 | tf_op jit(solution)/shard_map/ppermute | solution.py:484
  49.2 1.3 %collective-permute-start.14 = (bf16[64,1024]{1,0:T(8,128)(2,1)S(1)}, bf16[64,1024]{1,0:T(8,128)(2,1)S(1)}, u32[]{:S(2)}, u32[]{:S(2)}) collective-permute-start(bf16[64,1024]{1,0:T(8,128)(2,1)S(1)} %chain_decb_encb.1), channel_id=1, source_target_pairs={{8,3},{9,2},{10,1},{11,0},{12,7},{13,6},{14,5},{15,4},{24,19},{25,... | collective-permute-start | bytes 393224 | tf_op jit(solution)/shard_map/ppermute | solution.py:484
  50.5 2.5 %collective-permute-done.11.refs_2_.refs_5_ = bf16[256,1024]{1,0:T(8,128)(2,1)S(1)} collective-permute-done((bf16[256,1024]{1,0:T(8,128)(2,1)S(1)}, bf16[256,1024]{1,0:T(8,128)(2,1)S(1)}, u32[]{:S(2)}, u32[]{:S(2)}) %collective-permute-start.11) | collective-permute-done | bytes 524320 | tf_op jit(solution)/shard_map/ppermute | solution.py:473
  52.9 2.0 %wide_enc.1 = (bf16[2,256,1024]{2,1,0:T(8,128)(2,1)S(1)}, f32[2,256,128]{2,1,0:T(8,128)S(1)}, f32[2,256,1024]{2,1,0:T(8,128)S(1)}) custom-call(bf16[128,1024]{1,0:T(8,128)(2,1)S(1)} %pack.1.refs_0_.refs_1_.refs_3_, bf16[128,1024]{1,0:T(8,128)(2,1)S(1)} %collective-permute-done.10.refs_1_.refs_4_, ...), custom_call_target="tpu_custom_call" | custom-call | flops 1024 | bytes 1024 | tf_op jit(solution)/shard_map/wide_enc/pallas_call | solution.py:340
  55.1 1.9 %collective-permute-done.8.refs_2_ = bf16[128,1024]{1,0:T(8,128)(2,1)S(1)} collective-permute-done((bf16[128,1024]{1,0:T(8,128)(2,1)S(1)}, bf16[128,1024]{1,0:T(8,128)(2,1)S(1)}, u32[]{:S(2)}, u32[]{:S(2)}) %collective-permute-start.8) | collective-permute-done | bytes 262176 | tf_op jit(solution)/shard_map/ppermute | solution.py:473
  57.0 5.3 %wide_dec_decb.1 = (bf16[2,256,1024]{2,1,0:T(8,128)(2,1)S(1)}, bf16[256,1792]{1,0:T(8,128)(2,1)S(1)}, bf16[256,1792]{1,0:T(8,128)(2,1)S(1)}) custom-call(bf16[64,1024]{1,0:T(8,128)(2,1)S(1)} %collective-permute-done.3.refs_0_.refs_2_, bf16[64,1024]{1,0:T(8,128)(2,1)S(1)} %collective-permute-done.6.refs_1_.refs_3_, ...), custom_call_target="tpu_custom_call" | custom-call | flops 1024 | bytes 1024 | tf_op jit(solution)/shard_map/wide_dec_decb/pallas_call | solution.py:340
  62.7 0.6 collective-permute-done.12.refs_1_
  63.3 1.5 %wide_encb.1 = (bf16[256,1024]{1,0:T(8,128)(2,1)S(1)}, bf16[256,1024]{1,0:T(8,128)(2,1)S(1)}) custom-call(bf16[64,1024]{1,0:T(8,128)(2,1)S(1)} %collective-permute-done.7.refs_0_, bf16[64,1024]{1,0:T(8,128)(2,1)S(1)} %collective-permute-done.12.refs_1_, bf16[64,1024]{1,0:T(8,128)(2,1)S(1)} %collective-permute-done.13.refs_2_, ...), custom_call_target="tpu_custom_call" | custom-call | flops 1024 | bytes 1024 | tf_op jit(solution)/shard_map/wide_encb/pallas_call | solution.py:340
  64.8 0.6 collective-permute-start.16
  65.7 1.8 %wgrad_dec.1 = f32[512,1024]{1,0:T(8,128)} custom-call(bf16[256,1792]{1,0:T(8,128)(2,1)S(1)} %get-tuple-element.61.a_own.b_own, bf16[256,1792]{1,0:T(8,128)(2,1)S(1)} %collective-permute-done.15.a_oth.b_oth, bf16[256,1792]{1,0:T(8,128)(2,1)S(1)} %get-tuple-element.61.a_own.b_own, bf16[256,1792]{1,0:T(8,128)(2,1)S(1)} %collective-permute-done.15.a_oth.b_oth), custom_call_target="tpu_custom_call" | custom-call | flops 1024 | bytes 1024 | tf_op jit(solution)/shard_map/wgrad_dec/pallas_call | solution.py:377
  67.6 1.3 %wgrad_enc.1 = f32[256,1024]{1,0:T(8,128)} custom-call(bf16[256,1792]{1,0:T(8,128)(2,1)S(1)} %get-tuple-element.61.a_own.b_own, bf16[256,1792]{1,0:T(8,128)(2,1)S(1)} %collective-permute-done.15.a_oth.b_oth, bf16[256,1024]{1,0:T(8,128)(2,1)S(1)} %get-tuple-element.68.b_own, bf16[256,1024]{1,0:T(8,128)(2,1)S(1)} %collective-permute-done.16.b_oth), custom_call_target="tpu_custom_call" | custom-call | flops 1024 | bytes 1024 | tf_op jit(solution)/shard_map/wgrad_enc/pallas_call | solution.py:377
  (29 shorter events, 3.3 us)
Async XLA Ops:
  0.6 4.5 %copy-start = (bf16[1,2048,1024]{2,1,0:T(8,128)(2,1)S(1)}, bf16[1,2048,1024]{2,1,0:T(8,128)(2,1)}, u32[]{:S(2)}) copy-start(bf16[1,2048,1024]{2,1,0:T(8,128)(2,1)} %param.7) | copy-start | bytes 12582916
  0.6 4.5 %collective-permute-start = (bf16[1024,1024]{1,0:T(8,128)(2,1)}, bf16[1024,1024]{1,0:T(8,128)(2,1)S(1)}, u32[]{:S(2)}, u32[]{:S(2)}) collective-permute-start(bf16[1024,1024]{1,0:T(8,128)(2,1)} %bitcast.6), channel_id=1, source_target_pairs={{0,4},{4,0},{8,12},{12,8},{1,5},{5,1},{9,13},{13,9},{2,6},{6,2},{1... | collective-permute-start | bytes 6291464 | tf_op jit(solution)/shard_map/ppermute | solution.py:469
  1.2 1.9 %copy-start.1 = (bf16[1,1024,1024]{2,1,0:T(8,128)(2,1)S(1)}, bf16[1,1024,1024]{2,1,0:T(8,128)(2,1)}, u32[]{:S(2)}) copy-start(bf16[1,1024,1024]{2,1,0:T(8,128)(2,1)} %param.6) | copy-start | bytes 6291460
  3.0 0.9 %copy-start.2 = (bf16[4,32,1024]{2,1,0:T(8,128)(2,1)S(1)}, bf16[4,32,1024]{2,1,0:T(8,128)(2,1)}, u32[]{:S(2)}) copy-start(bf16[4,32,1024]{2,1,0:T(8,128)(2,1)} %inputs.1) | copy-start | bytes 786436
  3.0 1.0 %copy-start.3 = (bf16[4,32,1024]{2,1,0:T(8,128)(2,1)S(1)}, bf16[4,32,1024]{2,1,0:T(8,128)(2,1)}, u32[]{:S(2)}) copy-start(bf16[4,32,1024]{2,1,0:T(8,128)(2,1)} %cotangent.1) | copy-start | bytes 786436
  5.2 7.2 %collective-permute-start.2 = (bf16[2048,1024]{1,0:T(8,128)(2,1)S(1)}, bf16[2048,1024]{1,0:T(8,128)(2,1)S(1)}, u32[]{:S(2)}, u32[]{:S(2)}) collective-permute-start(bf16[2048,1024]{1,0:T(8,128)(2,1)S(1)} %bitcast.4), channel_id=1, source_target_pairs={{0,4},{4,0},{8,12},{12,8},{1,5},{5,1},{9,13},{13,9},{2,6},{6,2},{1... | collective-permute-start | bytes 12582920 | tf_op jit(solution)/shard_map/ppermute | solution.py:469
  7.5 6.7 %collective-permute-start.1 = (bf16[64,1024]{1,0:T(8,128)(2,1)S(1)}, bf16[64,1024]{1,0:T(8,128)(2,1)S(1)}, u32[]{:S(2)}, u32[]{:S(2)}) collective-permute-start(bf16[64,1024]{1,0:T(8,128)(2,1)S(1)} %get-tuple-element.36), channel_id=1, source_target_pairs={{0,8},{1,9},{2,10},{3,11},{4,12},{5,13},{6,14},{7,15},{16,24},{17,... | collective-permute-start | bytes 393224 | tf_op jit(solution)/shard_map/ppermute | solution.py:484
  14.2 9.8 %collective-permute-start.3 = (bf16[64,1024]{1,0:T(8,128)(2,1)S(1)}, bf16[64,1024]{1,0:T(8,128)(2,1)S(1)}, u32[]{:S(2)}, u32[]{:S(2)}) collective-permute-start(bf16[64,1024]{1,0:T(8,128)(2,1)S(1)} %get-tuple-element.38), channel_id=1, source_target_pairs={{8,0},{9,1},{10,2},{11,3},{12,4},{13,5},{14,6},{15,7},{24,16},{25,... | collective-permute-start | bytes 393224 | tf_op jit(solution)/shard_map/ppermute | solution.py:484
  15.5 20.7 %collective-permute-start.10 = (bf16[128,1024]{1,0:T(8,128)(2,1)S(1)}, bf16[128,1024]{1,0:T(8,128)(2,1)S(1)}, u32[]{:S(2)}, u32[]{:S(2)}) collective-permute-start(bf16[128,1024]{1,0:T(8,128)(2,1)S(1)} %pack.1.refs_0_.refs_1_.refs_3_), channel_id=1, source_target_pairs={{0,2},{1,3},{2,0},{3,1},{4,6},{5,7},{6,4},{7,5},{16,18},{17,19},{1... | collective-permute-start | bytes 786440 | tf_op jit(solution)/shard_map/ppermute | solution.py:475
  20.0 16.2 %collective-permute-start.9 = (bf16[64,1024]{1,0:T(8,128)(2,1)S(1)}, bf16[64,1024]{1,0:T(8,128)(2,1)S(1)}, u32[]{:S(2)}, u32[]{:S(2)}) collective-permute-start(bf16[64,1024]{1,0:T(8,128)(2,1)S(1)} %collective-permute-done.1.refs_0_.refs_2_.refs_4_), channel_id=1, source_target_pairs={{8,10},{9,11},{10,8},{11,9},{12,14},{13,15},{14,12},{15,13},{24,26... | collective-permute-start | bytes 393224 | tf_op jit(solution)/shard_map/ppermute | solution.py:475
  27.2 9.0 %collective-permute-start.4 = (bf16[64,1024]{1,0:T(8,128)(2,1)S(1)}, bf16[64,1024]{1,0:T(8,128)(2,1)S(1)}, u32[]{:S(2)}, u32[]{:S(2)}) collective-permute-start(bf16[64,1024]{1,0:T(8,128)(2,1)S(1)} %chain_dec_decb.1), channel_id=1, source_target_pairs={{0,8},{1,9},{2,10},{3,11},{4,12},{5,13},{6,14},{7,15},{16,24},{17,... | collective-permute-start | bytes 393224 | tf_op jit(solution)/shard_map/ppermute | solution.py:484
  28.5 10.7 %collective-permute-start.6 = (bf16[64,1024]{1,0:T(8,128)(2,1)S(1)}, bf16[64,1024]{1,0:T(8,128)(2,1)S(1)}, u32[]{:S(2)}, u32[]{:S(2)}) collective-permute-start(bf16[64,1024]{1,0:T(8,128)(2,1)S(1)} %get-tuple-element.38), channel_id=1, source_target_pairs={{8,2},{9,3},{10,0},{11,1},{12,6},{13,7},{14,4},{15,5},{24,18},{25,... | collective-permute-start | bytes 393224 | tf_op jit(solution)/shard_map/ppermute | solution.py:484
  29.8 10.2 %collective-permute-start.5 = (bf16[64,1024]{1,0:T(8,128)(2,1)S(1)}, bf16[64,1024]{1,0:T(8,128)(2,1)S(1)}, u32[]{:S(2)}, u32[]{:S(2)}) collective-permute-start(bf16[64,1024]{1,0:T(8,128)(2,1)S(1)} %chain_dec_decb.1), channel_id=1, source_target_pairs={{0,10},{1,11},{2,8},{3,9},{4,14},{5,15},{6,12},{7,13},{16,26},{17,... | collective-permute-start | bytes 393224 | tf_op jit(solution)/shard_map/ppermute | solution.py:484
  36.3 16.7 %collective-permute-start.11 = (bf16[256,1024]{1,0:T(8,128)(2,1)S(1)}, bf16[256,1024]{1,0:T(8,128)(2,1)S(1)}, u32[]{:S(2)}, u32[]{:S(2)}) collective-permute-start(bf16[256,1024]{1,0:T(8,128)(2,1)S(1)} %merge.5), channel_id=1, source_target_pairs={{0,1},{1,0},{2,3},{3,2},{4,5},{5,4},{6,7},{7,6},{8,9},{9,8},{10,11... | collective-permute-start | bytes 1572872 | tf_op jit(solution)/shard_map/ppermute | solution.py:473
  37.9 8.1 %collective-permute-start.7 = (bf16[64,1024]{1,0:T(8,128)(2,1)S(1)}, bf16[64,1024]{1,0:T(8,128)(2,1)S(1)}, u32[]{:S(2)}, u32[]{:S(2)}) collective-permute-start(bf16[64,1024]{1,0:T(8,128)(2,1)S(1)} %chain_decb_encb.1), channel_id=1, source_target_pairs={{8,0},{9,1},{10,2},{11,3},{12,4},{13,5},{14,6},{15,7},{24,16},{25,... | collective-permute-start | bytes 393224 | tf_op jit(solution)/shard_map/ppermute | solution.py:484
  46.1 10.9 %collective-permute-start.8 = (bf16[128,1024]{1,0:T(8,128)(2,1)S(1)}, bf16[128,1024]{1,0:T(8,128)(2,1)S(1)}, u32[]{:S(2)}, u32[]{:S(2)}) collective-permute-start(bf16[128,1024]{1,0:T(8,128)(2,1)S(1)} %merge.4), channel_id=1, source_target_pairs={{0,1},{1,0},{2,3},{3,2},{4,5},{5,4},{6,7},{7,6},{8,9},{9,8},{10,11... | collective-permute-start | bytes 786440 | tf_op jit(solution)/shard_map/ppermute | solution.py:473
  46.6 16.7 %collective-permute-start.12 = (bf16[64,1024]{1,0:T(8,128)(2,1)S(1)}, bf16[64,1024]{1,0:T(8,128)(2,1)S(1)}, u32[]{:S(2)}, u32[]{:S(2)}) collective-permute-start(bf16[64,1024]{1,0:T(8,128)(2,1)S(1)} %chain_decb_encb.1), channel_id=1, source_target_pairs={{8,1},{9,0},{10,3},{11,2},{12,5},{13,4},{14,7},{15,6},{24,17},{25,... | collective-permute-start | bytes 393224 | tf_op jit(solution)/shard_map/ppermute | solution.py:484
  47.9 15.4 %collective-permute-start.13 = (bf16[64,1024]{1,0:T(8,128)(2,1)S(1)}, bf16[64,1024]{1,0:T(8,128)(2,1)S(1)}, u32[]{:S(2)}, u32[]{:S(2)}) collective-permute-start(bf16[64,1024]{1,0:T(8,128)(2,1)S(1)} %chain_decb_encb.1), channel_id=1, source_target_pairs={{8,2},{9,3},{10,0},{11,1},{12,6},{13,7},{14,4},{15,5},{24,18},{25,... | collective-permute-start | bytes 393224 | tf_op jit(solution)/shard_map/ppermute | solution.py:484
  49.2 14.1 %collective-permute-start.14 = (bf16[64,1024]{1,0:T(8,128)(2,1)S(1)}, bf16[64,1024]{1,0:T(8,128)(2,1)S(1)}, u32[]{:S(2)}, u32[]{:S(2)}) collective-permute-start(bf16[64,1024]{1,0:T(8,128)(2,1)S(1)} %chain_decb_encb.1), channel_id=1, source_target_pairs={{8,3},{9,2},{10,1},{11,0},{12,7},{13,6},{14,5},{15,4},{24,19},{25,... | collective-permute-start | bytes 393224 | tf_op jit(solution)/shard_map/ppermute | solution.py:484
  63.3 2.5 %collective-permute-start.15 = (bf16[256,1792]{1,0:T(8,128)(2,1)S(1)}, bf16[256,1792]{1,0:T(8,128)(2,1)S(1)}, u32[]{:S(2)}, u32[]{:S(2)}) collective-permute-start(bf16[256,1792]{1,0:T(8,128)(2,1)S(1)} %get-tuple-element.63), channel_id=1, source_target_pairs={{0,4},{4,0},{8,12},{12,8},{1,5},{5,1},{9,13},{13,9},{2,6},{6,2},{1... | collective-permute-start | bytes 2752520 | tf_op jit(solution)/shard_map/ppermute | solution.py:469
  64.8 2.8 %collective-permute-start.16 = (bf16[256,1024]{1,0:T(8,128)(2,1)S(1)}, bf16[256,1024]{1,0:T(8,128)(2,1)S(1)}, u32[]{:S(2)}, u32[]{:S(2)}) collective-permute-start(bf16[256,1024]{1,0:T(8,128)(2,1)S(1)} %get-tuple-element.69), channel_id=1, source_target_pairs={{0,4},{4,0},{8,12},{12,8},{1,5},{5,1},{9,13},{13,9},{2,6},{6,2},{1... | collective-permute-start | bytes 1572872 | tf_op jit(solution)/shard_map/ppermute | solution.py:469
